TPU v7x, 128 devices: a whole 4x4x4 slice. The times are simulated.
128 devices in a mesh: dp: 8 (over y_hi, z), tm: 16 (over y_lo, x, core).
Axes of the slice: x: 4, y: 4 (y_hi: 2, y_lo: 2; y = y_hi * 2 + y_lo), z: 4, core: 2. Of those that a mesh axis runs over, the one named last changes fastest.
Arguments:
- frames: bfloat16 [8, 4096, 1536], P('dp', 'tm'), may hold values from -6 to 6
- cotangent: bfloat16 [8, 4096, 1536], P('dp', 'tm'), may hold values from -6 to 6
- layer_norm_gain: float32 [1536], replicated, may hold values from 0.1 to 1.9
- w_query: bfloat16 [1536, 768], P('dp'), may hold values from -0.12757759 to 0.12757759
- w_key: bfloat16 [1536, 768], P('dp'), may hold values from -0.12757759 to 0.12757759
- w_value: bfloat16 [1536, 768], P('dp'), may hold values from -0.15625 to 0.15625
- w_out: bfloat16 [768, 1536], P('dp'), may hold values from -0.21875 to 0.21875
- lengths: int32 [8], P('dp'), may hold values from 2048 to 4096
- win_lo: int32 [8, 4096], P('dp', 'tm'), may hold values from 0 to 4095, as said below
- win_hi: int32 [8, 4096], P('dp', 'tm'), may hold values from 1 to 4096, as said below
Outputs:
- frames_out: bfloat16 [8, 4096, 1536], P('dp', 'tm')
- grad_frames: bfloat16 [8, 4096, 1536], P('dp', 'tm')
- grad_w_query: float32 [1536, 768], P(('dp', 'tm'))
- grad_w_key: float32 [1536, 768], P(('dp', 'tm'))
- grad_w_value: float32 [1536, 768], P(('dp', 'tm'))
- grad_w_out: float32 [768, 1536], P(('dp', 'tm'))
- grad_gain: float32 [1536], P(('dp', 'tm'))
Inputs may be any that keep to these rules, and one draw needn't show every extreme that they name: win_lo[b, t] lies between t - 128 and t, and equals t - 128 at some frames of every utterance. win_hi[b, t] lies between t + 1 and t + 129, and equals t + 129 at some frames of every utterance. frames from lengths[b] on are padding.
All inputs are finite; a program needn't handle non-finite values.
Results may differ from a plain program's by a relative error of at most 0.035.
The roundings to bfloat16 on the way count: a program that leaves them out, or rounds other values in their place, can miss the bound.
Values may be sent and summed in bfloat16 or wider, within the bound.
A program may use at most 128 MiB of HBM per device.

v0:
```python
import jax
import jax.numpy as jnp
from jax import lax
from jax.sharding import PartitionSpec as P

HEADS = 12
HEAD_DIM = 64
REACH = 128


def extended_2(value, sides, width):
    for axis, dim in sides:
        devices, length = (lax.axis_size(axis), value.shape[dim])
        up = [(i, (i + 1) % devices) for i in range(devices - 1)]
        down = [(j, i) for i, j in up]
        last = lax.slice_in_dim(value, length - width, length, axis=dim)
        first = lax.slice_in_dim(value, 0, width, axis=dim)
        before = lax.ppermute(last, axis, up)
        after = lax.ppermute(first, axis, down)
        value = jnp.concatenate([before, value, after], axis=dim)
    return value


def shifted(value, axis, by):
    devices = lax.axis_size(axis)
    pairs = [(i, i + by) for i in range(devices) if 0 <= i + by < devices]
    return lax.ppermute(value, axis, pairs)


def layer_normalize(input_rows, norm_gain):
    xf = input_rows.astype(jnp.float32)
    feature_mean = jnp.mean(xf, -1, keepdims=True)
    centered_input = xf - feature_mean
    var = jnp.mean(centered_input * centered_input, -1, keepdims=True)
    inverse_deviation = lax.rsqrt(var + 1e-05)
    standardized_input = centered_input * inverse_deviation
    return (
        (standardized_input * norm_gain).astype(jnp.bfloat16),
        standardized_input,
        inverse_deviation,
    )


def layer_normalize_backward(normalized_gradient, standardized_input, inverse_deviation, norm_gain):
    scaled_output = normalized_gradient * norm_gain
    gain_gradient = jnp.sum(normalized_gradient * standardized_input, 0)
    first_term = jnp.mean(scaled_output, -1, keepdims=True)
    second_term = jnp.mean(scaled_output * standardized_input, -1, keepdims=True)
    return (
        inverse_deviation * (scaled_output - first_term - standardized_input * second_term),
        gain_gradient,
    )


def window_mask(lo, hi, length, qpos, kpos):
    kp = kpos[None, :]
    inside = (kp >= lo[:, None]) & (kp < hi[:, None]) & (kp < length)
    return inside | (kp == qpos[:, None])


def split_heads(a):
    return a.reshape(a.shape[0], HEADS, HEAD_DIM)


def attend(query, key, value, mask):
    scale = HEAD_DIM ** (-0.5)
    scores = (
        jnp.einsum(
            "qhe,khe->hqk", split_heads(query), split_heads(key), preferred_element_type=jnp.float32
        )
        * scale
    )
    scores = jnp.where(mask[None], scores, -1e30)
    expo = jnp.exp(scores - jnp.max(scores, -1, keepdims=True))
    probs = expo / jnp.sum(expo, -1, keepdims=True)
    probs_low = probs.astype(jnp.bfloat16)
    context = jnp.einsum(
        "hqk,khe->qhe", probs_low, split_heads(value), preferred_element_type=jnp.float32
    )
    return (
        context.reshape(query.shape[0], HEADS * HEAD_DIM).astype(jnp.bfloat16),
        probs,
        probs_low,
    )


def attend_back(query, key, value, probs, probs_low, grad_context):
    scale = HEAD_DIM ** (-0.5)
    grad_heads = split_heads(grad_context)
    grad_value = jnp.einsum(
        "hqk,qhe->khe", probs_low, grad_heads, preferred_element_type=jnp.float32
    )
    grad_probs = jnp.einsum(
        "qhe,khe->hqk", grad_heads, split_heads(value), preferred_element_type=jnp.float32
    )
    delta = jnp.sum(probs * grad_probs, -1, keepdims=True)
    grad_scores = (probs * (grad_probs - delta)).astype(jnp.bfloat16)
    grad_query = (
        jnp.einsum(
            "hqk,khe->qhe", grad_scores, split_heads(key), preferred_element_type=jnp.float32
        )
        * scale
    )
    grad_key = (
        jnp.einsum(
            "hqk,qhe->khe", grad_scores, split_heads(query), preferred_element_type=jnp.float32
        )
        * scale
    )
    width = HEADS * HEAD_DIM
    return (
        grad_query.reshape(query.shape[0], width).astype(jnp.bfloat16),
        grad_key.reshape(key.shape[0], width),
        grad_value.reshape(key.shape[0], width),
    )


def per_device(
    frames, cotangent, layer_norm_gain, w_query, w_key, w_value, w_out, lengths, win_lo, win_hi
):
    input_rows = frames[0]
    grad_y = cotangent[0]
    length = lengths[0]
    rows = input_rows.shape[0]
    width = HEADS * HEAD_DIM
    base = lax.axis_index("tm") * rows
    normalized_input, standardized_input, inverse_deviation = layer_normalize(
        input_rows, layer_norm_gain
    )
    full_q, full_k, full_v, full_o = (
        lax.all_gather(w_query, "dp", axis=0, tiled=True),
        lax.all_gather(w_key, "dp", axis=0, tiled=True),
        lax.all_gather(w_value, "dp", axis=0, tiled=True),
        lax.all_gather(w_out, "dp", axis=0, tiled=True),
    )
    query = jnp.dot(normalized_input, full_q, preferred_element_type=jnp.float32).astype(
        jnp.bfloat16
    )
    key = jnp.dot(normalized_input, full_k, preferred_element_type=jnp.float32).astype(jnp.bfloat16)
    value = jnp.dot(normalized_input, full_v, preferred_element_type=jnp.float32).astype(
        jnp.bfloat16
    )
    extended = extended_2(jnp.concatenate([key, value], 1), (("tm", 0),), REACH)
    key_ext = extended[:, :width]
    value_ext = extended[:, width:]
    qpos = base + jnp.arange(rows, dtype=jnp.int32)
    kpos = base - REACH + jnp.arange(rows + 2 * REACH, dtype=jnp.int32)
    mask = window_mask(win_lo[0], win_hi[0], length, qpos, kpos)
    context, probs, probs_low = attend(query, key_ext, value_ext, mask)
    attn = jnp.dot(context, full_o, preferred_element_type=jnp.float32)
    valid = qpos < length
    frames_out = (input_rows.astype(jnp.float32) + jnp.where(valid[:, None], attn, 0.0)).astype(
        jnp.bfloat16
    )
    masked_grad = jnp.where(valid[:, None], grad_y, jnp.zeros_like(grad_y))
    grad_wo = jnp.einsum("th,td->hd", context, masked_grad, preferred_element_type=jnp.float32)
    grad_context = jnp.einsum(
        "td,hd->th", masked_grad, full_o, preferred_element_type=jnp.float32
    ).astype(jnp.bfloat16)
    grad_query, grad_key_ext, grad_value_ext = attend_back(
        query, key_ext, value_ext, probs, probs_low, grad_context
    )
    grad_kv_ext = jnp.concatenate([grad_key_ext, grad_value_ext], 1)
    lower_rim = grad_kv_ext[:REACH]
    upper_rim = grad_kv_ext[REACH + rows :]
    from_next = shifted(lower_rim.astype(jnp.bfloat16), "tm", -1).astype(lower_rim.dtype)
    from_prev = shifted(upper_rim.astype(jnp.bfloat16), "tm", 1).astype(upper_rim.dtype)
    center = grad_kv_ext[REACH : REACH + rows]
    center = center.at[:REACH].add(from_prev)
    center = center.at[rows - REACH :].add(from_next)
    grad_kv = center.astype(jnp.bfloat16)
    grad_key = grad_kv[:, :width]
    grad_value = grad_kv[:, width:]
    grad_wq = jnp.einsum(
        "td,th->dh", normalized_input, grad_query, preferred_element_type=jnp.float32
    )
    grad_wk = jnp.einsum(
        "td,th->dh", normalized_input, grad_key, preferred_element_type=jnp.float32
    )
    grad_wv = jnp.einsum(
        "td,th->dh", normalized_input, grad_value, preferred_element_type=jnp.float32
    )
    normalized_gradient = (
        jnp.einsum("th,dh->td", grad_query, full_q, preferred_element_type=jnp.float32)
        + jnp.einsum("th,dh->td", grad_key, full_k, preferred_element_type=jnp.float32)
        + jnp.einsum("th,dh->td", grad_value, full_v, preferred_element_type=jnp.float32)
    )
    layer_norm_gradient, gain_product = layer_normalize_backward(
        normalized_gradient, standardized_input, inverse_deviation, layer_norm_gain
    )
    grad_frames = (grad_y.astype(jnp.float32) + layer_norm_gradient).astype(jnp.bfloat16)
    owned = (
        lax.psum_scatter(grad_wq, ("dp", "tm"), scatter_dimension=0, tiled=True),
        lax.psum_scatter(grad_wk, ("dp", "tm"), scatter_dimension=0, tiled=True),
        lax.psum_scatter(grad_wv, ("dp", "tm"), scatter_dimension=0, tiled=True),
        lax.psum_scatter(grad_wo, ("dp", "tm"), scatter_dimension=0, tiled=True),
        lax.psum_scatter(gain_product, ("dp", "tm"), scatter_dimension=0, tiled=True),
    )
    return (frames_out[None], grad_frames[None], owned[0], owned[1], owned[2], owned[3], owned[4])


def solution(mesh):
    in_specs = (
        P("dp", "tm", None),
        P("dp", "tm", None),
        P(),
        P("dp", None),
        P("dp", None),
        P("dp", None),
        P("dp", None),
        P("dp"),
        P("dp", "tm"),
        P("dp", "tm"),
    )
    out_specs = (
        P("dp", "tm", None),
        P("dp", "tm", None),
        P(("dp", "tm"), None),
        P(("dp", "tm"), None),
        P(("dp", "tm"), None),
        P(("dp", "tm"), None),
        P(("dp", "tm")),
    )
    return jax.shard_map(
        per_device, mesh=mesh, in_specs=in_specs, out_specs=out_specs, check_vma=False
    )
```

profile of v0, /device:TPU:1, one launch (start us, length us, event | category | flops | bytes accessed | tf_op | source)
XLA Modules:
  0.0 1152.0 jit_solution(17186514883900988188)
XLA Ops:
  12.7 55.9 %all-gather.5.cloned.1.call-done = bf16[1536,768]{1,0:T(8,128)(2,1)} async-done(((bf16[192,768]{1,0:T(8,128)(2,1)}), bf16[1536,768]{1,0:T(8,128)(2,1)}) %all-gather.5.cloned.1.call-update) | async-done | bytes 2359312 | tf_op jit(solution)/shard_map/all_gather | solution.py:132
  71.1 53.3 %all-gather.7.cloned.1.call-done = bf16[1536,768]{1,0:T(8,128)(2,1)} async-done(((bf16[192,768]{1,0:T(8,128)(2,1)}), bf16[1536,768]{1,0:T(8,128)(2,1)}) %all-gather.7.cloned.1.call-update) | async-done | bytes 2359312 | tf_op jit(solution)/shard_map/all_gather | solution.py:133
  134.3 47.1 %all-gather.9.cloned.1.call-done = bf16[1536,768]{1,0:T(8,128)(2,1)} async-done(((bf16[192,768]{1,0:T(8,128)(2,1)}), bf16[1536,768]{1,0:T(8,128)(2,1)}) %all-gather.9.cloned.1.call-update) | async-done | bytes 2359312 | tf_op jit(solution)/shard_map/all_gather | solution.py:131
  185.9 51.2 %all-gather.11.cloned.1.call-done = bf16[768,1536]{1,0:T(8,128)(2,1)} async-done(((bf16[96,1536]{1,0:T(8,128)(2,1)}), bf16[768,1536]{1,0:T(8,128)(2,1)}) %all-gather.11.cloned.1.call-update) | async-done | bytes 2359312 | tf_op jit(solution)/shard_map/all_gather | solution.py:134
  244.0 6.5 fusion.79
  250.6 4.1 fusion.37
  261.6 4.4 collective-permute-start.2
  281.5 366.0 %fusion.76 = (f32[16,768]{1,0:T(8,128)S(1)}, f32[16,768]{1,0:T(8,128)S(1)}, f32[16,768]{1,0:T(8,128)S(1)}, f32[8,1536]{1,0:T(8,128)S(1)}) fusion(f32[1536,768]{1,0:T(8,128)} %fusion.41, f32[1536,768]{1,0:T(8,128)} %fusion.64, f32[1536,768]{1,0:T(8,128)} %fusion.61, f32[768,1536]{1,0:T(8,128)} %fusion.48), kind=kCustom, calls=%all-reduce-scatter.4 | all-reduce-scatter fusion | flops 6291458 | bytes 19070976
  650.2 6.5 collective-permute-start.99
  656.7 5.4 collective-permute-start.34
  662.1 5.6 collective-permute-start.33
  667.7 4.7 collective-permute-start.32
  672.5 5.9 collective-permute-start.31
  684.3 6.7 collective-permute-start.29
  718.9 4.0 collective-permute-start.17
  728.1 3.9 collective-permute-start.14
  746.9 3.8 collective-permute-start.7
  770.1 4.2 collective-permute-start.59
  795.3 4.0 collective-permute-start.49
  873.2 4.9 collective-permute-start.81
  899.4 12.7 %collective-permute-start.72 = (f32[16,768]{1,0:T(8,128)S(1)}, f32[16,768]{1,0:T(8,128)S(1)}, u32[]{:S(2)}, u32[]{:S(2)}) collective-permute-start(f32[16,768]{1,0:T(8,128)S(1)} %get-tuple-element.40), channel_id=1, source_target_pairs={{0,5},{1,6},{2,7},{3,8},{4,9},{5,10},{6,11},{7,12},{8,13},{9,14},{... | collective-permute-start | bytes 147464
  962.3 63.3 %all-reduce.4 = f32[1536]{0:T(1024)S(1)} all-reduce(f32[1536]{0:T(1024)S(1)} %copy-done.129), channel_id=6, replica_groups=mesh['dp'=8,'tm'=16] {'dp','tm'}, use_global_device_ids=true, to_apply=%region_12.13.clone | all-reduce | flops 1536 | bytes 12288
  1026.4 21.2 %concatenate.16 = f32[524,768]{1,0:T(8,128)S(1)} concatenate(f32[12,768]{1,0:T(8,128)S(1)} %collective-permute-done.35, f32[16,768]{1,0:T(8,128)S(1)} %collective-permute-done.34, f32[16,768]{1,0:T(8,128)S(1)} %collective-permute-done.33, f32[16,768]{1,0:T(8,128)S(1)} %collective-permute-done.32, f32[16,768]{1,0:T(8,128)S(1)} %collective-permute-done.31, ...), dimensions={0} | concatenate | bytes 3219456
  1047.6 4.2 collective-permute-start.114
  1051.8 4.0 collective-permute-start.113
  1057.8 5.6 collective-permute-start.111
  1063.3 6.1 collective-permute-start.110
  1070.4 10.8 concatenate.17
  1090.8 4.6 collective-permute-start.105
  1096.2 19.1 %concatenate.18 = f32[524,768]{1,0:T(8,128)S(1)} concatenate(f32[12,768]{1,0:T(8,128)S(1)} %collective-permute-done.99, f32[16,768]{1,0:T(8,128)} %collective-permute-done.98, f32[16,768]{1,0:T(8,128)} %collective-permute-done.97, f32[16,768]{1,0:T(8,128)} %collective-permute-done.96, f32[16,768]{1,0:T(8,128)} %collective-permute-done.95, f32[16,768]{1,0:T(8,128)} %collective-permute-done.94, ...), dimensions={0} | concatenate | bytes 3219456
  1122.0 5.5 collective-permute-start.102
  1133.0 11.8 %concatenate.19 = f32[262,1536]{1,0:T(8,128)S(1)} concatenate(f32[6,1536]{1,0:T(8,128)S(1)} %collective-permute-done.131, f32[8,1536]{1,0:T(8,128)S(1)} %copy-done.92, f32[8,1536]{1,0:T(8,128)S(1)} %copy-done.96, f32[8,1536]{1,0:T(8,128)S(1)} %copy-done.100, f32[8,1536]{1,0:T(8,128)S(1)} %copy-done.104, f32[8,1536]{1,0:T(8,128)S(1)} %copy-done.108, f32[8,1536]{1,0:T(8,128)S(1)} %copy-done.112, ...), dimensions={0} | concatenate | bytes 3219456
  (568 shorter events, 317.2 us)
Async XLA Ops:
  7.2 61.4 %all-gather.5.cloned.1.call-start = ((), (), s32[]{:S(2)}) async-start(), calls=%async_computation | async-start | bytes 2654208 | tf_op jit(solution)/shard_map/all_gather | solution.py:132
  7.9 116.5 %all-gather.7.cloned.1.call-start = ((), (), s32[]{:S(2)}) async-start(), calls=%async_computation.1 | async-start | bytes 2654208 | tf_op jit(solution)/shard_map/all_gather | solution.py:133
  8.7 172.8 %all-gather.9.cloned.1.call-start = ((), (), s32[]{:S(2)}) async-start(), calls=%async_computation.2 | async-start | bytes 2654208 | tf_op jit(solution)/shard_map/all_gather | solution.py:131
  9.4 227.7 %all-gather.11.cloned.1.call-start = ((), (), s32[]{:S(2)}) async-start(), calls=%async_computation.3 | async-start | bytes 2654208 | tf_op jit(solution)/shard_map/all_gather | solution.py:134
  127.9 114.4 %collective-permute-start.1 = (bf16[128,1536]{1,0:T(8,128)(2,1)}, bf16[128,1536]{1,0:T(8,128)(2,1)S(1)}, u32[]{:S(2)}, u32[]{:S(2)}) collective-permute-start(bf16[128,1536]{1,0:T(8,128)(2,1)} %get-tuple-element.47), channel_id=1, source_target_pairs={{1,0},{2,1},{3,2},{4,3},{5,4},{6,5},{7,6},{8,7},{9,8},{10,9},{11,1... | collective-permute-start | bytes 1179656 | tf_op jit(solution)/shard_map/ppermute | solution.py:19
  131.2 111.1 %collective-permute-start = (bf16[128,1536]{1,0:T(8,128)(2,1)}, bf16[128,1536]{1,0:T(8,128)(2,1)S(1)}, u32[]{:S(2)}, u32[]{:S(2)}) collective-permute-start(bf16[128,1536]{1,0:T(8,128)(2,1)} %get-tuple-element.46), channel_id=1, source_target_pairs={{0,1},{1,2},{2,3},{3,4},{4,5},{5,6},{6,7},{7,8},{8,9},{9,10},{10,1... | collective-permute-start | bytes 1179656 | tf_op jit(solution)/shard_map/ppermute | solution.py:18
  648.8 23.6 %collective-permute-start.67 = (f32[12,768]{1,0:T(8,128)S(1)}, f32[12,768]{1,0:T(8,128)S(1)}, u32[]{:S(2)}, u32[]{:S(2)}) collective-permute-start(f32[12,768]{1,0:T(8,128)S(1)} %slice.93), channel_id=1, source_target_pairs={{0,32},{1,33},{2,34},{3,35},{4,36},{5,37},{6,38},{7,39},{8,40},{9,... | collective-permute-start | bytes 110600
  650.2 28.3 %collective-permute-start.99 = (f32[12,768]{1,0:T(8,128)S(1)}, f32[12,768]{1,0:T(8,128)S(1)}, u32[]{:S(2)}, u32[]{:S(2)}) collective-permute-start(f32[12,768]{1,0:T(8,128)S(1)} %slice.94), channel_id=1, source_target_pairs={{0,32},{1,33},{2,34},{3,35},{4,36},{5,37},{6,38},{7,39},{8,40},{9,... | collective-permute-start | bytes 110600
  656.7 27.6 %collective-permute-start.34 = (f32[16,768]{1,0:T(8,128)S(1)}, f32[16,768]{1,0:T(8,128)S(1)}, u32[]{:S(2)}, u32[]{:S(2)}) collective-permute-start(f32[16,768]{1,0:T(8,128)S(1)} %get-tuple-element.38), channel_id=1, source_target_pairs={{0,31},{1,32},{2,33},{3,34},{4,35},{5,36},{6,37},{7,38},{8,39},{9,... | collective-permute-start | bytes 147464
  662.1 28.9 %collective-permute-start.33 = (f32[16,768]{1,0:T(8,128)S(1)}, f32[16,768]{1,0:T(8,128)S(1)}, u32[]{:S(2)}, u32[]{:S(2)}) collective-permute-start(f32[16,768]{1,0:T(8,128)S(1)} %get-tuple-element.38), channel_id=1, source_target_pairs={{0,30},{1,31},{2,32},{3,33},{4,34},{5,35},{6,36},{7,37},{8,38},{9,... | collective-permute-start | bytes 147464
  667.7 24.8 %collective-permute-start.32 = (f32[16,768]{1,0:T(8,128)S(1)}, f32[16,768]{1,0:T(8,128)S(1)}, u32[]{:S(2)}, u32[]{:S(2)}) collective-permute-start(f32[16,768]{1,0:T(8,128)S(1)} %get-tuple-element.38), channel_id=1, source_target_pairs={{0,29},{1,30},{2,31},{3,32},{4,33},{5,34},{6,35},{7,36},{8,37},{9,... | collective-permute-start | bytes 147464
  672.5 23.3 %collective-permute-start.31 = (f32[16,768]{1,0:T(8,128)S(1)}, f32[16,768]{1,0:T(8,128)S(1)}, u32[]{:S(2)}, u32[]{:S(2)}) collective-permute-start(f32[16,768]{1,0:T(8,128)S(1)} %get-tuple-element.38), channel_id=1, source_target_pairs={{0,28},{1,29},{2,30},{3,31},{4,32},{5,33},{6,34},{7,35},{8,36},{9,... | collective-permute-start | bytes 147464
  888.5 25.5 %collective-permute-start.76 = (f32[16,768]{1,0:T(8,128)S(1)}, f32[16,768]{1,0:T(8,128)S(1)}, u32[]{:S(2)}, u32[]{:S(2)}) collective-permute-start(f32[16,768]{1,0:T(8,128)S(1)} %get-tuple-element.40), channel_id=1, source_target_pairs={{0,9},{1,10},{2,11},{3,12},{4,13},{5,14},{6,15},{7,16},{8,17},{9,1... | collective-permute-start | bytes 147464
  891.3 25.9 %collective-permute-start.75 = (f32[16,768]{1,0:T(8,128)S(1)}, f32[16,768]{1,0:T(8,128)S(1)}, u32[]{:S(2)}, u32[]{:S(2)}) collective-permute-start(f32[16,768]{1,0:T(8,128)S(1)} %get-tuple-element.40), channel_id=1, source_target_pairs={{0,8},{1,9},{2,10},{3,11},{4,12},{5,13},{6,14},{7,15},{8,16},{9,17... | collective-permute-start | bytes 147464
  893.8 27.0 %collective-permute-start.74 = (f32[16,768]{1,0:T(8,128)S(1)}, f32[16,768]{1,0:T(8,128)S(1)}, u32[]{:S(2)}, u32[]{:S(2)}) collective-permute-start(f32[16,768]{1,0:T(8,128)S(1)} %get-tuple-element.40), channel_id=1, source_target_pairs={{0,7},{1,8},{2,9},{3,10},{4,11},{5,12},{6,13},{7,14},{8,15},{9,16}... | collective-permute-start | bytes 147464
  896.9 25.9 %collective-permute-start.73 = (f32[16,768]{1,0:T(8,128)S(1)}, f32[16,768]{1,0:T(8,128)S(1)}, u32[]{:S(2)}, u32[]{:S(2)}) collective-permute-start(f32[16,768]{1,0:T(8,128)S(1)} %get-tuple-element.40), channel_id=1, source_target_pairs={{0,6},{1,7},{2,8},{3,9},{4,10},{5,11},{6,12},{7,13},{8,14},{9,15},... | collective-permute-start | bytes 147464
  899.4 26.5 %collective-permute-start.72 = (f32[16,768]{1,0:T(8,128)S(1)}, f32[16,768]{1,0:T(8,128)S(1)}, u32[]{:S(2)}, u32[]{:S(2)}) collective-permute-start(f32[16,768]{1,0:T(8,128)S(1)} %get-tuple-element.40), channel_id=1, source_target_pairs={{0,5},{1,6},{2,7},{3,8},{4,9},{5,10},{6,11},{7,12},{8,13},{9,14},{... | collective-permute-start | bytes 147464
  947.6 100.0 %collective-permute-start.119 = (f32[8,1536]{1,0:T(8,128)S(1)}, f32[8,1536]{1,0:T(8,128)}, u32[]{:S(2)}, u32[]{:S(2)}) collective-permute-start(f32[8,1536]{1,0:T(8,128)S(1)} %get-tuple-element.41), channel_id=1, source_target_pairs={{0,20},{1,21},{2,22},{3,23},{4,24},{5,25},{6,26},{7,27},{8,28},{9,... | collective-permute-start | bytes 147464
  951.0 100.7 %collective-permute-start.118 = (f32[8,1536]{1,0:T(8,128)S(1)}, f32[8,1536]{1,0:T(8,128)}, u32[]{:S(2)}, u32[]{:S(2)}) collective-permute-start(f32[8,1536]{1,0:T(8,128)S(1)} %get-tuple-element.41), channel_id=1, source_target_pairs={{0,19},{1,20},{2,21},{3,22},{4,23},{5,24},{6,25},{7,26},{8,27},{9,... | collective-permute-start | bytes 147464
  953.6 102.2 %collective-permute-start.117 = (f32[8,1536]{1,0:T(8,128)S(1)}, f32[8,1536]{1,0:T(8,128)}, u32[]{:S(2)}, u32[]{:S(2)}) collective-permute-start(f32[8,1536]{1,0:T(8,128)S(1)} %get-tuple-element.41), channel_id=1, source_target_pairs={{0,18},{1,19},{2,20},{3,21},{4,22},{5,23},{6,24},{7,25},{8,26},{9,... | collective-permute-start | bytes 147464
  955.5 102.3 %collective-permute-start.116 = (f32[8,1536]{1,0:T(8,128)S(1)}, f32[8,1536]{1,0:T(8,128)}, u32[]{:S(2)}, u32[]{:S(2)}) collective-permute-start(f32[8,1536]{1,0:T(8,128)S(1)} %get-tuple-element.41), channel_id=1, source_target_pairs={{0,17},{1,18},{2,19},{3,20},{4,21},{5,22},{6,23},{7,24},{8,25},{9,... | collective-permute-start | bytes 147464
  957.8 105.5 %collective-permute-start.115 = (f32[8,1536]{1,0:T(8,128)S(1)}, f32[8,1536]{1,0:T(8,128)}, u32[]{:S(2)}, u32[]{:S(2)}) collective-permute-start(f32[8,1536]{1,0:T(8,128)S(1)} %get-tuple-element.41), channel_id=1, source_target_pairs={{0,16},{1,17},{2,18},{3,19},{4,20},{5,21},{6,22},{7,23},{8,24},{9,... | collective-permute-start | bytes 147464
  1047.6 33.6 %collective-permute-start.114 = (f32[8,1536]{1,0:T(8,128)S(1)}, f32[8,1536]{1,0:T(8,128)}, u32[]{:S(2)}, u32[]{:S(2)}) collective-permute-start(f32[8,1536]{1,0:T(8,128)S(1)} %get-tuple-element.41), channel_id=1, source_target_pairs={{0,15},{1,16},{2,17},{3,18},{4,19},{5,20},{6,21},{7,22},{8,23},{9,... | collective-permute-start | bytes 147464
  1051.8 30.9 %collective-permute-start.113 = (f32[8,1536]{1,0:T(8,128)S(1)}, f32[8,1536]{1,0:T(8,128)}, u32[]{:S(2)}, u32[]{:S(2)}) collective-permute-start(f32[8,1536]{1,0:T(8,128)S(1)} %get-tuple-element.41), channel_id=1, source_target_pairs={{0,14},{1,15},{2,16},{3,17},{4,18},{5,19},{6,20},{7,21},{8,22},{9,... | collective-permute-start | bytes 147464
  1055.7 29.4 %collective-permute-start.112 = (f32[8,1536]{1,0:T(8,128)S(1)}, f32[8,1536]{1,0:T(8,128)}, u32[]{:S(2)}, u32[]{:S(2)}) collective-permute-start(f32[8,1536]{1,0:T(8,128)S(1)} %get-tuple-element.41), channel_id=1, source_target_pairs={{0,13},{1,14},{2,15},{3,16},{4,17},{5,18},{6,19},{7,20},{8,21},{9,... | collective-permute-start | bytes 147464
  1057.8 30.9 %collective-permute-start.111 = (f32[8,1536]{1,0:T(8,128)S(1)}, f32[8,1536]{1,0:T(8,128)}, u32[]{:S(2)}, u32[]{:S(2)}) collective-permute-start(f32[8,1536]{1,0:T(8,128)S(1)} %get-tuple-element.41), channel_id=1, source_target_pairs={{0,12},{1,13},{2,14},{3,15},{4,16},{5,17},{6,18},{7,19},{8,20},{9,... | collective-permute-start | bytes 147464
  1063.3 27.4 %collective-permute-start.110 = (f32[8,1536]{1,0:T(8,128)S(1)}, f32[8,1536]{1,0:T(8,128)}, u32[]{:S(2)}, u32[]{:S(2)}) collective-permute-start(f32[8,1536]{1,0:T(8,128)S(1)} %get-tuple-element.41), channel_id=1, source_target_pairs={{0,11},{1,12},{2,13},{3,14},{4,15},{5,16},{6,17},{7,18},{8,19},{9,... | collective-permute-start | bytes 147464
  1081.2 34.2 %collective-permute-start.109 = (f32[8,1536]{1,0:T(8,128)S(1)}, f32[8,1536]{1,0:T(8,128)S(1)}, u32[]{:S(2)}, u32[]{:S(2)}) collective-permute-start(f32[8,1536]{1,0:T(8,128)S(1)} %get-tuple-element.41), channel_id=1, source_target_pairs={{0,10},{1,11},{2,12},{3,13},{4,14},{5,15},{6,16},{7,17},{8,18},{9,... | collective-permute-start | bytes 147464
  1082.7 36.4 %collective-permute-start.108 = (f32[8,1536]{1,0:T(8,128)S(1)}, f32[8,1536]{1,0:T(8,128)S(1)}, u32[]{:S(2)}, u32[]{:S(2)}) collective-permute-start(f32[8,1536]{1,0:T(8,128)S(1)} %get-tuple-element.41), channel_id=1, source_target_pairs={{0,9},{1,10},{2,11},{3,12},{4,13},{5,14},{6,15},{7,16},{8,17},{9,1... | collective-permute-start | bytes 147464
  1085.2 36.8 %collective-permute-start.107 = (f32[8,1536]{1,0:T(8,128)S(1)}, f32[8,1536]{1,0:T(8,128)S(1)}, u32[]{:S(2)}, u32[]{:S(2)}) collective-permute-start(f32[8,1536]{1,0:T(8,128)S(1)} %get-tuple-element.41), channel_id=1, source_target_pairs={{0,8},{1,9},{2,10},{3,11},{4,12},{5,13},{6,14},{7,15},{8,16},{9,17... | collective-permute-start | bytes 147464
  1088.6 38.9 %collective-permute-start.106 = (f32[8,1536]{1,0:T(8,128)S(1)}, f32[8,1536]{1,0:T(8,128)S(1)}, u32[]{:S(2)}, u32[]{:S(2)}) collective-permute-start(f32[8,1536]{1,0:T(8,128)S(1)} %get-tuple-element.41), channel_id=1, source_target_pairs={{0,7},{1,8},{2,9},{3,10},{4,11},{5,12},{6,13},{7,14},{8,15},{9,16}... | collective-permute-start | bytes 147464
  1090.8 39.1 %collective-permute-start.105 = (f32[8,1536]{1,0:T(8,128)S(1)}, f32[8,1536]{1,0:T(8,128)S(1)}, u32[]{:S(2)}, u32[]{:S(2)}) collective-permute-start(f32[8,1536]{1,0:T(8,128)S(1)} %get-tuple-element.41), channel_id=1, source_target_pairs={{0,6},{1,7},{2,8},{3,9},{4,10},{5,11},{6,12},{7,13},{8,14},{9,15},... | collective-permute-start | bytes 147464
  (237 other events, 7904.4 us)
Sparse Core Ops, SparseCore 0:
  10.3 58.2 all-gather.4
  70.9 53.4 all-gather.6
  126.8 54.6 all-gather.8
  183.6 53.4 all-gather.10
where the time goes:
time: 1170 us; the launch traced here: 1150 us
  blocking collectives  429 us (37%)
  starting transfers between devices  367 us (31%)
  waiting for transfers between devices  213 us (18%)
  local copies, waits for them, and re-layouts  71.9 us (6%)
  matrix products  46.4 us (4%)
  between operations  17.9 us (2%)
    unnamed x2, blocking collectives  429 us
    unnamed x128, starting transfers between devices  354 us
    unnamed x279, local copies, waits for them, and re-layouts  67.2 us
    all_gather x1, waiting for transfers between devices, per_device(): lax.all_gather(w_key, 'dp', axis=0, tiled=True)  55.9 us
    all_gather x1, waiting for transfers between devices, per_device(): lax.all_gather(w_value, 'dp', axis=0, tiled=True)  53.3 us
    all_gather x1, waiting for transfers between devices, per_device(): lax.all_gather(w_out, 'dp', axis=0, tiled=True)  51.2 us
    all_gather x1, waiting for transfers between devices, per_device(): lax.all_gather(w_query, 'dp', axis=0, tiled=True)  47.1 us
  transfers between devices with their start and end apart: 136, of which 7 were waited for; matrix products, arithmetic and copies ran while one was open for 7% of the time, Pallas kernels for 0%

commit v1 on v0

--- a/solution.py
+++ b/solution.py
@@ -1,7 +1,474 @@
 import jax
 import jax.numpy as jnp
 from jax import lax
+from jax.experimental import pallas as pl
+from jax.experimental.pallas import tpu as pltpu
+
 from jax.sharding import PartitionSpec as P
+
+MESH = pl.DeviceIdType.MESH
+BF = jnp.bfloat16
+F32 = jnp.float32
+
+
+class Place:
+    def __init__(self):
+        dp, tm = lax.axis_index("dp"), lax.axis_index("tm")
+        self.yh, self.z = dp // 4, lax.rem(dp, 4)
+        self.yl, self.x, self.core = tm // 8, lax.rem(tm // 2, 4), lax.rem(tm, 2)
+        self.y = self.yh * 2 + self.yl
+
+    def at(self, axis):
+        return {"x": self.x, "y": self.y, "z": self.z}[axis]
+
+    def device(self, axis=None, j=None):
+        y, z, x, core = self.y, self.z, self.x, self.core
+        if axis == "x":
+            x = j
+        elif axis == "y":
+            y = j
+        elif axis == "z":
+            z = j
+        else:
+            core = 1 - core
+        return ((y // 2) * 4 + z, (lax.rem(y, 2) * 4 + x) * 2 + core)
+
+    def right(self, axis):
+        return lax.rem(self.at(axis) + 1, 4)
+
+    def left(self, axis):
+        return lax.rem(self.at(axis) + 3, 4)
+
+    def over(self, axis):
+        return lax.rem(self.at(axis) + 2, 4)
+
+
+def greet(me):
+    barrier = pltpu.get_barrier_semaphore()
+    for axis in "xyz":
+        for j in (me.left(axis), me.right(axis)):
+            pl.semaphore_signal(barrier, inc=1, device_id=me.device(axis, j), device_id_type=MESH)
+    pl.semaphore_signal(barrier, inc=1, device_id=me.device(), device_id_type=MESH)
+    pl.semaphore_wait(barrier, 7)
+
+
+def gather_regions(me, w, h):
+    return (
+        (
+            ("y", lambda j, p: w.at[j // 2, me.z, h, 0, lax.rem(j, 2), pl.ds(2 * p, 2)]),
+            ("z", lambda j, p: w.at[p, j, h, 0]),
+        ),
+        (
+            ("z", lambda j, p: w.at[me.yh, j, h, 1, me.yl, pl.ds(2 * p, 2)]),
+            ("y", lambda j, p: w.at[j // 2, pl.ds(2 * p, 2), h, 1, lax.rem(j, 2)]),
+        ),
+        (
+            ("z", lambda j, p: w.at[me.yh, j, h, 2, me.yl, me.x, :, pl.ds(384 * p, 384)]),
+            ("y", lambda j, p: w.at[j // 2, pl.ds(2 * p, 2), h, 2, lax.rem(j, 2), me.x]),
+            ("x", lambda j, p: w.at[p, :, h, 2, :, j]),
+        ),
+    )
+
+
+class GatherStage:
+    def __init__(self, me, axis, region, other, send, recv, base):
+        self.me, self.axis, self.region, self.other = me, axis, region, other
+        self.send, self.recv, self.base = send, recv, base
+
+    def hop(self, k, j, p, right):
+        me, n = self.me, self.base + k
+        to = me.right(self.axis) if right else me.left(self.axis)
+        part = self.region(j, p)
+        return pltpu.make_async_remote_copy(
+            src_ref=part, dst_ref=part, send_sem=self.send.at[n], recv_sem=self.recv.at[n],
+            device_id=me.device(self.axis, to), device_id_type=MESH)
+
+    def share(self, k, j, p, region=None):
+        n = self.base + 6 + k
+        part = (region or self.region)(j, p)
+        return pltpu.make_async_remote_copy(
+            src_ref=part, dst_ref=part, send_sem=self.send.at[n], recv_sem=self.recv.at[n],
+            device_id=self.me.device(), device_id_type=MESH)
+
+    def start(self):
+        i = self.me.at(self.axis)
+        self.hop(0, i, 0, True).start()
+        self.hop(1, i, 1, False).start()
+        self.hop(2, i, 1, True).start()
+        self.hop(3, i, 0, False).start()
+
+    def relay(self):
+        me = self.me
+        l, r = me.left(self.axis), me.right(self.axis)
+        self.hop(0, l, 0, True).wait_recv()
+        self.hop(4, l, 0, True).start()
+        self.share(0, l, 0).start()
+        self.hop(1, r, 1, False).wait_recv()
+        self.hop(5, r, 1, False).start()
+        self.share(1, r, 1).start()
+
+    def finish(self):
+        me = self.me
+        l, r, o = me.left(self.axis), me.right(self.axis), me.over(self.axis)
+        self.hop(2, l, 1, True).wait_recv()
+        self.share(2, l, 1).start()
+        self.hop(3, r, 0, False).wait_recv()
+        self.share(3, r, 0).start()
+        self.hop(4, o, 0, True).wait_recv()
+        self.share(4, o, 0).start()
+        self.hop(5, o, 1, False).wait_recv()
+        self.share(5, o, 1).start()
+
+    def arrive(self):
+        me = self.me
+        l, r, o = me.left(self.axis), me.right(self.axis), me.over(self.axis)
+        for k, (j, p) in enumerate(((l, 0), (r, 1), (l, 1), (r, 0), (o, 0), (o, 1))):
+            self.share(k, j, p, self.other).wait_recv()
+
+    def drain(self):
+        me = self.me
+        i, l, r, o = me.at(self.axis), me.left(self.axis), me.right(self.axis), me.over(self.axis)
+        for k, (j, p, right) in enumerate(((i, 0, True), (i, 1, False), (i, 1, True), (i, 0, False), (l, 0, True), (r, 1, False))):
+            self.hop(k, j, p, right).wait_send()
+        for k, (j, p) in enumerate(((l, 0), (r, 1), (l, 1), (r, 0), (o, 0), (o, 1))):
+            self.share(k, j, p).wait_send()
+
+
+def gather_stages(me, w, send, recv):
+    mine, theirs = gather_regions(me, w, me.core), gather_regions(me, w, 1 - me.core)
+    stages, base = [], 0
+    for colour, other in zip(mine, theirs):
+        row = []
+        for (axis, region), (_, other_region) in zip(colour, other):
+            row.append(GatherStage(me, axis, region, other_region, send, recv, base))
+            base += 12
+        stages.append(row)
+    return stages
+
+
+GATHER_SEMS = 84
+
+
+def run_gather(me, w_own, w, send, recv, local):
+    own = (
+        pltpu.make_async_copy(w_own.at[:, pl.ds(0, 2), me.yl], w.at[me.yh, me.z, :, pl.ds(0, 2), me.yl], local.at[0]),
+        pltpu.make_async_copy(w_own.at[:, 2, me.yl, me.x], w.at[me.yh, me.z, :, 2, me.yl, me.x], local.at[1]),
+    )
+    for copy in own:
+        copy.start()
+    greet(me)
+    for copy in own:
+        copy.wait()
+    a, b, c = gather_stages(me, w, send, recv)
+    c[0].start()
+    a[0].start()
+    b[0].start()
+    c[0].relay()
+    c[0].finish()
+    c[1].start()
+    a[0].relay()
+    b[0].relay()
+    a[0].finish()
+    a[1].start()
+    b[0].finish()
+    b[1].start()
+    c[1].relay()
+    c[1].finish()
+    c[2].start()
+    a[1].relay()
+    b[1].relay()
+    c[2].relay()
+    a[1].finish()
+    b[1].finish()
+    c[2].finish()
+    for row in (a, b, c):
+        for stage in row:
+            stage.arrive()
+    for row in (a, b, c):
+        for stage in row:
+            stage.drain()
+
+
+def gather_kernel(w_own, w, send, recv, local):
+    run_gather(Place(), w_own, w, send, recv, local)
+
+
+def gather_weights(own):
+    return pl.pallas_call(
+        gather_kernel,
+        out_shape=jax.ShapeDtypeStruct((2, 4) + own.shape, BF),
+        in_specs=[pl.BlockSpec(memory_space=pltpu.VMEM)],
+        out_specs=pl.BlockSpec(memory_space=pltpu.VMEM),
+        scratch_shapes=[
+            pltpu.SemaphoreType.DMA((GATHER_SEMS,)),
+            pltpu.SemaphoreType.DMA((GATHER_SEMS,)),
+            pltpu.SemaphoreType.DMA((2,)),
+        ],
+        compiler_params=pltpu.CompilerParams(collective_id=0, has_side_effects=True, vmem_limit_bytes=40 << 20),
+        name="gather_weights",
+    )(own)
+
+
+ORDERS = (("x", "y", "z"), ("y", "z", "x"), ("z", "x", "y"))
+DIMS = {"y": 0, "z": 1, "x": 2}
+
+
+class ReduceStage:
+    def __init__(self, me, axis, load, count, out, bufs, sems, base):
+        self.me, self.axis, self.load, self.count, self.out = me, axis, load, count, out
+        self.sent, self.got = bufs
+        self.send, self.recv = sems
+        self.base = base
+
+    def hop(self, k):
+        me = self.me
+        to = me.right(self.axis) if k % 2 == 0 else me.left(self.axis)
+        return pltpu.make_async_remote_copy(
+            src_ref=self.sent.at[k], dst_ref=self.got.at[k],
+            send_sem=self.send.at[self.base + k], recv_sem=self.recv.at[self.base + k],
+            device_id=me.device(self.axis, to), device_id_type=MESH)
+
+    def each(self, body):
+        if self.count == 1:
+            body(0)
+        else:
+            @pl.loop(0, self.count)
+            def _(m):
+                body(m)
+
+    def fill(self, k, j, p, extra=None):
+        def body(m):
+            v = self.load(j, p, m)
+            if extra is not None:
+                v = v + self.got[extra, m].astype(F32)
+            self.sent[k, m] = v.astype(self.sent.dtype)
+        self.each(body)
+        self.hop(k).start()
+
+    def start(self):
+        me = self.me
+        l, r, o = me.left(self.axis), me.right(self.axis), me.over(self.axis)
+        self.fill(0, o, 0)
+        self.fill(1, o, 1)
+        self.fill(2, r, 1)
+        self.fill(3, l, 0)
+
+    def relay(self):
+        me = self.me
+        self.hop(0).wait_recv()
+        self.fill(4, me.right(self.axis), 0, 0)
+        self.hop(1).wait_recv()
+        self.fill(5, me.left(self.axis), 1, 1)
+
+    def finish(self):
+        me = self.me
+        i = me.at(self.axis)
+        for k in (2, 3, 4, 5):
+            self.hop(k).wait_recv()
+
+        for p, a, b in ((0, 4, 3), (1, 2, 5)):
+            def body(m, p=p, a=a, b=b):
+                v = self.load(i, p, m) + self.got[a, m].astype(F32) + self.got[b, m].astype(F32)
+                self.out(p, m, v)
+            self.each(body)
+
+    def drain(self):
+        for k in range(6):
+            self.hop(k).wait_send()
+
+
+class GainSum:
+    STEPS = (None, "x1", "x3", "y1", "y3", "z1", "z3")
+
+    def __init__(self, me, total, got, send, recv):
+        self.me, self.total, self.got, self.send, self.recv = me, total, got, send, recv
+
+    def hop(self, s):
+        me, step = self.me, self.STEPS[s]
+        if step is None:
+            device = me.device()
+        else:
+            i = me.at(step[0])
+            j = 3 - i if step[1] == "3" else i + 1 - 2 * lax.rem(i, 2)
+            device = me.device(step[0], j)
+        return pltpu.make_async_remote_copy(
+            src_ref=self.total.at[s], dst_ref=self.got.at[s], send_sem=self.send.at[s], recv_sem=self.recv.at[s],
+            device_id=device, device_id_type=MESH)
+
+    def start(self, s):
+        self.hop(s).start()
+
+    def finish(self, s):
+        self.hop(s).wait_recv()
+        self.total[s + 1] = self.total[s] + self.got[s]
+
+    def drain(self):
+        for s in range(7):
+            self.hop(s).wait_send()
+
+
+def reduce_scratch():
+    sem = pltpu.SemaphoreType.DMA
+    return [
+        pltpu.VMEM((3, 4, 4, 4, 96, 128), BF),
+        pltpu.VMEM((3, 6, 8, 96, 128), BF), pltpu.VMEM((3, 6, 8, 96, 128), BF),
+        pltpu.VMEM((3, 6, 2, 96, 128), BF), pltpu.VMEM((3, 6, 2, 96, 128), BF),
+        pltpu.VMEM((3, 6, 1, 48, 128), F32), pltpu.VMEM((3, 6, 1, 48, 128), F32),
+        pltpu.VMEM((3, 4, 4, 96, 128), F32),
+        pltpu.VMEM((3, 4, 96, 128), F32),
+        pltpu.VMEM((2, 3, 96, 128), F32),
+        pltpu.VMEM((8, 16, 128), F32), pltpu.VMEM((7, 16, 128), F32),
+        sem((54,)), sem((54,)), sem((3,)), sem((3,)), sem((8,)), sem((8,)),
+    ]
+
+
+def reduce_stages(me, g_at, scratch):
+    (r0, s1, d1, s2, d2, s3, d3, t1, t2, fin, gt, gg, send, recv, csend, crecv, gsend, grecv) = scratch
+
+    def load1(c):
+        axis = ORDERS[c][0]
+
+        def load(j, p, m):
+            a, b = 2 * p + m // 4, lax.rem(m, 4)
+            at = {"x": (a, b, j), "y": (j, a, b), "z": (a, j, b)}[axis]
+            return g_at(c, at) + r0[(c,) + at].astype(F32)
+        return load
+
+    def out1(c):
+        def out(p, m, v):
+            t1[c, 2 * p + m // 4, lax.rem(m, 4)] = v
+        return out
+
+    def load2(c):
+        def load(j, p, m):
+            return t1[c, 2 * p + m, j] if c == 2 else t1[c, j, 2 * p + m]
+        return load
+
+    def out2(c):
+        def out(p, m, v):
+            t2[c, 2 * p + m] = v
+        return out
+
+    def load3(c):
+        def load(j, p, m):
+            return t2[c, j, pl.ds(48 * p, 48)]
+        return load
+
+    def out3(c):
+        def out(p, m, v):
+            fin[me.core, c, pl.ds(48 * p, 48)] = v
+        return out
+
+    stages, base = [], 0
+    for c in range(3):
+        row = []
+        for n, (load, out, bufs, count) in enumerate(
+            ((load1, out1, (s1, d1), 8), (load2, out2, (s2, d2), 2), (load3, out3, (s3, d3), 1))
+        ):
+            row.append(ReduceStage(me, ORDERS[c][n], load(c), count, out(c), (bufs[0].at[c], bufs[1].at[c]), (send, recv), base))
+            base += 6
+        stages.append(row)
+    return stages
+
+
+def core_hop(me, g, scratch, c):
+    r0, csend, crecv = scratch[0], scratch[14], scratch[15]
+    return pltpu.make_async_remote_copy(
+        src_ref=g.at[1 - me.core, c], dst_ref=r0.at[c], send_sem=csend.at[c], recv_sem=crecv.at[c],
+        device_id=me.device(), device_id_type=MESH)
+
+
+def run_reduce(me, g_at, hop0, scratch):
+    fin, gt, gg, gsend, grecv = scratch[9], scratch[10], scratch[11], scratch[16], scratch[17]
+    stages = reduce_stages(me, g_at, scratch)
+    gain = GainSum(me, gt, gg, gsend, grecv)
+    gain.start(0)
+    for c in range(3):
+        hop0(c).wait_recv()
+        stages[c][0].start()
+    gain.finish(0)
+    gain.start(1)
+    for c in range(3):
+        stages[c][0].relay()
+    gain.finish(1)
+    gain.start(2)
+    for n in range(3):
+        for c in range(3):
+            stages[c][n].finish()
+            if n < 2:
+                stages[c][n + 1].start()
+        gain.finish(2 * n + 2)
+        if n < 2:
+            gain.start(2 * n + 3)
+            for c in range(3):
+                stages[c][n + 1].relay()
+            gain.finish(2 * n + 3)
+            gain.start(2 * n + 4)
+    last = pltpu.make_async_remote_copy(
+        src_ref=fin.at[me.core], dst_ref=fin.at[me.core], send_sem=gsend.at[7], recv_sem=grecv.at[7],
+        device_id=me.device(), device_id_type=MESH)
+    last.start()
+    arrived = pltpu.make_async_remote_copy(
+        src_ref=fin.at[1 - me.core], dst_ref=fin.at[1 - me.core], send_sem=gsend.at[7], recv_sem=grecv.at[7],
+        device_id=me.device(), device_id_type=MESH)
+    for c in range(3):
+        hop0(c).wait_send()
+        for n in range(3):
+            stages[c][n].drain()
+    gain.drain()
+    last.wait_send()
+    arrived.wait_recv()
+
+
+def reduce_kernel(g, gain, out, gain_out, *scratch):
+    me = Place()
+    scratch[10][0] = gain[...]
+    greet(me)
+
+    def hop0(c):
+        return core_hop(me, g, scratch, c)
+
+    for c in range(3):
+        hop0(c).start()
+    run_reduce(me, lambda c, at: g[(me.core, c) + at].astype(F32), hop0, scratch)
+    out[...] = scratch[9][...]
+    gain_out[...] = scratch[10][7]
+
+
+def reduce_grads(g, gain):
+    vm = pl.BlockSpec(memory_space=pltpu.VMEM)
+    return pl.pallas_call(
+        reduce_kernel,
+        out_shape=(jax.ShapeDtypeStruct((2, 3, 96, 128), F32), jax.ShapeDtypeStruct((16, 128), F32)),
+        in_specs=[vm, vm],
+        out_specs=(vm, vm),
+        scratch_shapes=reduce_scratch(),
+        compiler_params=pltpu.CompilerParams(collective_id=1, has_side_effects=True, vmem_limit_bytes=56 << 20),
+        name="reduce_grads",
+    )(g, gain)
+
+
+def chunks(a, rows):
+    a = a.reshape(2, 4, 2, 4, rows, 2, 3, a.shape[1] // 768 * 128)
+    return a.transpose(5, 6, 0, 2, 1, 3, 4, 7).reshape(2, 3, 4, 4, 4, rows, -1)
+
+
+def pack_grads(gq, gk, gv, go):
+    o = chunks(go, 12).reshape(2, 3, 4, 4, 4, 12, 2, 128).swapaxes(5, 6).reshape(2, 3, 4, 4, 4, 24, 128)
+    return jnp.concatenate([chunks(gq, 24), chunks(gk, 24), chunks(gv, 24), o], 5).astype(BF)
+
+
+def unpack_grads(total):
+    core = lax.rem(lax.axis_index("tm"), 2)
+    parts = []
+    for n in range(3):
+        t = lax.dynamic_slice_in_dim(total[:, :, 24 * n: 24 * n + 24], 12 * core, 12, 2)
+        parts.append(t.transpose(2, 0, 1, 3).reshape(12, 768))
+    o = total[:, :, 72:].reshape(2, 3, 2, 12, 128)
+    o = lax.dynamic_slice_in_dim(o, 6 * core, 6, 3)
+    parts.append(o.transpose(3, 0, 1, 2, 4).reshape(6, 1536))
+    return parts
+
 
 HEADS = 12
 HEAD_DIM = 64
@@ -127,12 +594,10 @@
     normalized_input, standardized_input, inverse_deviation = layer_normalize(
         input_rows, layer_norm_gain
     )
-    full_q, full_k, full_v, full_o = (
-        lax.all_gather(w_query, "dp", axis=0, tiled=True),
-        lax.all_gather(w_key, "dp", axis=0, tiled=True),
-        lax.all_gather(w_value, "dp", axis=0, tiled=True),
-        lax.all_gather(w_out, "dp", axis=0, tiled=True),
-    )
+    own = jnp.concatenate([w_query, w_key, w_value, w_out[:, :768], w_out[:, 768:]], 0)
+    gathered = gather_weights(own.reshape(2, 3, 2, 4, 16, 768)).reshape(8, 48, 16, 768)
+    full_q, full_k, full_v = (gathered[:, 12 * n: 12 * n + 12].reshape(1536, 768) for n in range(3))
+    full_o = jnp.concatenate([gathered[:, 36:42].reshape(768, 768), gathered[:, 42:].reshape(768, 768)], 1)
     query = jnp.dot(normalized_input, full_q, preferred_element_type=jnp.float32).astype(
         jnp.bfloat16
     )
@@ -189,13 +654,13 @@
         normalized_gradient, standardized_input, inverse_deviation, layer_norm_gain
     )
     grad_frames = (grad_y.astype(jnp.float32) + layer_norm_gradient).astype(jnp.bfloat16)
-    owned = (
-        lax.psum_scatter(grad_wq, ("dp", "tm"), scatter_dimension=0, tiled=True),
-        lax.psum_scatter(grad_wk, ("dp", "tm"), scatter_dimension=0, tiled=True),
-        lax.psum_scatter(grad_wv, ("dp", "tm"), scatter_dimension=0, tiled=True),
-        lax.psum_scatter(grad_wo, ("dp", "tm"), scatter_dimension=0, tiled=True),
-        lax.psum_scatter(gain_product, ("dp", "tm"), scatter_dimension=0, tiled=True),
-    )
+    total, gain_total = reduce_grads(
+        pack_grads(grad_wq, grad_wk, grad_wv, grad_wo),
+        jnp.pad(gain_product.reshape(12, 128), ((0, 4), (0, 0))),
+    )
+    owner = lax.axis_index("dp") * 16 + lax.axis_index("tm")
+    gain_own = lax.dynamic_slice_in_dim(gain_total.reshape(2048), owner * 12, 12)
+    owned = unpack_grads(total) + [gain_own]
     return (frames_out[None], grad_frames[None], owned[0], owned[1], owned[2], owned[3], owned[4])
 
 

time: 1170 us -> 192 us (0.16); the launches traced: 1150 us -> 192 us
  blocking collectives: 429 us -> 0 us
  starting transfers between devices: 367 us -> 11 us
  waiting for transfers between devices: 213 us -> 0.01 us
  Pallas kernels: 0 us -> 91.4 us
  local copies, waits for them, and re-layouts: 71.9 us -> 44 us
  matrix products: 46.4 us -> 27.5 us
  between operations: 17.9 us -> 1.94 us
    unnamed x2 -> x0, blocking collectives: 429 us -> none
    unnamed x128 -> x0, starting transfers between devices: 354 us -> none
    all_gather x4 -> x0, waiting for transfers between devices: 208 us -> none  [the longest x1 55.9 us: per_device(): lax.all_gather(w_key, 'dp', axis=0, tiled=True)]
    pallas_call x0 -> x2, Pallas kernels: none -> 91.4 us  [the longest x1 48.2 us: reduce_grads(): pl.pallas_call(reduce_kernel, out_shape=(jax.ShapeDtypeStruct((2, 3, 96,...]
    unnamed x279 -> x76, local copies, waits for them, and re-layouts: 67.2 us -> 12.8 us
  transfers between devices with their start and end apart: 136 -> 4, of which waited for: 7 -> 0; matrix products, arithmetic and copies ran while one was open for 7% -> 15% of each run, Pallas kernels for 0% -> 0%
where the time goes in v1:
time: 192 us
  Pallas kernels  91.4 us (48%)
  local copies, waits for them, and re-layouts  44 us (23%)
  matrix products  27.5 us (14%)
  other arithmetic  15.7 us (8%)
  starting transfers between devices  11 us (6%)
  between operations  1.94 us (1%)
    pallas_call x1, Pallas kernels, reduce_grads(): pl.pallas_call(reduce_kernel, out_shape=(jax.ShapeDtypeStruct((2, 3, 96,...  48.2 us
    pallas_call x1, Pallas kernels, gather_weights(): pl.pallas_call(gather_kernel, out_shape=jax.ShapeDtypeStruct((2, 4) + own...  43.2 us
    unnamed x76, local copies, waits for them, and re-layouts  12.8 us
    transpose x4, local copies, waits for them, and re-layouts, chunks(): return a.transpose(5, 6, 0, 2, 1, 3, 4, 7).reshape(2, 3, 4, 4, 4, rows, -1)  6.39 us
    another operation x1, local copies, waits for them, and re-layouts, pack_grads(): chunks(go, 12).reshape(2, 3, 4, 4, 4, 12, 2, 128).swapaxes(5, 6)  5.88 us
    ppermute x2, starting transfers between devices, shifted(): return lax.ppermute(value, axis, pairs)  5.27 us
    sub x1, matrix products, attend(): expo = jnp.exp(scores - jnp.max(scores, -1, keepdims=True))  4.9 us
    concatenate x1, other arithmetic, pack_grads(): jnp.concatenate([chunks(gq, 24), chunks(gk, 24), chunks(gv, 24), o], 5)  4.79 us
  transfers between devices with their start and end apart: 4, of which 0 were waited for; matrix products, arithmetic and copies ran while one was open for 15% of the time, Pallas kernels for 0%

profile of v1, /device:TPU:1, one launch (start us, length us, event | category | flops | bytes accessed | tf_op | source)
XLA Modules:
  0.0 191.5 jit_solution(2665859941935724067)
XLA Ops:
  5.4 43.2 %gather_weights.1 = bf16[2,4,2,3,2,4,16,768]{7,6,5,4,3,2,1,0:T(8,128)(2,1)S(1)} custom-call(bf16[2,3,2,4,16,768]{5,4,3,2,1,0:T(8,128)(2,1)S(1)} %bitcast.177), custom_call_target="tpu_custom_call" | custom-call | tf_op jit(solution)/shard_map/gather_weights/pallas_call | solution.py:197
  54.5 1.9 collective-permute-start.1
  56.5 3.8 %collective-permute-start = (bf16[128,1536]{1,0:T(8,128)(2,1)}, bf16[128,1536]{1,0:T(8,128)(2,1)}, u32[]{:S(2)}, u32[]{:S(2)}) collective-permute-start(bf16[128,1536]{1,0:T(8,128)(2,1)} %get-tuple-element.51), channel_id=1, source_target_pairs={{0,1},{1,2},{2,3},{3,4},{4,5},{5,6},{6,7},{7,8},{8,9},{9,10},{10,1... | collective-permute-start | bytes 1179656 | tf_op jit(solution)/shard_map/ppermute | solution.py:485
  60.3 1.6 fusion.60
  63.1 1.6 convolution_convert_fusion
  66.6 1.2 copy.56
  68.7 1.2 pad_maximum_fusion.3
  70.9 4.9 %fusion.66 = (f32[12,256]{1,0:T(8,128)S(1)}, f32[12,256,512]{2,1,0:T(8,128)}) fusion(pred[256,512]{1,0:T(8,128)(4,1)S(1)} %copy-done.24, bf16[256,12,64]{0,2,1:T(8,128)(2,1)S(1)} %bitcast.203, bf16[512,12,64]{0,2,1:T(8,128)(2,1)S(1)} %bitcast.199), kind=kOutput, calls=%fused_computation.112 | convolution fusion | flops 207618560 | bytes 7614464 | tf_op jit(solution)/shard_map/sub | solution.py:541
  75.8 4.1 %fusion.35 = bf16[12,64,256]{2,1,0:T(8,128)(2,1)S(1)} fusion(bf16[512,12,64]{0,2,1:T(8,128)(2,1)S(1)} %bitcast.211, f32[12,256,512]{2,1,0:T(8,128)} %get-tuple-element.58, f32[12,256]{1,0:T(8,128)S(1)} %get-tuple-element.57), kind=kOutput, calls=%fused_computation.61 | convolution fusion | flops 204668928 | bytes 7483392 | tf_op jit(solution)/shard_map/hqk,khe->qhe/dot_general | solution.py:544
  80.4 2.0 %multiply_reduce_fusion = (f32[12,256]{1,0:T(8,128)S(1)}, f32[12,256,512]{2,1,0:T(8,128)S(1)}) fusion(f32[12,256,512]{2,1,0:T(8,128)S(1)} %copy-done.9, f32[12,256]{1,0:T(8,128)S(1)} %get-tuple-element.57, bf16[256,12,64]{0,2,1:T(8,128)(2,1)S(1)} %bitcast.215, bf16[512,12,64]{0,2,1:T(8,128)(2,1)S(1)} %bitcast.212), kind=kOutput, calls=%fused_computation.3 | convolution fusion | flops 206042112 | bytes 13787136 | tf_op jit(solution)/shard_map/qhe,khe->hqk/dot_general | solution.py:560
  82.5 1.1 multiply_convert_fusion
  83.6 1.1 fusion.33
  85.7 1.2 fusion.28
  86.8 1.4 fusion.27
  90.1 1.7 fusion.8
  92.7 1.9 collective-permute-start.2
  94.6 3.4 %collective-permute-start.3 = (bf16[128,1536]{0,1:T(8,128)(2,1)}, bf16[128,1536]{0,1:T(8,128)(2,1)}, u32[]{:S(2)}, u32[]{:S(2)}) collective-permute-start(bf16[128,1536]{0,1:T(8,128)(2,1)} %get-tuple-element.43), channel_id=1, source_target_pairs={{1,0},{2,1},{3,2},{4,3},{5,4},{6,5},{7,6},{8,7},{9,8},{10,9},{11,1... | collective-permute-start | bytes 1179656 | tf_op jit(solution)/shard_map/ppermute | solution.py:494
  98.0 1.9 reshape.388
  99.9 2.3 %convert_bitcast_fusion = bf16[2,3,2,2,4,4,12,256]{7,6,1,0,5,3,4,2:T(8,128)(2,1)S(1)} fusion(bf16[2,3,256,256,1,1,1,1]{3,2,1,0,7,6,5,4:T(8,128)(2,1)} %bitcast.198, bf16[2,4,2,4,12,256,1,1]{5,4,3,2,1,0,6,7:T(8,128)(2,1)} %reshape.388), kind=kOutput, calls=%fused_computation.13 | convolution fusion | flops 605159424 | bytes 3538944 | tf_op jit(solution)/shard_map/th,td->hd/dot_general | solution.py:621
  102.2 4.5 %copy.57 = bf16[2,3,2,2,4,4,12,256]{7,5,6,4,3,2,1,0:T(4,128)(2,1)} copy(bf16[2,3,2,2,4,4,12,256]{7,6,1,0,5,3,4,2:T(8,128)(2,1)S(1)} %convert_bitcast_fusion) | data formatting | bytes 4718592 | tf_op jit(solution)/shard_map/transpose | solution.py:453
  106.6 5.9 %reshape_reshape.4 = bf16[2,3,4,4,4,12,2,128]{7,6,4,5,3,2,1,0:T(2,128)(2,1)} reshape(bf16[2,3,2,2,4,4,12,256]{7,5,6,4,3,2,1,0:T(4,128)(2,1)} %copy.57) | data formatting | bytes 4718592 | tf_op jit(solution)/shard_map/reshape;reshape | solution.py:457
  112.5 2.9 %copy.58 = bf16[2,3,4,4,4,2,12,128]{7,4,6,5,3,2,1,0:T(4,128)(2,1)S(1)} copy(bf16[2,3,4,4,4,2,12,128]{7,5,4,6,3,2,1,0:T(2,128)(2,1)} %bitcast.194) | data formatting | bytes 4718592 | tf_op jit(solution)/shard_map/transpose | solution.py:457
  115.4 2.1 %copy.59 = bf16[2,3,4,4,4,24,128]{6,5,4,3,2,1,0:T(8,128)(2,1)} copy(bf16[2,3,4,4,4,24,128]{6,4,5,3,2,1,0:T(4,128)(2,1)S(1)} %bitcast.195) | data formatting | bytes 4718592 | tf_op jit(solution)/shard_map/reshape | solution.py:457
  118.9 1.1 fusion.43
  120.0 1.1 fusion.44
  121.3 1.5 copy-done.5
  124.8 1.3 fusion.22
  126.1 1.6 fusion.39
  133.4 4.8 %pad_maximum_fusion.g = bf16[2,3,4,4,4,96,128]{6,5,4,3,2,1,0:T(8,128)(2,1)} fusion(bf16[2,3,4,4,4,24,128]{6,5,4,3,2,1,0:T(8,128)(2,1)S(1)} %copy-done.1, bf16[2,3,4,4,4,24,128]{6,5,4,3,2,1,0:T(8,128)(2,1)S(1)} %bitcast.187, bf16[2,3,4,4,4,24,128]{6,5,4,3,2,1,0:T(8,128)(2,1)S(1)} %bitcast.188, bf16[2,3,4,4,4,24,128]{6,5,4,3,2,1,0:T(8,128)(2,1)S(1)} %bitcast.189), kind=kLoop, calls=%fused_computation.1 | loop fusion | flops 37748736 | bytes 18874368 | tf_op jit(solution)/shard_map/concatenate | solution.py:458
  138.2 48.2 %reduce_grads.1 = (f32[2,3,96,128]{3,2,1,0:T(8,128)}, f32[16,128]{1,0:T(8,128)}) custom-call(bf16[2,3,4,4,4,96,128]{6,5,4,3,2,1,0:T(8,128)(2,1)} %pad_maximum_fusion.g, f32[16,128]{1,0:T(8,128)} %pad.8.gain), custom_call_target="tpu_custom_call" | custom-call | tf_op jit(solution)/shard_map/reduce_grads/pallas_call | solution.py:440
  186.4 1.0 fusion.65
  190.2 1.3 dynamic_slice.19
  (129 shorter events, 31.0 us)
Async XLA Ops:
  48.6 1.7 copy-start.27
  49.8 1.5 copy-start.4
  49.8 2.2 %copy-start.12 = (bf16[8,12,16,768]{3,2,1,0:T(8,128)(2,1)}, bf16[8,12,16,768]{3,2,1,0:T(8,128)(2,1)S(1)}, u32[]{:S(2)}) copy-start(bf16[8,12,16,768]{3,2,1,0:T(8,128)(2,1)S(1)} %get-tuple-element.41) | copy-start | bytes 7077892
  49.8 13.3 %copy-start.2 = (bf16[8,12,16,768]{3,2,1,0:T(8,128)(2,1)}, bf16[8,12,16,768]{3,2,1,0:T(8,128)(2,1)S(1)}, u32[]{:S(2)}) copy-start(bf16[8,12,16,768]{3,2,1,0:T(8,128)(2,1)S(1)} %get-tuple-element.40) | copy-start | bytes 7077892
  50.0 13.1 %copy-start.25 = (f32[256]{0:T(256)}, f32[256]{0:T(256)S(1)}, u32[]{:S(2)}) copy-start(f32[256]{0:T(256)S(1)} %broadcast_multiply_fusion.2) | copy-start | bytes 3076
  50.3 12.8 %copy-start.29 = (f32[256]{0:T(256)}, f32[256]{0:T(256)S(1)}, u32[]{:S(2)}) copy-start(f32[256]{0:T(256)S(1)} %add_rsqrt_fusion) | copy-start | bytes 3076
  54.5 14.1 %collective-permute-start.1 = (bf16[128,1536]{1,0:T(8,128)(2,1)}, bf16[128,1536]{1,0:T(8,128)(2,1)}, u32[]{:S(2)}, u32[]{:S(2)}) collective-permute-start(bf16[128,1536]{1,0:T(8,128)(2,1)} %get-tuple-element.52), channel_id=1, source_target_pairs={{1,0},{2,1},{3,2},{4,3},{5,4},{6,5},{7,6},{8,7},{9,8},{10,9},{11,1... | collective-permute-start | bytes 1179656 | tf_op jit(solution)/shard_map/ppermute | solution.py:486
  56.5 12.2 %collective-permute-start = (bf16[128,1536]{1,0:T(8,128)(2,1)}, bf16[128,1536]{1,0:T(8,128)(2,1)}, u32[]{:S(2)}, u32[]{:S(2)}) collective-permute-start(bf16[128,1536]{1,0:T(8,128)(2,1)} %get-tuple-element.51), channel_id=1, source_target_pairs={{0,1},{1,2},{2,3},{3,4},{4,5},{5,6},{6,7},{7,8},{8,9},{9,10},{10,1... | collective-permute-start | bytes 1179656 | tf_op jit(solution)/shard_map/ppermute | solution.py:485
  63.1 1.6 copy-start.10
  63.1 2.1 %copy-start.16 = (bf16[8,6,16,768]{3,2,1,0:T(8,128)(2,1)S(1)}, bf16[8,6,16,768]{3,2,1,0:T(8,128)(2,1)}, u32[]{:S(2)}) copy-start(bf16[8,6,16,768]{3,2,1,0:T(8,128)(2,1)} %get-tuple-element.38) | copy-start | bytes 3538948
  63.1 2.1 %copy-start.18 = (bf16[8,6,16,768]{3,2,1,0:T(8,128)(2,1)S(1)}, bf16[8,6,16,768]{3,2,1,0:T(8,128)(2,1)}, u32[]{:S(2)}) copy-start(bf16[8,6,16,768]{3,2,1,0:T(8,128)(2,1)} %get-tuple-element.39) | copy-start | bytes 3538948
  66.1 1.7 copy-start.31
  66.1 1.7 copy-start.32
  66.1 1.7 copy-start.33
  66.1 2.6 %copy-start.15 = (bf16[256,768]{1,0:T(8,128)(2,1)S(1)}, bf16[256,768]{1,0:T(8,128)(2,1)}, u32[]{:S(2)}) copy-start(bf16[256,768]{1,0:T(8,128)(2,1)} %copy-done.14) | copy-start | bytes 1179652
  66.6 13.3 %copy-start.21 = (bf16[256,768]{0,1:T(8,128)(2,1)}, bf16[256,768]{0,1:T(8,128)(2,1)S(1)}, u32[]{:S(2)}) copy-start(bf16[256,768]{0,1:T(8,128)(2,1)S(1)} %copy.51) | copy-start | bytes 1179652
  75.8 4.6 %copy-start.9 = (f32[12,256,512]{2,1,0:T(8,128)S(1)}, f32[12,256,512]{2,1,0:T(8,128)}, u32[]{:S(2)}) copy-start(f32[12,256,512]{2,1,0:T(8,128)} %get-tuple-element.58) | copy-start | bytes 18874372
  79.9 8.5 %copy-start.20 = (bf16[12,64,256]{2,1,0:T(8,128)(2,1)}, bf16[12,64,256]{2,1,0:T(8,128)(2,1)S(1)}, u32[]{:S(2)}) copy-start(bf16[12,64,256]{2,1,0:T(8,128)(2,1)S(1)} %fusion.35) | copy-start | bytes 1179652
  88.2 1.5 copy-start.17
  88.2 1.9 copy-start.19
  88.2 1.9 copy-start.35
  92.7 25.6 %collective-permute-start.2 = (bf16[128,1536]{0,1:T(8,128)(2,1)}, bf16[128,1536]{0,1:T(8,128)(2,1)}, u32[]{:S(2)}, u32[]{:S(2)}) collective-permute-start(bf16[128,1536]{0,1:T(8,128)(2,1)} %get-tuple-element.44), channel_id=1, source_target_pairs={{0,1},{1,2},{2,3},{3,4},{4,5},{5,6},{6,7},{7,8},{8,9},{9,10},{10,1... | collective-permute-start | bytes 1179656 | tf_op jit(solution)/shard_map/ppermute | solution.py:494
  94.6 25.4 %collective-permute-start.3 = (bf16[128,1536]{0,1:T(8,128)(2,1)}, bf16[128,1536]{0,1:T(8,128)(2,1)}, u32[]{:S(2)}, u32[]{:S(2)}) collective-permute-start(bf16[128,1536]{0,1:T(8,128)(2,1)} %get-tuple-element.43), channel_id=1, source_target_pairs={{1,0},{2,1},{3,2},{4,3},{5,4},{6,5},{7,6},{8,7},{9,8},{10,9},{11,1... | collective-permute-start | bytes 1179656 | tf_op jit(solution)/shard_map/ppermute | solution.py:494
  115.4 2.1 %copy-start.3 = (bf16[8,12,16,768]{3,2,1,0:T(8,128)(2,1)S(1)}, bf16[8,12,16,768]{3,2,1,0:T(8,128)(2,1)}, u32[]{:S(2)}) copy-start(bf16[8,12,16,768]{3,2,1,0:T(8,128)(2,1)} %copy-done.2) | copy-start | bytes 7077892
  117.5 1.4 copy-start
  121.2 1.7 copy-start.5
  122.8 1.9 copy-start.13
  122.8 1.9 %copy-start.26 = (f32[256]{0:T(256)S(1)}, f32[256]{0:T(256)}, u32[]{:S(2)}) copy-start(f32[256]{0:T(256)} %copy-done.25) | copy-start | bytes 3076
  122.8 1.9 %copy-start.28 = (f32[1536]{0:T(1024)S(1)}, f32[1536]{0:T(1024)}, u32[]{:S(2)}) copy-start(f32[1536]{0:T(1024)} %param.16) | copy-start | bytes 18436
  122.8 1.9 copy-start.30
  124.8 1.4 copy-start.11
  131.8 1.7 copy-start.1
  (8 other events, 7.6 us)

commit v2 on v1

--- a/solution.py
+++ b/solution.py
@@ -43,13 +43,13 @@
         return lax.rem(self.at(axis) + 2, 4)
 
 
-def greet(me):
+def greet(me, far=False):
     barrier = pltpu.get_barrier_semaphore()
     for axis in "xyz":
-        for j in (me.left(axis), me.right(axis)):
+        for j in (me.left(axis), me.right(axis)) + ((me.over(axis),) if far else ()):
             pl.semaphore_signal(barrier, inc=1, device_id=me.device(axis, j), device_id_type=MESH)
     pl.semaphore_signal(barrier, inc=1, device_id=me.device(), device_id_type=MESH)
-    pl.semaphore_wait(barrier, 7)
+    pl.semaphore_wait(barrier, 10 if far else 7)
 
 
 def gather_regions(me, w, h):
@@ -149,14 +149,24 @@
 GATHER_SEMS = 84
 
 
-def run_gather(me, w_own, w, send, recv, local):
-    own = (
-        pltpu.make_async_copy(w_own.at[:, pl.ds(0, 2), me.yl], w.at[me.yh, me.z, :, pl.ds(0, 2), me.yl], local.at[0]),
-        pltpu.make_async_copy(w_own.at[:, 2, me.yl, me.x], w.at[me.yh, me.z, :, 2, me.yl, me.x], local.at[1]),
-    )
+def run_gather(me, shards, held, w, send, recv, local):
+    wq, wk, wv, wo = shards
+    loads = [pltpu.make_async_copy(part, held.at[pl.ds(12 * n, 12)], local.at[n]) for n, part in enumerate((wq, wk, wv))]
+    for n in range(2):
+        loads.append(pltpu.make_async_copy(wo.at[:, :, pl.ds(768 * n, 768)], held.at[pl.ds(36 + 6 * n, 6)], local.at[3 + n]))
+    for copy in loads:
+        copy.start()
+    greet(me)
+    for copy in loads:
+        copy.wait()
+    own = []
+    for h in range(2):
+        for c in range(2):
+            own.append((held.at[pl.ds(24 * h + 8 * c + 4 * me.yl, 4)], w.at[me.yh, me.z, h, c, me.yl]))
+        own.append((held.at[24 * h + 16 + 4 * me.yl + me.x], w.at[me.yh, me.z, h, 2, me.yl, me.x]))
+    own = [pltpu.make_async_copy(src, dst, local.at[n]) for n, (src, dst) in enumerate(own)]
     for copy in own:
         copy.start()
-    greet(me)
     for copy in own:
         copy.wait()
     a, b, c = gather_stages(me, w, send, recv)
@@ -189,24 +199,25 @@
             stage.drain()
 
 
-def gather_kernel(w_own, w, send, recv, local):
-    run_gather(Place(), w_own, w, send, recv, local)
-
-
-def gather_weights(own):
+def gather_kernel(wq, wk, wv, wo, w, held, send, recv, local):
+    run_gather(Place(), (wq, wk, wv, wo), held, w, send, recv, local)
+
+
+def gather_weights(wq, wk, wv, wo):
     return pl.pallas_call(
         gather_kernel,
-        out_shape=jax.ShapeDtypeStruct((2, 4) + own.shape, BF),
-        in_specs=[pl.BlockSpec(memory_space=pltpu.VMEM)],
+        out_shape=jax.ShapeDtypeStruct((2, 4, 2, 3, 2, 4, 16, 768), BF),
+        in_specs=[pl.BlockSpec(memory_space=pl.ANY)] * 4,
         out_specs=pl.BlockSpec(memory_space=pltpu.VMEM),
         scratch_shapes=[
+            pltpu.VMEM((48, 16, 768), BF),
             pltpu.SemaphoreType.DMA((GATHER_SEMS,)),
             pltpu.SemaphoreType.DMA((GATHER_SEMS,)),
-            pltpu.SemaphoreType.DMA((2,)),
+            pltpu.SemaphoreType.DMA((6,)),
         ],
         compiler_params=pltpu.CompilerParams(collective_id=0, has_side_effects=True, vmem_limit_bytes=40 << 20),
         name="gather_weights",
-    )(own)
+    )(wq.reshape(12, 16, 768), wk.reshape(12, 16, 768), wv.reshape(12, 16, 768), wo.reshape(6, 16, 1536))
 
 
 ORDERS = (("x", "y", "z"), ("y", "z", "x"), ("z", "x", "y"))
@@ -278,33 +289,38 @@
 
 
 class GainSum:
-    STEPS = (None, "x1", "x3", "y1", "y3", "z1", "z3")
-
     def __init__(self, me, total, got, send, recv):
         self.me, self.total, self.got, self.send, self.recv = me, total, got, send, recv
 
-    def hop(self, s):
-        me, step = self.me, self.STEPS[s]
-        if step is None:
-            device = me.device()
+    def hops(self, s):
+        me = self.me
+        if s == 3:
+            devices = (me.device(),)
         else:
-            i = me.at(step[0])
-            j = 3 - i if step[1] == "3" else i + 1 - 2 * lax.rem(i, 2)
-            device = me.device(step[0], j)
-        return pltpu.make_async_remote_copy(
-            src_ref=self.total.at[s], dst_ref=self.got.at[s], send_sem=self.send.at[s], recv_sem=self.recv.at[s],
-            device_id=device, device_id_type=MESH)
+            axis = "xyz"[s]
+            devices = tuple(me.device(axis, j) for j in (me.right(axis), me.left(axis), me.over(axis)))
+        return [
+            pltpu.make_async_remote_copy(
+                src_ref=self.total.at[s], dst_ref=self.got.at[3 * s + n], send_sem=self.send.at[3 * s + n],
+                recv_sem=self.recv.at[3 * s + n], device_id=device, device_id_type=MESH)
+            for n, device in enumerate(devices)
+        ]
 
     def start(self, s):
-        self.hop(s).start()
+        for hop in self.hops(s):
+            hop.start()
 
     def finish(self, s):
-        self.hop(s).wait_recv()
-        self.total[s + 1] = self.total[s] + self.got[s]
+        v = self.total[s]
+        for n, hop in enumerate(self.hops(s)):
+            hop.wait_recv()
+            v = v + self.got[3 * s + n]
+        self.total[s + 1] = v
 
     def drain(self):
-        for s in range(7):
-            self.hop(s).wait_send()
+        for s in range(4):
+            for hop in self.hops(s):
+                hop.wait_send()
 
 
 def reduce_scratch():
@@ -317,13 +333,18 @@
         pltpu.VMEM((3, 4, 4, 96, 128), F32),
         pltpu.VMEM((3, 4, 96, 128), F32),
         pltpu.VMEM((2, 3, 96, 128), F32),
-        pltpu.VMEM((8, 16, 128), F32), pltpu.VMEM((7, 16, 128), F32),
-        sem((54,)), sem((54,)), sem((3,)), sem((3,)), sem((8,)), sem((8,)),
+        pltpu.VMEM((5, 16, 128), F32), pltpu.VMEM((10, 16, 128), F32),
+        sem((54,)), sem((54,)), sem((3,)), sem((3,)), sem((11,)), sem((11,)),
+        pltpu.VMEM((3, 4, 4, 4, 96, 128), BF),
+        pltpu.VMEM((3, 4, 4, 4, 96, 128), F32),
+        pltpu.VMEM((1536, 256), BF), pltpu.VMEM((768, 256), BF),
+        pltpu.VMEM((1536, 384), F32), pltpu.VMEM((768, 256), F32),
+        pltpu.VMEM((256, 1536), F32), pltpu.VMEM((256, 1536), F32),
     ]
 
 
-def reduce_stages(me, g_at, scratch):
-    (r0, s1, d1, s2, d2, s3, d3, t1, t2, fin, gt, gg, send, recv, csend, crecv, gsend, grecv) = scratch
+def reduce_stages(me, half, scratch):
+    (r0, s1, d1, s2, d2, s3, d3, t1, t2, fin, gt, gg, send, recv, csend, crecv, gsend, grecv) = scratch[:18]
 
     def load1(c):
         axis = ORDERS[c][0]
@@ -331,7 +352,7 @@
         def load(j, p, m):
             a, b = 2 * p + m // 4, lax.rem(m, 4)
             at = {"x": (a, b, j), "y": (j, a, b), "z": (a, j, b)}[axis]
-            return g_at(c, at) + r0[(c,) + at].astype(F32)
+            return half[(c,) + at]
         return load
 
     def out1(c):
@@ -371,103 +392,162 @@
     return stages
 
 
-def core_hop(me, g, scratch, c):
-    r0, csend, crecv = scratch[0], scratch[14], scratch[15]
+def core_hop(me, scratch, c):
+    r0, csend, crecv, g = scratch[0], scratch[14], scratch[15], scratch[18]
     return pltpu.make_async_remote_copy(
-        src_ref=g.at[1 - me.core, c], dst_ref=r0.at[c], send_sem=csend.at[c], recv_sem=crecv.at[c],
+        src_ref=g.at[c], dst_ref=r0.at[c], send_sem=csend.at[c], recv_sem=crecv.at[c],
         device_id=me.device(), device_id_type=MESH)
 
 
-def run_reduce(me, g_at, hop0, scratch):
-    fin, gt, gg, gsend, grecv = scratch[9], scratch[10], scratch[11], scratch[16], scratch[17]
-    stages = reduce_stages(me, g_at, scratch)
-    gain = GainSum(me, gt, gg, gsend, grecv)
-    gain.start(0)
+def weight_terms(refs, scratch, h, c, put):
+    gq, gk, gv, masked = refs
+    nt, ct, prod, prod_o = scratch[20:24]
+    columns = pl.ds(pl.multiple_of(h * 384 + c * 128, 128), 128)
+    rhs = jnp.concatenate([gq[:, columns], gk[:, columns], gv[:, columns]], 1)
+    prod[...] = jnp.dot(nt[...], rhs, preferred_element_type=F32)
+    columns = pl.ds(pl.multiple_of(h * 768 + c * 256, 128), 256)
+    prod_o[...] = jnp.dot(ct[...], masked[:, columns], preferred_element_type=F32)
+
+    @pl.loop(0, 32)
+    def _(pair):
+        upper = lax.broadcasted_iota(jnp.int32, (8, 128), 0) < 4
+        at = pl.multiple_of(pair * 24, 8)
+        tiles = [[prod_o[pl.ds(at + 8 * n, 8), pl.ds(128 * b, 128)] for b in range(2)] for n in range(3)]
+        mixed = (
+            jnp.where(upper, tiles[1][0], pltpu.roll(tiles[1][1], 4, 0)),
+            jnp.where(upper, pltpu.roll(tiles[1][0], 4, 0), tiles[1][1]),
+        )
+        yh, z, yl, xh = pair // 16, lax.rem(pair // 4, 4), lax.rem(pair // 2, 2), lax.rem(pair, 2)
+        for odd in range(2):
+            rows = pl.ds(pl.multiple_of(pair * 48 + 24 * odd, 8), 24)
+            parts = [prod[rows, pl.ds(128 * n, 128)] for n in range(3)]
+            parts += [tiles[2 * odd][0], tiles[2 * odd][1], mixed[odd]]
+            put((yh * 2 + yl, z, xh * 2 + odd), jnp.concatenate(parts, 0))
+
+
+def norm(frames):
+    xf = frames.astype(F32)
+    mean = jnp.mean(xf, -1, keepdims=True)
+    centered = xf - mean
+    var = jnp.mean(centered * centered, -1, keepdims=True)
+    inverse = lax.rsqrt(var + 1e-05)
+    return centered * inverse, inverse
+
+
+def grad_normed(w, gq, gk, gv, out):
+    for s in range(4):
+        total = None
+        for n, g in enumerate((gq, gk, gv)):
+            rows = w[2 * s: 2 * s + 2, 12 * n: 12 * n + 12].reshape(384, 768)
+            term = lax.dot_general(g[...], rows, (((1,), (1,)), ((), ())), preferred_element_type=F32)
+            total = term if total is None else total + term
+        out[:, 384 * s: 384 * s + 384] = total
+
+
+def norm_backward(frames, cotangent, gain, gn, gx, grad_frames, gain_total):
+    @pl.loop(0, 8)
+    def _(n):
+        rows = pl.ds(pl.multiple_of(n * 32, 32), 32)
+        xhat, inverse = norm(frames[rows])
+        grad = gn[rows]
+        gx[rows] = grad * xhat
+        g = grad * gain[...]
+        first = jnp.mean(g, -1, keepdims=True)
+        second = jnp.mean(g * xhat, -1, keepdims=True)
+        back = inverse * (g - first - xhat * second)
+        grad_frames[rows] = (cotangent[rows].astype(F32) + back).astype(BF)
+
+    gain_total[0] = jnp.zeros((16, 128), F32)
+    for b in range(12):
+        gain_total[0, b:b + 1] = jnp.sum(gx[:, 128 * b: 128 * b + 128], 0, keepdims=True)
+
+
+def reduce_kernel(
+    normed, gq, gk, gv, context, masked, w, frames, cotangent, gain,
+    out_q, out_k, out_v, out_o, gain_out, grad_frames, *scratch
+):
+    me = Place()
+    r0, fin, gt, gg, gsend, grecv = scratch[0], scratch[9], scratch[10], scratch[11], scratch[16], scratch[17]
+    for_other, half, nt, ct = scratch[18:22]
+    gn, gx = scratch[24:26]
+    nt[...] = normed[...].T
+    ct[...] = context[...].T
+    refs = (gq, gk, gv, masked)
+    greet(me, far=True)
     for c in range(3):
-        hop0(c).wait_recv()
+        def put(at, v, c=c):
+            for_other[(c,) + at] = v.astype(BF)
+        weight_terms(refs, scratch, 1 - me.core, c, put)
+        core_hop(me, scratch, c).start()
+    stages = reduce_stages(me, half, scratch)
+    sum_gain = GainSum(me, gt, gg, gsend, grecv)
+    for c in range(3):
+        core_hop(me, scratch, c).wait_recv()
+
+        def put(at, v, c=c):
+            half[(c,) + at] = v + r0[(c,) + at].astype(F32)
+        weight_terms(refs, scratch, me.core, c, put)
         stages[c][0].start()
-    gain.finish(0)
-    gain.start(1)
+    grad_normed(w, gq, gk, gv, gn)
     for c in range(3):
         stages[c][0].relay()
-    gain.finish(1)
-    gain.start(2)
+    norm_backward(frames, cotangent, gain, gn, gx, grad_frames, gt)
+    sum_gain.start(0)
     for n in range(3):
         for c in range(3):
             stages[c][n].finish()
             if n < 2:
                 stages[c][n + 1].start()
-        gain.finish(2 * n + 2)
+        sum_gain.finish(n)
+        sum_gain.start(n + 1)
         if n < 2:
-            gain.start(2 * n + 3)
             for c in range(3):
                 stages[c][n + 1].relay()
-            gain.finish(2 * n + 3)
-            gain.start(2 * n + 4)
-    last = pltpu.make_async_remote_copy(
-        src_ref=fin.at[me.core], dst_ref=fin.at[me.core], send_sem=gsend.at[7], recv_sem=grecv.at[7],
-        device_id=me.device(), device_id_type=MESH)
-    last.start()
-    arrived = pltpu.make_async_remote_copy(
-        src_ref=fin.at[1 - me.core], dst_ref=fin.at[1 - me.core], send_sem=gsend.at[7], recv_sem=grecv.at[7],
-        device_id=me.device(), device_id_type=MESH)
+
+    def last(core):
+        return pltpu.make_async_remote_copy(
+            src_ref=fin.at[core], dst_ref=fin.at[core], send_sem=gsend.at[10], recv_sem=grecv.at[10],
+            device_id=me.device(), device_id_type=MESH)
+
+    last(me.core).start()
+    sum_gain.finish(3)
+    gain_out[...] = gt[4]
     for c in range(3):
-        hop0(c).wait_send()
+        core_hop(me, scratch, c).wait_send()
         for n in range(3):
             stages[c][n].drain()
-    gain.drain()
-    last.wait_send()
-    arrived.wait_recv()
-
-
-def reduce_kernel(g, gain, out, gain_out, *scratch):
-    me = Place()
-    scratch[10][0] = gain[...]
-    greet(me)
-
-    def hop0(c):
-        return core_hop(me, g, scratch, c)
-
-    for c in range(3):
-        hop0(c).start()
-    run_reduce(me, lambda c, at: g[(me.core, c) + at].astype(F32), hop0, scratch)
-    out[...] = scratch[9][...]
-    gain_out[...] = scratch[10][7]
-
-
-def reduce_grads(g, gain):
+    sum_gain.drain()
+    last(me.core).wait_send()
+    last(1 - me.core).wait_recv()
+    odd = lax.rem(me.x, 2)
+    for h in range(2):
+        for c in range(3):
+            lanes = pl.ds(384 * h + 128 * c, 128)
+            for n, out in enumerate((out_q, out_k, out_v)):
+                t = fin[h, c, pl.ds(24 * n, 24)]
+                out[:, lanes] = jnp.where(me.core == 0, t[:12], t[12:])
+            for b in range(2):
+                lanes = pl.ds(768 * h + 256 * c + 128 * b, 128)
+                for r in range(6):
+                    even0, even1 = 8 * b + r, 8 * b + 6 + r if r < 2 else 14 + 4 * b + r
+                    odd0, odd1 = 16 + 4 * b + r if r < 4 else 8 * b + r - 4, 8 * b + 2 + r
+                    row = 72 + jnp.where(
+                        odd == 0, jnp.where(me.core == 0, even0, even1), jnp.where(me.core == 0, odd0, odd1))
+                    out_o[r:r + 1, lanes] = fin[h, c, pl.ds(row, 1)]
+
+
+def reduce_grads(*args):
     vm = pl.BlockSpec(memory_space=pltpu.VMEM)
+    sds = jax.ShapeDtypeStruct
     return pl.pallas_call(
         reduce_kernel,
-        out_shape=(jax.ShapeDtypeStruct((2, 3, 96, 128), F32), jax.ShapeDtypeStruct((16, 128), F32)),
-        in_specs=[vm, vm],
-        out_specs=(vm, vm),
+        out_shape=(sds((12, 768), F32),) * 3 + (sds((6, 1536), F32), sds((16, 128), F32), sds((256, 1536), BF)),
+        in_specs=[vm] * 10,
+        out_specs=(vm,) * 6,
         scratch_shapes=reduce_scratch(),
-        compiler_params=pltpu.CompilerParams(collective_id=1, has_side_effects=True, vmem_limit_bytes=56 << 20),
+        compiler_params=pltpu.CompilerParams(collective_id=1, has_side_effects=True, vmem_limit_bytes=62 << 20),
         name="reduce_grads",
-    )(g, gain)
-
-
-def chunks(a, rows):
-    a = a.reshape(2, 4, 2, 4, rows, 2, 3, a.shape[1] // 768 * 128)
-    return a.transpose(5, 6, 0, 2, 1, 3, 4, 7).reshape(2, 3, 4, 4, 4, rows, -1)
-
-
-def pack_grads(gq, gk, gv, go):
-    o = chunks(go, 12).reshape(2, 3, 4, 4, 4, 12, 2, 128).swapaxes(5, 6).reshape(2, 3, 4, 4, 4, 24, 128)
-    return jnp.concatenate([chunks(gq, 24), chunks(gk, 24), chunks(gv, 24), o], 5).astype(BF)
-
-
-def unpack_grads(total):
-    core = lax.rem(lax.axis_index("tm"), 2)
-    parts = []
-    for n in range(3):
-        t = lax.dynamic_slice_in_dim(total[:, :, 24 * n: 24 * n + 24], 12 * core, 12, 2)
-        parts.append(t.transpose(2, 0, 1, 3).reshape(12, 768))
-    o = total[:, :, 72:].reshape(2, 3, 2, 12, 128)
-    o = lax.dynamic_slice_in_dim(o, 6 * core, 6, 3)
-    parts.append(o.transpose(3, 0, 1, 2, 4).reshape(6, 1536))
-    return parts
+    )(*args)
 
 
 HEADS = 12
@@ -508,17 +588,6 @@
     )
 
 
-def layer_normalize_backward(normalized_gradient, standardized_input, inverse_deviation, norm_gain):
-    scaled_output = normalized_gradient * norm_gain
-    gain_gradient = jnp.sum(normalized_gradient * standardized_input, 0)
-    first_term = jnp.mean(scaled_output, -1, keepdims=True)
-    second_term = jnp.mean(scaled_output * standardized_input, -1, keepdims=True)
-    return (
-        inverse_deviation * (scaled_output - first_term - standardized_input * second_term),
-        gain_gradient,
-    )
-
-
 def window_mask(lo, hi, length, qpos, kpos):
     kp = kpos[None, :]
     inside = (kp >= lo[:, None]) & (kp < hi[:, None]) & (kp < length)
@@ -594,8 +663,7 @@
     normalized_input, standardized_input, inverse_deviation = layer_normalize(
         input_rows, layer_norm_gain
     )
-    own = jnp.concatenate([w_query, w_key, w_value, w_out[:, :768], w_out[:, 768:]], 0)
-    gathered = gather_weights(own.reshape(2, 3, 2, 4, 16, 768)).reshape(8, 48, 16, 768)
+    gathered = gather_weights(w_query, w_key, w_value, w_out).reshape(8, 48, 16, 768)
     full_q, full_k, full_v = (gathered[:, 12 * n: 12 * n + 12].reshape(1536, 768) for n in range(3))
     full_o = jnp.concatenate([gathered[:, 36:42].reshape(768, 768), gathered[:, 42:].reshape(768, 768)], 1)
     query = jnp.dot(normalized_input, full_q, preferred_element_type=jnp.float32).astype(
@@ -618,7 +686,6 @@
         jnp.bfloat16
     )
     masked_grad = jnp.where(valid[:, None], grad_y, jnp.zeros_like(grad_y))
-    grad_wo = jnp.einsum("th,td->hd", context, masked_grad, preferred_element_type=jnp.float32)
     grad_context = jnp.einsum(
         "td,hd->th", masked_grad, full_o, preferred_element_type=jnp.float32
     ).astype(jnp.bfloat16)
@@ -636,31 +703,12 @@
     grad_kv = center.astype(jnp.bfloat16)
     grad_key = grad_kv[:, :width]
     grad_value = grad_kv[:, width:]
-    grad_wq = jnp.einsum(
-        "td,th->dh", normalized_input, grad_query, preferred_element_type=jnp.float32
-    )
-    grad_wk = jnp.einsum(
-        "td,th->dh", normalized_input, grad_key, preferred_element_type=jnp.float32
-    )
-    grad_wv = jnp.einsum(
-        "td,th->dh", normalized_input, grad_value, preferred_element_type=jnp.float32
-    )
-    normalized_gradient = (
-        jnp.einsum("th,dh->td", grad_query, full_q, preferred_element_type=jnp.float32)
-        + jnp.einsum("th,dh->td", grad_key, full_k, preferred_element_type=jnp.float32)
-        + jnp.einsum("th,dh->td", grad_value, full_v, preferred_element_type=jnp.float32)
-    )
-    layer_norm_gradient, gain_product = layer_normalize_backward(
-        normalized_gradient, standardized_input, inverse_deviation, layer_norm_gain
-    )
-    grad_frames = (grad_y.astype(jnp.float32) + layer_norm_gradient).astype(jnp.bfloat16)
-    total, gain_total = reduce_grads(
-        pack_grads(grad_wq, grad_wk, grad_wv, grad_wo),
-        jnp.pad(gain_product.reshape(12, 128), ((0, 4), (0, 0))),
+    *owned, gain_total, grad_frames = reduce_grads(
+        normalized_input, grad_query, grad_key, grad_value, context, masked_grad, gathered,
+        input_rows, grad_y, layer_norm_gain[None],
     )
     owner = lax.axis_index("dp") * 16 + lax.axis_index("tm")
-    gain_own = lax.dynamic_slice_in_dim(gain_total.reshape(2048), owner * 12, 12)
-    owned = unpack_grads(total) + [gain_own]
+    owned.append(lax.dynamic_slice_in_dim(gain_total.reshape(2048), owner * 12, 12))
     return (frames_out[None], grad_frames[None], owned[0], owned[1], owned[2], owned[3], owned[4])
 
 

time: 192 us -> 175 us (0.911)
  local copies, waits for them, and re-layouts: 44 us -> 28.1 us
  other arithmetic: 15.7 us -> 8.81 us
  Pallas kernels: 91.4 us -> 97.4 us
    transpose x13 -> x0, local copies, waits for them, and re-layouts: 9.4 us -> none  [the longest x4 6.39 us: chunks(): return a.transpose(5, 6, 0, 2, 1, 3, 4, 7).reshape(2, 3, 4, 4, 4, rows, -1)]
    dot_general x7 -> x0, matrix products: 7.76 us -> none  [the longest x1 2.31 us: per_device(): jnp.einsum('th,td->hd', context, masked_grad, preferred_element_type=jnp....]
    pallas_call x2, Pallas kernels: 91.4 us -> 97.4 us  [the longest x1 53.6 us: reduce_grads(): pl.pallas_call(reduce_kernel, out_shape=(sds((12, 768), F32),) * 3 + (sds...]
    another operation x1 -> x0, local copies, waits for them, and re-layouts: 5.88 us -> none  [pack_grads(): chunks(go, 12).reshape(2, 3, 4, 4, 4, 12, 2, 128).swapaxes(5, 6)]
    concatenate x1 -> x0, other arithmetic: 4.79 us -> none  [pack_grads(): jnp.concatenate([chunks(gq, 24), chunks(gk, 24), chunks(gv, 24), o], 5)]
    dot_general x3 -> x0, local copies, waits for them, and re-layouts: 3.32 us -> none  [the longest x2 3.05 us: per_device(): jnp.einsum('th,td->hd', context, masked_grad, preferred_element_type=jnp....]
    convert_element_type x0 -> x2, local copies, waits for them, and re-layouts: none -> 2.83 us  [the longest x1 1.91 us: attend(): context.reshape(query.shape[0], HEADS * HEAD_DIM).astype(jnp.bfloat16)]
    reshape x5 -> x2, local copies, waits for them, and re-layouts: 4.63 us -> 2.34 us  [the longest x1 1.87 us: attend_back(): grad_value.reshape(key.shape[0], width)]
  transfers between devices with their start and end apart: 4 -> 4, of which waited for: 0 -> 0; matrix products, arithmetic and copies ran while one was open for 15% -> 13% of each run, Pallas kernels for 0% -> 0%
where the time goes in v2:
time: 175 us
  Pallas kernels  97.4 us (56%)
  local copies, waits for them, and re-layouts  28.1 us (16%)
  matrix products  27.5 us (16%)
  starting transfers between devices  11.2 us (6%)
  other arithmetic  8.81 us (5%)
    pallas_call x1, Pallas kernels, reduce_grads(): pl.pallas_call(reduce_kernel, out_shape=(sds((12, 768), F32),) * 3 + (sds...  53.6 us
    pallas_call x1, Pallas kernels, gather_weights(): pl.pallas_call(gather_kernel, out_shape=jax.ShapeDtypeStruct((2, 4, 2, 3,...  43.8 us
    unnamed x49, local copies, waits for them, and re-layouts  12.9 us
    ppermute x2, starting transfers between devices, shifted(): return lax.ppermute(value, axis, pairs)  5.43 us
    sub x1, matrix products, attend(): expo = jnp.exp(scores - jnp.max(scores, -1, keepdims=True))  4.94 us
    dot_general x1, matrix products, attend(): jnp.einsum('hqk,khe->qhe', probs_low, split_heads(value), preferred_eleme...  4.86 us
    ppermute x1, starting transfers between devices, extended_2(): before = lax.ppermute(last, axis, up)  3.82 us
    dot_general x1, matrix products, per_device(): attn = jnp.dot(context, full_o, preferred_element_type=jnp.float32)  3.76 us
  transfers between devices with their start and end apart: 4, of which 0 were waited for; matrix products, arithmetic and copies ran while one was open for 13% of the time, Pallas kernels for 0%

profile of v2, /device:TPU:1, one launch (start us, length us, event | category | flops | bytes accessed | tf_op | source)
XLA Modules:
  0.0 174.6 jit_solution(11697024324168612647)
XLA Ops:
  1.6 1.0 copy-done.2
  2.6 1.0 copy-done.3
  3.5 1.0 copy-done.4
  4.5 43.8 %gather_weights.1 = bf16[2,4,2,3,2,4,16,768]{7,6,5,4,3,2,1,0:T(8,128)(2,1)S(1)} custom-call(bf16[12,16,768]{2,1,0:T(8,128)(2,1)S(1)} %bitcast.67, bf16[12,16,768]{2,1,0:T(8,128)(2,1)S(1)} %bitcast.68, bf16[12,16,768]{2,1,0:T(8,128)(2,1)S(1)} %bitcast.69, bf16[6,16,1536]{2,1,0:T(8,128)(2,1)S(1)} %bitcast.70), custom_call_target="tpu_custom_call" | custom-call | tf_op jit(solution)/shard_map/gather_weights/pallas_call | solution.py:207
  48.3 2.0 %fusion.41 = (bf16[8,12,16,768]{3,2,1,0:T(8,128)(2,1)}, bf16[8,12,16,768]{3,2,1,0:T(8,128)(2,1)S(1)}, bf16[8,12,16,768]{3,2,1,0:T(8,128)(2,1)S(1)}) fusion(bf16[8,48,16,768]{3,2,1,0:T(8,128)(2,1)S(1)} %bitcast.64), kind=kLoop, calls=%fused_computation.68 | loop fusion | bytes 14155776 | tf_op jit(solution)/shard_map/slice | solution.py:667
  53.6 1.9 %collective-permute-start.1 = (bf16[128,1536]{1,0:T(8,128)(2,1)}, bf16[128,1536]{1,0:T(8,128)(2,1)S(1)}, u32[]{:S(2)}, u32[]{:S(2)}) collective-permute-start(bf16[128,1536]{1,0:T(8,128)(2,1)} %get-tuple-element.55), channel_id=1, source_target_pairs={{1,0},{2,1},{3,2},{4,3},{5,4},{6,5},{7,6},{8,7},{9,8},{10,9},{11,1... | collective-permute-start | bytes 1179656 | tf_op jit(solution)/shard_map/ppermute | solution.py:566
  55.5 3.8 %collective-permute-start = (bf16[128,1536]{1,0:T(8,128)(2,1)}, bf16[128,1536]{1,0:T(8,128)(2,1)S(1)}, u32[]{:S(2)}, u32[]{:S(2)}) collective-permute-start(bf16[128,1536]{1,0:T(8,128)(2,1)} %get-tuple-element.54), channel_id=1, source_target_pairs={{0,1},{1,2},{2,3},{3,4},{4,5},{5,6},{6,7},{7,8},{8,9},{9,10},{10,1... | collective-permute-start | bytes 1179656 | tf_op jit(solution)/shard_map/ppermute | solution.py:565
  59.3 1.6 fusion.40
  63.2 3.3 %convolution_convert_fusion = bf16[256,768]{1,0:T(8,128)(2,1)} fusion(bf16[1536,768]{1,0:T(8,128)(2,1)} %bitcast.76, bf16[1,256,1536]{2,1,0:T(8,128)(2,1)S(1)} %copy-done.5, f32[1536]{0:T(1024)S(1)} %copy-done.13, f32[256]{0:T(256)S(1)} %add_rsqrt_fusion, f32[256]{0:T(256)S(1)} %broadcast_multiply_fusion), kind=kOutput, calls=%fused_computation.41 | convolution fusion | flops 606142464 | bytes 3547136 | tf_op jit(solution)/shard_map/dot_general | solution.py:669
  66.6 1.2 copy.30
  68.8 2.5 %fusion.21 = bf16[256,768]{1,0:T(8,128)(2,1)S(1)} fusion(bf16[256,1536]{1,0:T(8,128)(2,1)S(1)} %broadcast_select_fusion.masked, bf16[768,768]{1,0:T(8,128)(2,1)} %bitcast.85, bf16[768,768]{1,0:T(8,128)(2,1)} %bitcast.83), kind=kOutput, calls=%fused_computation.39 | convolution fusion | flops 608894976 | bytes 3538944 | tf_op jit(solution)/shard_map/td,hd->th/dot_general | solution.py:689
  73.1 1.2 fusion.13.normed
  75.5 4.9 %fusion.45 = (f32[12,256]{1,0:T(8,128)S(1)}, f32[12,256,512]{2,1,0:T(8,128)}) fusion(pred[256,512]{1,0:T(8,128)(4,1)S(1)} %copy-done.12, bf16[256,12,64]{0,2,1:T(8,128)(2,1)S(1)} %bitcast.80, bf16[512,12,64]{0,2,1:T(8,128)(2,1)S(1)} %bitcast.74), kind=kOutput, calls=%fused_computation.72 | convolution fusion | flops 207618560 | bytes 7614464 | tf_op jit(solution)/shard_map/sub | solution.py:610
  80.4 4.9 %fusion.22 = bf16[12,64,256]{2,1,0:T(8,128)(2,1)} fusion(bf16[512,12,64]{0,2,1:T(8,128)(2,1)S(1)} %bitcast.88, f32[12,256,512]{2,1,0:T(8,128)} %get-tuple-element.57, f32[12,256]{1,0:T(8,128)S(1)} %get-tuple-element.56), kind=kOutput, calls=%fused_computation.40 | convolution fusion | flops 204668928 | bytes 7483392 | tf_op jit(solution)/shard_map/hqk,khe->qhe/dot_general | solution.py:613
  85.3 2.0 %multiply_reduce_fusion = (f32[12,256]{1,0:T(8,128)S(1)}, f32[12,256,512]{2,1,0:T(8,128)S(1)}) fusion(f32[12,256,512]{2,1,0:T(8,128)S(1)} %copy-done.7, f32[12,256]{1,0:T(8,128)S(1)} %get-tuple-element.56, bf16[256,12,64]{0,2,1:T(8,128)(2,1)S(1)} %bitcast.90, bf16[512,12,64]{0,2,1:T(8,128)(2,1)S(1)} %bitcast.89), kind=kOutput, calls=%fused_computation.2 | convolution fusion | flops 206042112 | bytes 13787136 | tf_op jit(solution)/shard_map/qhe,khe->hqk/dot_general | solution.py:629
  87.3 1.1 multiply_convert_fusion
  88.4 1.8 %fusion.20 = bf16[12,64,256]{2,1,0:T(8,128)(2,1)} fusion(bf16[512,12,64]{0,2,1:T(8,128)(2,1)S(1)} %bitcast.75, bf16[12,256,512]{2,1,0:T(8,128)(2,1)S(1)} %multiply_convert_fusion), kind=kOutput, calls=%fused_computation.38 | convolution fusion | flops 201719808 | bytes 4325376 | tf_op jit(solution)/shard_map/hqk,khe->qhe/dot_general | solution.py:635
  90.9 1.9 %fusion.15 = f32[12,64,512]{2,1,0:T(8,128)} fusion(bf16[256,12,64]{0,2,1:T(8,128)(2,1)S(1)} %bitcast.91, f32[12,256,512]{2,1,0:T(8,128)S(1)} %copy-done.7, f32[12,256]{1,0:T(8,128)S(1)} %get-tuple-element.56), kind=kOutput, calls=%fused_computation.30 | convolution fusion | flops 204472320 | bytes 8269824 | tf_op jit(solution)/shard_map/hqk,qhe->khe/dot_general | solution.py:626
  93.3 1.9 %copy.34 = f32[512,768]{1,0:T(8,128)S(1)} copy(f32[512,768]{0,1:T(8,128)} %bitcast.79) | data formatting | bytes 3145728 | tf_op jit(solution)/shard_map/reshape | solution.py:650
  96.3 2.0 %collective-permute-start.2 = (bf16[128,1536]{1,0:T(8,128)(2,1)}, bf16[128,1536]{1,0:T(8,128)(2,1)}, u32[]{:S(2)}, u32[]{:S(2)}) collective-permute-start(bf16[128,1536]{1,0:T(8,128)(2,1)} %get-tuple-element.49), channel_id=1, source_target_pairs={{0,1},{1,2},{2,3},{3,4},{4,5},{5,6},{6,7},{7,8},{8,9},{9,10},{10,1... | collective-permute-start | bytes 1179656 | tf_op jit(solution)/shard_map/ppermute | solution.py:574
  98.3 1.3 fusion.14
  100.6 3.4 %collective-permute-start.3 = (bf16[128,1536]{1,0:T(8,128)(2,1)}, bf16[128,1536]{1,0:T(8,128)(2,1)S(1)}, u32[]{:S(2)}, u32[]{:S(2)}) collective-permute-start(bf16[128,1536]{1,0:T(8,128)(2,1)} %get-tuple-element.48), channel_id=1, source_target_pairs={{1,0},{2,1},{3,2},{4,3},{5,4},{6,5},{7,6},{8,7},{9,8},{10,9},{11,1... | collective-permute-start | bytes 1179656 | tf_op jit(solution)/shard_map/ppermute | solution.py:574
  104.0 1.9 %copy.36.context = bf16[256,768]{1,0:T(8,128)(2,1)} copy(bf16[256,768]{0,1:T(8,128)(2,1)} %bitcast.92) | data formatting | bytes 786432 | tf_op jit(solution)/shard_map/convert_element_type | solution.py:617
  105.9 3.8 %fusion.8 = bf16[1,256,1536]{2,1,0:T(8,128)(2,1)} fusion(bf16[256,768]{0,1:T(8,128)(2,1)} %bitcast.93, bf16[768,768]{1,0:T(8,128)(2,1)} %bitcast.86, bf16[768,768]{1,0:T(8,128)(2,1)} %bitcast.84, pred[256]{0:T(512)(128)(4,1)S(1)} %copy-done.20, bf16[1,256,1536]{2,1,0:T(8,128)(2,1)} %param.14), kind=kOutput, calls=%fused_computation.19 | convolution fusion | flops 610271232 | bytes 4325632 | tf_op jit(solution)/shard_map/dot_general | solution.py:683
  109.7 1.1 fusion.28
  112.0 53.6 %reduce_grads.1 = (f32[12,768]{1,0:T(8,128)}, f32[12,768]{1,0:T(8,128)}, f32[12,768]{1,0:T(8,128)}, f32[6,1536]{1,0:T(8,128)}, f32[16,128]{1,0:T(8,128)}, /*index=5*/bf16[256,1536]{1,0:T(8,128)(2,1)}) custom-call(bf16[256,1536]{1,0:T(8,128)(2,1)} %fusion.13.normed, bf16[256,768]{1,0:T(8,128)(2,1)} %copy.35.gq, bf16[256,768]{1,0:T(8,128)(2,1)} %get-tuple-element.53.gk, ...), custom_call_target="tpu_custom_call" | custom-call | tf_op jit(solution)/shard_map/reduce_grads/pallas_call | solution.py:542
  165.6 1.3 dynamic_slice.3
  166.8 2.1 %copy.45 = bf16[1,256,1536]{2,1,0:T(8,128)(2,1)} copy(bf16[1,256,1536]{2,1,0:T(8,128)(2,1)} %bitcast.87) | data formatting | bytes 1572864
  168.9 1.4 copy.46
  170.3 1.4 copy.47
  171.8 1.4 copy.48
  173.2 1.4 copy.49
  (72 shorter events, 14.2 us)
Async XLA Ops:
  0.6 1.0 copy-start.1
  1.6 1.0 copy-start.2
  2.6 1.0 copy-start.3
  3.5 1.0 copy-start.4
  48.3 11.0 %copy-start = (bf16[2,4,2,3,2,4,16,768]{7,6,5,4,3,2,1,0:T(8,128)(2,1)}, bf16[2,4,2,3,2,4,16,768]{7,6,5,4,3,2,1,0:T(8,128)(2,1)S(1)}, u32[]{:S(2)}) copy-start(bf16[2,4,2,3,2,4,16,768]{7,6,5,4,3,2,1,0:T(8,128)(2,1)S(1)} %gather_weights.1) | copy-start | bytes 28311556
  48.3 2.0 %copy-start.5 = (bf16[1,256,1536]{2,1,0:T(8,128)(2,1)S(1)}, bf16[1,256,1536]{2,1,0:T(8,128)(2,1)}, u32[]{:S(2)}) copy-start(bf16[1,256,1536]{2,1,0:T(8,128)(2,1)} %param.14) | copy-start | bytes 2359300
  48.3 2.5 %copy-start.13 = (f32[1536]{0:T(1024)S(1)}, f32[1536]{0:T(1024)}, u32[]{:S(2)}) copy-start(f32[1536]{0:T(1024)} %param.16) | copy-start | bytes 18436
  50.8 12.4 %copy-start.14 = (f32[256]{0:T(256)}, f32[256]{0:T(256)S(1)}, u32[]{:S(2)}) copy-start(f32[256]{0:T(256)S(1)} %add_rsqrt_fusion) | copy-start | bytes 3076
  53.6 20.8 %collective-permute-start.1 = (bf16[128,1536]{1,0:T(8,128)(2,1)}, bf16[128,1536]{1,0:T(8,128)(2,1)S(1)}, u32[]{:S(2)}, u32[]{:S(2)}) collective-permute-start(bf16[128,1536]{1,0:T(8,128)(2,1)} %get-tuple-element.55), channel_id=1, source_target_pairs={{1,0},{2,1},{3,2},{4,3},{5,4},{6,5},{7,6},{8,7},{9,8},{10,9},{11,1... | collective-permute-start | bytes 1179656 | tf_op jit(solution)/shard_map/ppermute | solution.py:566
  55.5 18.9 %collective-permute-start = (bf16[128,1536]{1,0:T(8,128)(2,1)}, bf16[128,1536]{1,0:T(8,128)(2,1)S(1)}, u32[]{:S(2)}, u32[]{:S(2)}) collective-permute-start(bf16[128,1536]{1,0:T(8,128)(2,1)} %get-tuple-element.54), channel_id=1, source_target_pairs={{0,1},{1,2},{2,3},{3,4},{4,5},{5,6},{6,7},{7,8},{8,9},{9,10},{10,1... | collective-permute-start | bytes 1179656 | tf_op jit(solution)/shard_map/ppermute | solution.py:565
  63.2 4.5 %copy-start.8 = (bf16[1,256,1536]{2,1,0:T(8,128)(2,1)S(1)}, bf16[1,256,1536]{2,1,0:T(8,128)(2,1)}, u32[]{:S(2)}) copy-start(bf16[1,256,1536]{2,1,0:T(8,128)(2,1)} %param.15) | copy-start | bytes 2359300
  67.7 0.5 copy-start.19
  67.9 0.9 copy-start.9
  68.8 3.5 %copy-start.16 = (s32[1,256]{1,0:T(1,128)S(1)}, s32[1,256]{1,0:T(1,128)}, u32[]{:S(2)}) copy-start(s32[1,256]{1,0:T(1,128)} %param.23) | copy-start | bytes 3076
  68.8 3.5 %copy-start.17 = (s32[1,256]{1,0:T(1,128)S(1)}, s32[1,256]{1,0:T(1,128)}, u32[]{:S(2)}) copy-start(s32[1,256]{1,0:T(1,128)} %param.22) | copy-start | bytes 3076
  68.8 3.5 %copy-start.18 = (s32[256]{0:T(256)S(1)}, s32[256]{0:T(256)}, u32[]{:S(2)}) copy-start(s32[256]{0:T(256)} %iota_add_fusion.1) | copy-start | bytes 3076
  68.8 3.5 %copy-start.21 = (pred[512]{0:T(512)(128)(4,1)S(1)}, pred[512]{0:T(512)(128)(4,1)}, u32[]{:S(2)}) copy-start(pred[512]{0:T(512)(128)(4,1)} %broadcast_compare_fusion) | copy-start | bytes 1540
  68.8 4.4 %copy-start.15 = (f32[256]{0:T(256)S(1)}, f32[256]{0:T(256)}, u32[]{:S(2)}) copy-start(f32[256]{0:T(256)} %copy-done.14) | copy-start | bytes 3076
  74.6 0.9 copy-start.12
  80.4 4.9 %copy-start.7 = (f32[12,256,512]{2,1,0:T(8,128)S(1)}, f32[12,256,512]{2,1,0:T(8,128)}, u32[]{:S(2)}) copy-start(f32[12,256,512]{2,1,0:T(8,128)} %get-tuple-element.57) | copy-start | bytes 18874372
  80.4 4.9 %copy-start.11 = (bf16[256,768]{0,1:T(8,128)(2,1)S(1)}, bf16[256,768]{0,1:T(8,128)(2,1)}, u32[]{:S(2)}) copy-start(bf16[256,768]{0,1:T(8,128)(2,1)} %copy.32) | copy-start | bytes 1179652
  96.3 3.4 %copy-start.10 = (bf16[12,64,256]{2,1,0:T(8,128)(2,1)S(1)}, bf16[12,64,256]{2,1,0:T(8,128)(2,1)}, u32[]{:S(2)}) copy-start(bf16[12,64,256]{2,1,0:T(8,128)(2,1)} %fusion.20) | copy-start | bytes 1179652
  96.3 9.6 %copy-start.20 = (pred[256]{0:T(512)(128)(4,1)S(1)}, pred[256]{0:T(512)(128)(4,1)}, u32[]{:S(2)}) copy-start(pred[256]{0:T(512)(128)(4,1)} %copy-done.19) | copy-start | bytes 772
  96.3 13.4 %collective-permute-start.2 = (bf16[128,1536]{1,0:T(8,128)(2,1)}, bf16[128,1536]{1,0:T(8,128)(2,1)}, u32[]{:S(2)}, u32[]{:S(2)}) collective-permute-start(bf16[128,1536]{1,0:T(8,128)(2,1)} %get-tuple-element.49), channel_id=1, source_target_pairs={{0,1},{1,2},{2,3},{3,4},{4,5},{5,6},{6,7},{7,8},{8,9},{9,10},{10,1... | collective-permute-start | bytes 1179656 | tf_op jit(solution)/shard_map/ppermute | solution.py:574
  100.6 10.2 %collective-permute-start.3 = (bf16[128,1536]{1,0:T(8,128)(2,1)}, bf16[128,1536]{1,0:T(8,128)(2,1)S(1)}, u32[]{:S(2)}, u32[]{:S(2)}) collective-permute-start(bf16[128,1536]{1,0:T(8,128)(2,1)} %get-tuple-element.48), channel_id=1, source_target_pairs={{1,0},{2,1},{3,2},{4,3},{5,4},{6,5},{7,6},{8,7},{9,8},{10,9},{11,1... | collective-permute-start | bytes 1179656 | tf_op jit(solution)/shard_map/ppermute | solution.py:574
  105.9 3.8 %copy-start.6 = (f32[256,1536]{1,0:T(8,128)S(1)}, f32[256,1536]{1,0:T(8,128)}, u32[]{:S(2)}) copy-start(f32[256,1536]{1,0:T(8,128)} %fusion.14) | copy-start | bytes 4718596

commit v3 on v2

--- a/solution.py
+++ b/solution.py
@@ -33,6 +33,9 @@
             core = 1 - core
         return ((y // 2) * 4 + z, (lax.rem(y, 2) * 4 + x) * 2 + core)
 
+    def along(self, by):
+        return (lax.axis_index("dp"), lax.rem(lax.axis_index("tm") + by, 16))
+
     def right(self, axis):
         return lax.rem(self.at(axis) + 1, 4)
 
@@ -43,13 +46,16 @@
         return lax.rem(self.at(axis) + 2, 4)
 
 
-def greet(me, far=False):
+def greet(me, far=False, ring=False):
     barrier = pltpu.get_barrier_semaphore()
     for axis in "xyz":
         for j in (me.left(axis), me.right(axis)) + ((me.over(axis),) if far else ()):
             pl.semaphore_signal(barrier, inc=1, device_id=me.device(axis, j), device_id_type=MESH)
     pl.semaphore_signal(barrier, inc=1, device_id=me.device(), device_id_type=MESH)
-    pl.semaphore_wait(barrier, 10 if far else 7)
+    if ring:
+        for by in (1, 15):
+            pl.semaphore_signal(barrier, inc=1, device_id=me.along(by), device_id_type=MESH)
+    pl.semaphore_wait(barrier, 7 + 3 * far + 2 * ring)
 
 
 def gather_regions(me, w, h):
@@ -149,14 +155,14 @@
 GATHER_SEMS = 84
 
 
-def run_gather(me, shards, held, w, send, recv, local):
+def start_gather(me, shards, held, w, send, recv, local):
     wq, wk, wv, wo = shards
     loads = [pltpu.make_async_copy(part, held.at[pl.ds(12 * n, 12)], local.at[n]) for n, part in enumerate((wq, wk, wv))]
     for n in range(2):
         loads.append(pltpu.make_async_copy(wo.at[:, :, pl.ds(768 * n, 768)], held.at[pl.ds(36 + 6 * n, 6)], local.at[3 + n]))
     for copy in loads:
         copy.start()
-    greet(me)
+    greet(me, ring=True)
     for copy in loads:
         copy.wait()
     own = []
@@ -169,10 +175,14 @@
         copy.start()
     for copy in own:
         copy.wait()
-    a, b, c = gather_stages(me, w, send, recv)
-    c[0].start()
-    a[0].start()
-    b[0].start()
+    rows = gather_stages(me, w, send, recv)
+    for row in (rows[2], rows[0], rows[1]):
+        row[0].start()
+    return rows
+
+
+def finish_gather(rows, under):
+    a, b, c = rows
     c[0].relay()
     c[0].finish()
     c[1].start()
@@ -185,39 +195,207 @@
     c[1].relay()
     c[1].finish()
     c[2].start()
+    under()
     a[1].relay()
     b[1].relay()
     c[2].relay()
     a[1].finish()
     b[1].finish()
     c[2].finish()
-    for row in (a, b, c):
+    for row in rows:
         for stage in row:
             stage.arrive()
-    for row in (a, b, c):
+
+
+def weight_rows(w, s, n):
+    parts = []
+    for k in range(3 * n, 3 * n + 3):
+        parts.append(w[s // 4, s % 4, k // 6, k % 6 // 2, k % 2].reshape(64, 768))
+    return jnp.concatenate(parts, 0)
+
+
+def pair_rows(w, i, n):
+    return jnp.concatenate([weight_rows(w, 2 * i, n), weight_rows(w, 2 * i + 1, n)], 0)
+
+
+def out_rows(w, yh, b):
+    parts = []
+    for z in range(4):
+        parts.append(w[yh, z, 1, 2, b].reshape(64, 768) if b else w[yh, z, 1, 1, 1].reshape(64, 768))
+        middle = w[yh, z, 1, 2, 0, 2 * b:2 * b + 2].reshape(32, 768)
+        parts.insert(len(parts) - 1 if b else len(parts), middle)
+    return jnp.concatenate(parts, 0)
+
+
+def norm(frames):
+    xf = frames.astype(F32)
+    mean = jnp.mean(xf, -1, keepdims=True)
+    centered = xf - mean
+    var = jnp.mean(centered * centered, -1, keepdims=True)
+    inverse = lax.rsqrt(var + 1e-05)
+    return centered * inverse, inverse
+
+
+ROWS, COLS = (((1,), (1,)), ((), ())), (((1,), (0,)), ((), ()))
+
+
+def dot(a, b, dims=COLS):
+    return lax.dot_general(a, b, dims, preferred_element_type=F32)
+
+
+def forward_kernel(
+    wq, wk, wv, wo, frames, cotangent, gain, lengths, lo, hi,
+    w_out, nt, ct, ctx, gq, gk, gv, masked,
+    held, w, nm, q6, gc6, kv, center, bias, rim_s, rim_r, send, recv, local, ring_send, ring_recv
+):
+    me = Place()
+    length = lengths[0]
+    base = lax.axis_index("tm") * 256
+    rows = start_gather(me, (wq, wk, wv, wo), held, w, send, recv, local)
+
+    @pl.loop(0, 8)
+    def _(n):
+        at = pl.ds(pl.multiple_of(n * 32, 32), 32)
+        xhat, _ = norm(frames[at])
+        nm[at] = (xhat * gain[...]).astype(BF)
+
+    def under():
+        nt[...] = nm[...].T
+
+        @pl.loop(0, 8)
+        def _(n):
+            at = pl.ds(pl.multiple_of(n * 32, 32), 32)
+            frame = base + n * 32 + lax.broadcasted_iota(jnp.int32, (32, 1536), 0)
+            masked[at] = jnp.where(frame < length, cotangent[at].astype(F32), 0.0).astype(BF)
+
+        for b in range(2):
+            kp = base + 128 * (b - 1) + lax.broadcasted_iota(jnp.int32, (384, 128), 0)
+            qp = base + 128 * b + lax.broadcasted_iota(jnp.int32, (384, 128), 1)
+            cols = pl.ds(128 * b, 128)
+            seen = (kp >= lo[:, cols]) & (kp < hi[:, cols]) & (kp < length)
+            bias[b] = jnp.where(seen | (kp == qp), 0.0, -1e30)
+
+    finish_gather(rows, under)
+    spread = pltpu.make_async_copy(w, w_out, local.at[6])
+    spread.start()
+
+    def project(n):
+        total = None
+        for i in range(4):
+            term = dot(nm[:, 384 * i:384 * i + 384], pair_rows(w, i, n))
+            total = term if total is None else total + term
+        return total.astype(BF)
+
+    def halo(p, right):
+        src, dst, by = (256, 0, 1) if right else (128, 384, 15)
+        n = 2 * p + right
+        return pltpu.make_async_remote_copy(
+            src_ref=kv.at[p, :, pl.ds(src, 128)], dst_ref=kv.at[p, :, pl.ds(dst, 128)],
+            send_sem=ring_send.at[n], recv_sem=ring_recv.at[n], device_id=me.along(by), device_id_type=MESH)
+
+    def rim(p, right):
+        n = 12 + 2 * p + right
+        return pltpu.make_async_remote_copy(
+            src_ref=rim_s.at[p, right], dst_ref=rim_r.at[p, right],
+            send_sem=ring_send.at[n], recv_sem=ring_recv.at[n], device_id=me.along(1 if right else 15), device_id_type=MESH)
+
+    for m in range(2):
+        k = project(1 + m)
+        for p in range(6):
+            kv[p, m, 128:384] = k[:, 128 * p:128 * p + 128]
+    for p in range(6):
+        for right in range(2):
+            halo(p, right).start()
+    q = project(0)
+    for p in range(6):
+        q6[p] = q[:, 128 * p:128 * p + 128]
+    for yh in range(2):
+        g = (dot(masked[:, :768], out_rows(w, yh, 0), ROWS) + dot(masked[:, 768:], out_rows(w, yh, 1), ROWS)).astype(BF)
+        for n in range(3):
+            gc6[3 * yh + n] = g[:, 128 * n:128 * n + 128]
+
+    @pl.loop(0, 6)
+    def _(p):
+        for right in range(2):
+            halo(p, right).wait_recv()
+        first = (lax.broadcasted_iota(jnp.int32, (128, 128), 1) < 64).astype(F32)
+        even, odd = first.astype(BF), (1.0 - first).astype(BF)
+        lanes = pl.ds(pl.multiple_of(128 * p, 128), 128)
+        grads = []
+        for b in range(2):
+            at = pl.ds(128 * b, 128)
+            q = q6[p, at]
+            g = gc6[p, at]
+            qm = jnp.concatenate([q * even, q * odd], 0)
+            gm = jnp.concatenate([g * even, g * odd], 0)
+            key = kv[p, 0, pl.ds(128 * b, 384)]
+            value = kv[p, 1, pl.ds(128 * b, 384)]
+            s = dot(key, qm, ROWS) * 0.125 + jnp.concatenate([bias[b], bias[b]], 1)
+            e = jnp.exp(s - jnp.max(s, 0, keepdims=True))
+            probs = e * (1.0 / jnp.sum(e, 0, keepdims=True))
+            low = probs.astype(BF)
+            grad = dot(value, gm, ROWS)
+            delta = jnp.sum(probs * grad, 0, keepdims=True)
+            ds = (probs * (grad - delta)).astype(BF)
+            c = dot(value.T, low)
+            c = jnp.concatenate([c[:64, :128], c[64:, 128:]], 0)
+            ct[lanes, at] = c.astype(BF)
+            ctx[at, lanes] = c.T.astype(BF)
+            d = dot(key.T, ds)
+            d = jnp.concatenate([d[:64, :128], d[64:, 128:]], 0) * 0.125
+            gq[at, lanes] = d.T.astype(BF)
+            grads.append((dot(ds, qm) * 0.125, dot(low, gm)))
+        for m in range(2):
+            here, there = grads[0][m], grads[1][m]
+            rim_s[p, 0, m] = here[:128].astype(BF)
+            rim_s[p, 1, m] = there[256:].astype(BF)
+            center[p, m] = here[128:] + there[:256]
+        for right in range(2):
+            rim(p, right).start()
+
+    for p in range(6):
+        for right in range(2):
+            rim(p, right).wait_recv()
+        for m, out in enumerate((gk, gv)):
+            lanes = pl.ds(128 * p, 128)
+            out[:128, lanes] = (center[p, m, :128] + rim_r[p, 1, m].astype(F32)).astype(BF)
+            out[128:, lanes] = (center[p, m, 128:] + rim_r[p, 0, m].astype(F32)).astype(BF)
+    for p in range(6):
+        for right in range(2):
+            halo(p, right).wait_send()
+            rim(p, right).wait_send()
+    for row in rows:
         for stage in row:
             stage.drain()
-
-
-def gather_kernel(wq, wk, wv, wo, w, held, send, recv, local):
-    run_gather(Place(), (wq, wk, wv, wo), held, w, send, recv, local)
-
-
-def gather_weights(wq, wk, wv, wo):
+    spread.wait()
+
+
+def forward(wq, wk, wv, wo, frames, cotangent, gain, lengths, lo, hi):
+    vm, hbm = pl.BlockSpec(memory_space=pltpu.VMEM), pl.BlockSpec(memory_space=pltpu.HBM)
+    sds, sem = jax.ShapeDtypeStruct, pltpu.SemaphoreType.DMA
     return pl.pallas_call(
-        gather_kernel,
-        out_shape=jax.ShapeDtypeStruct((2, 4, 2, 3, 2, 4, 16, 768), BF),
-        in_specs=[pl.BlockSpec(memory_space=pl.ANY)] * 4,
-        out_specs=pl.BlockSpec(memory_space=pltpu.VMEM),
+        forward_kernel,
+        out_shape=(
+            sds((2, 4, 2, 3, 2, 4, 16, 768), BF), sds((1536, 256), BF), sds((768, 256), BF),
+            sds((256, 768), BF), sds((256, 768), BF), sds((256, 768), BF), sds((256, 768), BF), sds((256, 1536), BF),
+        ),
+        in_specs=[hbm] * 4 + [vm] * 3 + [pl.BlockSpec(memory_space=pltpu.SMEM)] + [vm] * 2,
+        out_specs=(hbm,) + (vm,) * 7,
         scratch_shapes=[
             pltpu.VMEM((48, 16, 768), BF),
-            pltpu.SemaphoreType.DMA((GATHER_SEMS,)),
-            pltpu.SemaphoreType.DMA((GATHER_SEMS,)),
-            pltpu.SemaphoreType.DMA((6,)),
+            pltpu.VMEM((2, 4, 2, 3, 2, 4, 16, 768), BF),
+            pltpu.VMEM((256, 1536), BF),
+            pltpu.VMEM((6, 256, 128), BF), pltpu.VMEM((6, 256, 128), BF),
+            pltpu.VMEM((6, 2, 512, 128), BF),
+            pltpu.VMEM((6, 2, 256, 128), F32),
+            pltpu.VMEM((2, 384, 128), F32),
+            pltpu.VMEM((6, 2, 2, 128, 128), BF), pltpu.VMEM((6, 2, 2, 128, 128), BF),
+            sem((GATHER_SEMS,)), sem((GATHER_SEMS,)), sem((7,)), sem((24,)), sem((24,)),
         ],
-        compiler_params=pltpu.CompilerParams(collective_id=0, has_side_effects=True, vmem_limit_bytes=40 << 20),
-        name="gather_weights",
-    )(wq.reshape(12, 16, 768), wk.reshape(12, 16, 768), wv.reshape(12, 16, 768), wo.reshape(6, 16, 1536))
+        compiler_params=pltpu.CompilerParams(collective_id=0, has_side_effects=True, vmem_limit_bytes=48 << 20),
+        name="forward",
+    )(wq.reshape(12, 16, 768), wk.reshape(12, 16, 768), wv.reshape(12, 16, 768), wo.reshape(6, 16, 1536),
+      frames, cotangent, gain, lengths, lo, hi)
 
 
 ORDERS = (("x", "y", "z"), ("y", "z", "x"), ("z", "x", "y"))
@@ -337,9 +515,9 @@
         sem((54,)), sem((54,)), sem((3,)), sem((3,)), sem((11,)), sem((11,)),
         pltpu.VMEM((3, 4, 4, 4, 96, 128), BF),
         pltpu.VMEM((3, 4, 4, 4, 96, 128), F32),
-        pltpu.VMEM((1536, 256), BF), pltpu.VMEM((768, 256), BF),
         pltpu.VMEM((1536, 384), F32), pltpu.VMEM((768, 256), F32),
-        pltpu.VMEM((256, 1536), F32), pltpu.VMEM((256, 1536), F32),
+        pltpu.VMEM((256, 1536), F32),
+        pltpu.VMEM((2, 4, 2, 3, 2, 4, 16, 768), BF), sem,
     ]
 
 
@@ -400,8 +578,8 @@
 
 
 def weight_terms(refs, scratch, h, c, put):
-    gq, gk, gv, masked = refs
-    nt, ct, prod, prod_o = scratch[20:24]
+    nt, ct, gq, gk, gv, masked = refs
+    prod, prod_o = scratch[20:22]
     columns = pl.ds(pl.multiple_of(h * 384 + c * 128, 128), 128)
     rhs = jnp.concatenate([gq[:, columns], gk[:, columns], gv[:, columns]], 1)
     prod[...] = jnp.dot(nt[...], rhs, preferred_element_type=F32)
@@ -425,54 +603,53 @@
             put((yh * 2 + yl, z, xh * 2 + odd), jnp.concatenate(parts, 0))
 
 
-def norm(frames):
-    xf = frames.astype(F32)
-    mean = jnp.mean(xf, -1, keepdims=True)
-    centered = xf - mean
-    var = jnp.mean(centered * centered, -1, keepdims=True)
-    inverse = lax.rsqrt(var + 1e-05)
-    return centered * inverse, inverse
-
-
 def grad_normed(w, gq, gk, gv, out):
     for s in range(4):
         total = None
         for n, g in enumerate((gq, gk, gv)):
-            rows = w[2 * s: 2 * s + 2, 12 * n: 12 * n + 12].reshape(384, 768)
-            term = lax.dot_general(g[...], rows, (((1,), (1,)), ((), ())), preferred_element_type=F32)
+            term = dot(g[...], pair_rows(w, s, n), ROWS)
             total = term if total is None else total + term
         out[:, 384 * s: 384 * s + 384] = total
 
 
-def norm_backward(frames, cotangent, gain, gn, gx, grad_frames, gain_total):
+def norm_backward(frames, cotangent, gain, gn, grad_frames, gain_total):
+    gain_total[0] = jnp.zeros((16, 128), F32)
+
     @pl.loop(0, 8)
     def _(n):
         rows = pl.ds(pl.multiple_of(n * 32, 32), 32)
         xhat, inverse = norm(frames[rows])
         grad = gn[rows]
-        gx[rows] = grad * xhat
+        gx = grad * xhat
+        for b in range(12):
+            gain_total[0, b:b + 1] += jnp.sum(gx[:, 128 * b: 128 * b + 128], 0, keepdims=True)
         g = grad * gain[...]
         first = jnp.mean(g, -1, keepdims=True)
-        second = jnp.mean(g * xhat, -1, keepdims=True)
+        second = jnp.mean(gx * gain[...], -1, keepdims=True)
         back = inverse * (g - first - xhat * second)
         grad_frames[rows] = (cotangent[rows].astype(F32) + back).astype(BF)
 
-    gain_total[0] = jnp.zeros((16, 128), F32)
-    for b in range(12):
-        gain_total[0, b:b + 1] = jnp.sum(gx[:, 128 * b: 128 * b + 128], 0, keepdims=True)
+
+def project_out(w, ctx, frames, length, out):
+    base = lax.axis_index("tm") * 256
+    for b in range(2):
+        attn = dot(ctx[:, :384], out_rows(w, 0, b)) + dot(ctx[:, 384:], out_rows(w, 1, b))
+        lanes = pl.ds(768 * b, 768)
+        frame = base + lax.broadcasted_iota(jnp.int32, (256, 768), 0)
+        out[:, lanes] = (frames[:, lanes].astype(F32) + jnp.where(frame < length, attn, 0.0)).astype(BF)
 
 
 def reduce_kernel(
-    normed, gq, gk, gv, context, masked, w, frames, cotangent, gain,
-    out_q, out_k, out_v, out_o, gain_out, grad_frames, *scratch
+    nt, gq, gk, gv, ct, ctx, masked, w_hbm, frames, cotangent, gain, lengths,
+    total, gain_out, grad_frames, frames_out, *scratch
 ):
     me = Place()
     r0, fin, gt, gg, gsend, grecv = scratch[0], scratch[9], scratch[10], scratch[11], scratch[16], scratch[17]
-    for_other, half, nt, ct = scratch[18:22]
-    gn, gx = scratch[24:26]
-    nt[...] = normed[...].T
-    ct[...] = context[...].T
-    refs = (gq, gk, gv, masked)
+    for_other, half = scratch[18:20]
+    gn, w = scratch[22:24]
+    load = pltpu.make_async_copy(w_hbm, w, scratch[24])
+    load.start()
+    refs = (nt, ct, gq, gk, gv, masked)
     greet(me, far=True)
     for c in range(3):
         def put(at, v, c=c):
@@ -488,11 +665,13 @@
             half[(c,) + at] = v + r0[(c,) + at].astype(F32)
         weight_terms(refs, scratch, me.core, c, put)
         stages[c][0].start()
+    load.wait()
     grad_normed(w, gq, gk, gv, gn)
     for c in range(3):
         stages[c][0].relay()
-    norm_backward(frames, cotangent, gain, gn, gx, grad_frames, gt)
+    norm_backward(frames, cotangent, gain, gn, grad_frames, gt)
     sum_gain.start(0)
+    project_out(w, ctx, frames, lengths[0], frames_out)
     for n in range(3):
         for c in range(3):
             stages[c][n].finish()
@@ -519,12 +698,33 @@
     sum_gain.drain()
     last(me.core).wait_send()
     last(1 - me.core).wait_recv()
+    total[...] = fin[...]
+
+
+def reduce_grads(*args):
+    vm, hbm = pl.BlockSpec(memory_space=pltpu.VMEM), pl.BlockSpec(memory_space=pltpu.HBM)
+    sds = jax.ShapeDtypeStruct
+    return pl.pallas_call(
+        reduce_kernel,
+        out_shape=(sds((2, 3, 96, 128), F32), sds((16, 128), F32), sds((256, 1536), BF), sds((256, 1536), BF)),
+        in_specs=[vm] * 7 + [hbm] + [vm] * 3 + [pl.BlockSpec(memory_space=pltpu.SMEM)],
+        out_specs=(vm,) * 4,
+        scratch_shapes=reduce_scratch(),
+        compiler_params=pltpu.CompilerParams(collective_id=1, has_side_effects=True, vmem_limit_bytes=62 << 20),
+        name="reduce_grads",
+    )(*args)
+
+
+def outputs_kernel(total, gain, grad_in, frames_in, out_q, out_k, out_v, out_o, out_gain, grad_frames, frames_out):
+    me = Place()
+    frames_out[...] = frames_in[...]
+    grad_frames[...] = grad_in[...]
     odd = lax.rem(me.x, 2)
     for h in range(2):
         for c in range(3):
             lanes = pl.ds(384 * h + 128 * c, 128)
             for n, out in enumerate((out_q, out_k, out_v)):
-                t = fin[h, c, pl.ds(24 * n, 24)]
+                t = total[h, c, pl.ds(24 * n, 24)]
                 out[:, lanes] = jnp.where(me.core == 0, t[:12], t[12:])
             for b in range(2):
                 lanes = pl.ds(768 * h + 256 * c + 128 * b, 128)
@@ -533,183 +733,36 @@
                     odd0, odd1 = 16 + 4 * b + r if r < 4 else 8 * b + r - 4, 8 * b + 2 + r
                     row = 72 + jnp.where(
                         odd == 0, jnp.where(me.core == 0, even0, even1), jnp.where(me.core == 0, odd0, odd1))
-                    out_o[r:r + 1, lanes] = fin[h, c, pl.ds(row, 1)]
-
-
-def reduce_grads(*args):
+                    out_o[r:r + 1, lanes] = total[h, c, pl.ds(row, 1)]
+    at = (lax.axis_index("dp") * 16 + lax.axis_index("tm")) * 12
+    row, lane = at // 128, lax.rem(at, 128)
+    both = jnp.concatenate([gain[pl.ds(row, 1)], gain[pl.ds(row + 1, 1)]], 1)
+    both = jnp.broadcast_to(both, (8, 256))
+    out_gain[...] = pltpu.roll(both, lax.rem(256 - lane, 256), 1)[:1, :12]
+
+
+def write_outputs(*args):
     vm = pl.BlockSpec(memory_space=pltpu.VMEM)
     sds = jax.ShapeDtypeStruct
     return pl.pallas_call(
-        reduce_kernel,
-        out_shape=(sds((12, 768), F32),) * 3 + (sds((6, 1536), F32), sds((16, 128), F32), sds((256, 1536), BF)),
-        in_specs=[vm] * 10,
-        out_specs=(vm,) * 6,
-        scratch_shapes=reduce_scratch(),
-        compiler_params=pltpu.CompilerParams(collective_id=1, has_side_effects=True, vmem_limit_bytes=62 << 20),
-        name="reduce_grads",
+        outputs_kernel,
+        out_shape=(sds((12, 768), F32),) * 3 + (
+            sds((6, 1536), F32), sds((1, 12), F32), sds((256, 1536), BF), sds((256, 1536), BF)),
+        in_specs=[vm] * 4,
+        out_specs=(vm,) * 7,
+        name="write_outputs",
     )(*args)
-
-
-HEADS = 12
-HEAD_DIM = 64
-REACH = 128
-
-
-def extended_2(value, sides, width):
-    for axis, dim in sides:
-        devices, length = (lax.axis_size(axis), value.shape[dim])
-        up = [(i, (i + 1) % devices) for i in range(devices - 1)]
-        down = [(j, i) for i, j in up]
-        last = lax.slice_in_dim(value, length - width, length, axis=dim)
-        first = lax.slice_in_dim(value, 0, width, axis=dim)
-        before = lax.ppermute(last, axis, up)
-        after = lax.ppermute(first, axis, down)
-        value = jnp.concatenate([before, value, after], axis=dim)
-    return value
-
-
-def shifted(value, axis, by):
-    devices = lax.axis_size(axis)
-    pairs = [(i, i + by) for i in range(devices) if 0 <= i + by < devices]
-    return lax.ppermute(value, axis, pairs)
-
-
-def layer_normalize(input_rows, norm_gain):
-    xf = input_rows.astype(jnp.float32)
-    feature_mean = jnp.mean(xf, -1, keepdims=True)
-    centered_input = xf - feature_mean
-    var = jnp.mean(centered_input * centered_input, -1, keepdims=True)
-    inverse_deviation = lax.rsqrt(var + 1e-05)
-    standardized_input = centered_input * inverse_deviation
-    return (
-        (standardized_input * norm_gain).astype(jnp.bfloat16),
-        standardized_input,
-        inverse_deviation,
-    )
-
-
-def window_mask(lo, hi, length, qpos, kpos):
-    kp = kpos[None, :]
-    inside = (kp >= lo[:, None]) & (kp < hi[:, None]) & (kp < length)
-    return inside | (kp == qpos[:, None])
-
-
-def split_heads(a):
-    return a.reshape(a.shape[0], HEADS, HEAD_DIM)
-
-
-def attend(query, key, value, mask):
-    scale = HEAD_DIM ** (-0.5)
-    scores = (
-        jnp.einsum(
-            "qhe,khe->hqk", split_heads(query), split_heads(key), preferred_element_type=jnp.float32
-        )
-        * scale
-    )
-    scores = jnp.where(mask[None], scores, -1e30)
-    expo = jnp.exp(scores - jnp.max(scores, -1, keepdims=True))
-    probs = expo / jnp.sum(expo, -1, keepdims=True)
-    probs_low = probs.astype(jnp.bfloat16)
-    context = jnp.einsum(
-        "hqk,khe->qhe", probs_low, split_heads(value), preferred_element_type=jnp.float32
-    )
-    return (
-        context.reshape(query.shape[0], HEADS * HEAD_DIM).astype(jnp.bfloat16),
-        probs,
-        probs_low,
-    )
-
-
-def attend_back(query, key, value, probs, probs_low, grad_context):
-    scale = HEAD_DIM ** (-0.5)
-    grad_heads = split_heads(grad_context)
-    grad_value = jnp.einsum(
-        "hqk,qhe->khe", probs_low, grad_heads, preferred_element_type=jnp.float32
-    )
-    grad_probs = jnp.einsum(
-        "qhe,khe->hqk", grad_heads, split_heads(value), preferred_element_type=jnp.float32
-    )
-    delta = jnp.sum(probs * grad_probs, -1, keepdims=True)
-    grad_scores = (probs * (grad_probs - delta)).astype(jnp.bfloat16)
-    grad_query = (
-        jnp.einsum(
-            "hqk,khe->qhe", grad_scores, split_heads(key), preferred_element_type=jnp.float32
-        )
-        * scale
-    )
-    grad_key = (
-        jnp.einsum(
-            "hqk,qhe->khe", grad_scores, split_heads(query), preferred_element_type=jnp.float32
-        )
-        * scale
-    )
-    width = HEADS * HEAD_DIM
-    return (
-        grad_query.reshape(query.shape[0], width).astype(jnp.bfloat16),
-        grad_key.reshape(key.shape[0], width),
-        grad_value.reshape(key.shape[0], width),
-    )
 
 
 def per_device(
     frames, cotangent, layer_norm_gain, w_query, w_key, w_value, w_out, lengths, win_lo, win_hi
 ):
-    input_rows = frames[0]
-    grad_y = cotangent[0]
-    length = lengths[0]
-    rows = input_rows.shape[0]
-    width = HEADS * HEAD_DIM
-    base = lax.axis_index("tm") * rows
-    normalized_input, standardized_input, inverse_deviation = layer_normalize(
-        input_rows, layer_norm_gain
-    )
-    gathered = gather_weights(w_query, w_key, w_value, w_out).reshape(8, 48, 16, 768)
-    full_q, full_k, full_v = (gathered[:, 12 * n: 12 * n + 12].reshape(1536, 768) for n in range(3))
-    full_o = jnp.concatenate([gathered[:, 36:42].reshape(768, 768), gathered[:, 42:].reshape(768, 768)], 1)
-    query = jnp.dot(normalized_input, full_q, preferred_element_type=jnp.float32).astype(
-        jnp.bfloat16
-    )
-    key = jnp.dot(normalized_input, full_k, preferred_element_type=jnp.float32).astype(jnp.bfloat16)
-    value = jnp.dot(normalized_input, full_v, preferred_element_type=jnp.float32).astype(
-        jnp.bfloat16
-    )
-    extended = extended_2(jnp.concatenate([key, value], 1), (("tm", 0),), REACH)
-    key_ext = extended[:, :width]
-    value_ext = extended[:, width:]
-    qpos = base + jnp.arange(rows, dtype=jnp.int32)
-    kpos = base - REACH + jnp.arange(rows + 2 * REACH, dtype=jnp.int32)
-    mask = window_mask(win_lo[0], win_hi[0], length, qpos, kpos)
-    context, probs, probs_low = attend(query, key_ext, value_ext, mask)
-    attn = jnp.dot(context, full_o, preferred_element_type=jnp.float32)
-    valid = qpos < length
-    frames_out = (input_rows.astype(jnp.float32) + jnp.where(valid[:, None], attn, 0.0)).astype(
-        jnp.bfloat16
-    )
-    masked_grad = jnp.where(valid[:, None], grad_y, jnp.zeros_like(grad_y))
-    grad_context = jnp.einsum(
-        "td,hd->th", masked_grad, full_o, preferred_element_type=jnp.float32
-    ).astype(jnp.bfloat16)
-    grad_query, grad_key_ext, grad_value_ext = attend_back(
-        query, key_ext, value_ext, probs, probs_low, grad_context
-    )
-    grad_kv_ext = jnp.concatenate([grad_key_ext, grad_value_ext], 1)
-    lower_rim = grad_kv_ext[:REACH]
-    upper_rim = grad_kv_ext[REACH + rows :]
-    from_next = shifted(lower_rim.astype(jnp.bfloat16), "tm", -1).astype(lower_rim.dtype)
-    from_prev = shifted(upper_rim.astype(jnp.bfloat16), "tm", 1).astype(upper_rim.dtype)
-    center = grad_kv_ext[REACH : REACH + rows]
-    center = center.at[:REACH].add(from_prev)
-    center = center.at[rows - REACH :].add(from_next)
-    grad_kv = center.astype(jnp.bfloat16)
-    grad_key = grad_kv[:, :width]
-    grad_value = grad_kv[:, width:]
-    *owned, gain_total, grad_frames = reduce_grads(
-        normalized_input, grad_query, grad_key, grad_value, context, masked_grad, gathered,
-        input_rows, grad_y, layer_norm_gain[None],
-    )
-    owner = lax.axis_index("dp") * 16 + lax.axis_index("tm")
-    owned.append(lax.dynamic_slice_in_dim(gain_total.reshape(2048), owner * 12, 12))
-    return (frames_out[None], grad_frames[None], owned[0], owned[1], owned[2], owned[3], owned[4])
+    gain = layer_norm_gain[None]
+    weights, nt, ct, ctx, gq, gk, gv, masked = forward(
+        w_query, w_key, w_value, w_out, frames[0], cotangent[0], gain, lengths, win_lo, win_hi)
+    sums = reduce_grads(nt, gq, gk, gv, ct, ctx, masked, weights, frames[0], cotangent[0], gain, lengths)
+    grad_wq, grad_wk, grad_wv, grad_wo, grad_gain, grad_frames, frames_out = write_outputs(*sums)
+    return (frames_out[None], grad_frames[None], grad_wq, grad_wk, grad_wv, grad_wo, grad_gain.reshape(12))
 
 
 def solution(mesh):

time: 175 us -> 130 us (0.74)
  matrix products: 27.5 us -> 0 us
  Pallas kernels: 97.4 us -> 115 us
  local copies, waits for them, and re-layouts: 28.1 us -> 12.5 us
  starting transfers between devices: 11.2 us -> 0 us
  other arithmetic: 8.81 us -> 0 us
    dot_general x10 -> x0, matrix products: 22.6 us -> none  [the longest x1 4.86 us: attend(): jnp.einsum('hqk,khe->qhe', probs_low, split_heads(value), preferred_eleme...]
    pallas_call x2 -> x3, Pallas kernels: 97.4 us -> 115 us  [the longest x1 62.2 us: forward(): pl.pallas_call(forward_kernel, out_shape=(sds((2, 4, 2, 3, 2, 4, 16, 768)...]
    ppermute x4 -> x0, starting transfers between devices: 11.2 us -> none  [the longest x2 5.43 us: shifted(): return lax.ppermute(value, axis, pairs)]
    slice x7 -> x0, local copies, waits for them, and re-layouts: 6.07 us -> none  [the longest x1 1.97 us: per_device(): gathered[:, 12 * n:12 * n + 12].reshape(1536, 768)]
    convert_element_type x4 -> x0, local copies, waits for them, and re-layouts: 4.94 us -> none  [the longest x1 1.91 us: attend(): context.reshape(query.shape[0], HEADS * HEAD_DIM).astype(jnp.bfloat16)]
    sub x1 -> x0, matrix products: 4.94 us -> none  [attend(): expo = jnp.exp(scores - jnp.max(scores, -1, keepdims=True))]
    concatenate x3 -> x0, other arithmetic: 2.4 us -> none  [the longest x1 1.34 us: per_device(): grad_kv_ext = jnp.concatenate([grad_key_ext, grad_value_ext], 1)]
    convert_element_type x3 -> x0, other arithmetic: 2.35 us -> none  [the longest x1 1.18 us: layer_normalize(): (standardized_input * norm_gain).astype(jnp.bfloat16)]
  transfers between devices with their start and end apart: 4 -> 0, of which waited for: 0 -> 0; matrix products, arithmetic and copies ran while one was open for 13% -> 0% of each run, Pallas kernels for 0% -> 0%
where the time goes in v3:
time: 130 us; the launch traced here: 129 us
  Pallas kernels  115 us (88%)
  local copies, waits for them, and re-layouts  12.5 us (10%)
  between operations  1.32 us (1%)
    pallas_call x1, Pallas kernels, forward(): pl.pallas_call(forward_kernel, out_shape=(sds((2, 4, 2, 3, 2, 4, 16, 768)...  62.2 us
    pallas_call x1, Pallas kernels, reduce_grads(): pl.pallas_call(reduce_kernel, out_shape=(sds((2, 3, 96, 128), F32), sds((...  50.5 us
    unnamed x30, local copies, waits for them, and re-layouts  11.8 us
    pallas_call x1, Pallas kernels, write_outputs(): pl.pallas_call(outputs_kernel, out_shape=(sds((12, 768), F32),) * 3 + (sd...  2.74 us

profile of v3, /device:TPU:1, one launch (start us, length us, event | category | flops | bytes accessed | tf_op | source)
XLA Modules:
  0.0 129.2 jit_solution(15151331144158033951)
XLA Ops:
  1.3 0.7 broadcast_in_dim.9.gain
  2.0 0.0 copy-start
  2.0 1.1 copy-done
  3.1 0.0 copy-start.8
  3.1 1.0 copy-done.8
  4.1 0.0 copy-start.9
  4.1 1.0 copy-done.9
  5.0 0.0 copy-start.10
  5.0 1.0 copy-done.10
  6.0 0.0 copy-start.11
  6.0 1.0 copy-done.11
  7.0 0.0 copy-start.13
  7.0 0.7 copy-done.13
  7.6 0.0 copy-start.14
  7.6 0.7 copy-done.14
  8.3 62.2 %forward.1 = (bf16[2,4,2,3,2,4,16,768]{7,6,5,4,3,2,1,0:T(8,128)(2,1)}, bf16[1536,256]{1,0:T(8,128)(2,1)S(1)}, bf16[768,256]{1,0:T(8,128)(2,1)S(1)}, bf16[256,768...) custom-call(bf16[12,16,768]{2,1,0:T(8,128)(2,1)S(1)} %bitcast.11, ...), custom_call_target="tpu_custom_call" | custom-call | tf_op jit(solution)/shard_map/forward/pallas_call | solution.py:376
  70.5 0.0 copy-start.1
  70.5 0.9 copy-done.1
  71.4 0.0 copy-start.2
  71.4 0.9 copy-done.2
  72.3 0.0 copy-start.3
  72.3 0.8 copy-done.3
  73.0 0.0 copy-start.4
  73.0 0.8 copy-done.4
  73.8 0.0 copy-start.5
  73.8 0.7 copy-done.5
  74.5 0.0 copy-start.6
  74.5 0.7 copy-done.6
  75.3 0.7 copy-done.7
  76.0 0.0 copy-done.12
  76.0 50.5 %reduce_grads.1 = (f32[2,3,96,128]{3,2,1,0:T(8,128)}, f32[16,128]{1,0:T(8,128)}, bf16[256,1536]{1,0:T(8,128)(2,1)}, bf16[256,1536]{1,0:T(8,128)(2,1)}) custom-call(bf16[1536,256]{1,0:T(8,128)(2,1)} %copy-done.1, bf16[256,768]{1,0:T(8,128)(2,1)} %copy-done.5, bf16[256,768]{1,0:T(8,128)(2,1)} %copy-done.6, bf16[256,768]{1,0:T(8,128)(2,1)} %copy-done.7, ...), custom_call_target="tpu_custom_call" | custom-call | tf_op jit(solution)/shard_map/reduce_grads/pallas_call | solution.py:707
  126.5 2.7 %write_outputs.1 = (f32[12,768]{1,0:T(8,128)}, f32[12,768]{1,0:T(8,128)}, f32[12,768]{1,0:T(8,128)}, f32[6,1536]{1,0:T(8,128)}, f32[1,12]{1,0:T(1,128)}, /*index...) custom-call(f32[2,3,96,128]{3,2,1,0:T(8,128)} %get-tuple-element.34.total, f32[16,128]{1,0:T(8,128)} %get-tuple-element.35.gain, ...), custom_call_target="tpu_custom_call" | custom-call | tf_op jit(solution)/shard_map/write_outputs/pallas_call | solution.py:747
  (2 shorter events, 0.0 us)
Async XLA Ops:
  2.0 1.1 copy-start
  3.1 1.0 copy-start.8
  4.1 1.0 copy-start.9
  5.0 1.0 copy-start.10
  6.0 1.0 copy-start.11
  7.0 0.7 copy-start.13
  7.6 0.7 copy-start.14
  8.3 67.7 %copy-start.12 = (f32[1,1536]{1,0:T(1,128)}, f32[1,1536]{1,0:T(1,128)S(1)}, u32[]{:S(2)}) copy-start(f32[1,1536]{1,0:T(1,128)S(1)} %broadcast_in_dim.9.gain) | copy-start | bytes 18436
  70.5 0.9 copy-start.1
  71.4 0.9 copy-start.2
  72.3 0.8 copy-start.3
  73.0 0.8 copy-start.4
  73.8 0.7 copy-start.5
  74.5 0.7 copy-start.6
  75.3 0.7 copy-start.7

commit v4 on v3

--- a/solution.py
+++ b/solution.py
@@ -162,7 +162,7 @@
         loads.append(pltpu.make_async_copy(wo.at[:, :, pl.ds(768 * n, 768)], held.at[pl.ds(36 + 6 * n, 6)], local.at[3 + n]))
     for copy in loads:
         copy.start()
-    greet(me, ring=True)
+    greet(me, far=True, ring=True)
     for copy in loads:
         copy.wait()
     own = []
@@ -243,15 +243,262 @@
     return lax.dot_general(a, b, dims, preferred_element_type=F32)
 
 
-def forward_kernel(
-    wq, wk, wv, wo, frames, cotangent, gain, lengths, lo, hi,
-    w_out, nt, ct, ctx, gq, gk, gv, masked,
-    held, w, nm, q6, gc6, kv, center, bias, rim_s, rim_r, send, recv, local, ring_send, ring_recv
+ORDERS = (("x", "y", "z"), ("y", "z", "x"), ("z", "x", "y"))
+DIMS = {"y": 0, "z": 1, "x": 2}
+
+
+class ReduceStage:
+    def __init__(self, me, axis, load, count, out, bufs, sems, base):
+        self.me, self.axis, self.load, self.count, self.out = me, axis, load, count, out
+        self.sent, self.got = bufs
+        self.send, self.recv = sems
+        self.base = base
+
+    def hop(self, k):
+        me = self.me
+        to = me.right(self.axis) if k % 2 == 0 else me.left(self.axis)
+        return pltpu.make_async_remote_copy(
+            src_ref=self.sent.at[k], dst_ref=self.got.at[k],
+            send_sem=self.send.at[self.base + k], recv_sem=self.recv.at[self.base + k],
+            device_id=me.device(self.axis, to), device_id_type=MESH)
+
+    def each(self, body):
+        if self.count == 1:
+            body(0)
+        else:
+            @pl.loop(0, self.count)
+            def _(m):
+                body(m)
+
+    def fill(self, k, j, p, extra=None):
+        def body(m):
+            v = self.load(j, p, m)
+            if extra is not None:
+                v = v + self.got[extra, m].astype(F32)
+            self.sent[k, m] = v.astype(self.sent.dtype)
+        self.each(body)
+        self.hop(k).start()
+
+    def start(self):
+        me = self.me
+        l, r, o = me.left(self.axis), me.right(self.axis), me.over(self.axis)
+        self.fill(0, o, 0)
+        self.fill(1, o, 1)
+        self.fill(2, r, 1)
+        self.fill(3, l, 0)
+
+    def relay(self):
+        me = self.me
+        self.hop(0).wait_recv()
+        self.fill(4, me.right(self.axis), 0, 0)
+        self.hop(1).wait_recv()
+        self.fill(5, me.left(self.axis), 1, 1)
+
+    def finish(self):
+        me = self.me
+        i = me.at(self.axis)
+        for k in (2, 3, 4, 5):
+            self.hop(k).wait_recv()
+
+        for p, a, b in ((0, 4, 3), (1, 2, 5)):
+            def body(m, p=p, a=a, b=b):
+                v = self.load(i, p, m) + self.got[a, m].astype(F32) + self.got[b, m].astype(F32)
+                self.out(p, m, v)
+            self.each(body)
+
+    def drain(self):
+        for k in range(6):
+            self.hop(k).wait_send()
+
+
+class GainSum:
+    def __init__(self, me, total, got, send, recv):
+        self.me, self.total, self.got, self.send, self.recv = me, total, got, send, recv
+
+    def hops(self, s):
+        me = self.me
+        if s == 3:
+            devices = (me.device(),)
+        else:
+            axis = "xyz"[s]
+            devices = tuple(me.device(axis, j) for j in (me.right(axis), me.left(axis), me.over(axis)))
+        return [
+            pltpu.make_async_remote_copy(
+                src_ref=self.total.at[s], dst_ref=self.got.at[3 * s + n], send_sem=self.send.at[3 * s + n],
+                recv_sem=self.recv.at[3 * s + n], device_id=device, device_id_type=MESH)
+            for n, device in enumerate(devices)
+        ]
+
+    def start(self, s):
+        for hop in self.hops(s):
+            hop.start()
+
+    def finish(self, s):
+        v = self.total[s]
+        for n, hop in enumerate(self.hops(s)):
+            hop.wait_recv()
+            v = v + self.got[3 * s + n]
+        self.total[s + 1] = v
+
+    def drain(self):
+        for s in range(4):
+            for hop in self.hops(s):
+                hop.wait_send()
+
+
+def reduce_scratch():
+    sem = pltpu.SemaphoreType.DMA
+    return [
+        pltpu.VMEM((3, 4, 4, 4, 96, 128), BF),
+        pltpu.VMEM((3, 6, 8, 96, 128), BF), pltpu.VMEM((3, 6, 8, 96, 128), BF),
+        pltpu.VMEM((3, 6, 2, 96, 128), BF), pltpu.VMEM((3, 6, 2, 96, 128), BF),
+        pltpu.VMEM((3, 6, 1, 48, 128), F32), pltpu.VMEM((3, 6, 1, 48, 128), F32),
+        pltpu.VMEM((3, 4, 4, 96, 128), F32),
+        pltpu.VMEM((3, 4, 96, 128), F32),
+        pltpu.VMEM((2, 3, 96, 128), F32),
+        pltpu.VMEM((5, 16, 128), F32), pltpu.VMEM((10, 16, 128), F32),
+        sem((54,)), sem((54,)), sem((3,)), sem((3,)), sem((11,)), sem((11,)),
+        pltpu.VMEM((3, 4, 4, 4, 96, 128), BF),
+        pltpu.VMEM((3, 4, 4, 4, 96, 128), F32),
+        pltpu.VMEM((1536, 384), F32), pltpu.VMEM((768, 256), F32),
+    ]
+
+
+def reduce_stages(me, half, scratch):
+    (r0, s1, d1, s2, d2, s3, d3, t1, t2, fin, gt, gg, send, recv, csend, crecv, gsend, grecv) = scratch[:18]
+
+    def load1(c):
+        axis = ORDERS[c][0]
+
+        def load(j, p, m):
+            a, b = 2 * p + m // 4, lax.rem(m, 4)
+            at = {"x": (a, b, j), "y": (j, a, b), "z": (a, j, b)}[axis]
+            return half[(c,) + at]
+        return load
+
+    def out1(c):
+        def out(p, m, v):
+            t1[c, 2 * p + m // 4, lax.rem(m, 4)] = v
+        return out
+
+    def load2(c):
+        def load(j, p, m):
+            return t1[c, 2 * p + m, j] if c == 2 else t1[c, j, 2 * p + m]
+        return load
+
+    def out2(c):
+        def out(p, m, v):
+            t2[c, 2 * p + m] = v
+        return out
+
+    def load3(c):
+        def load(j, p, m):
+            return t2[c, j, pl.ds(48 * p, 48)]
+        return load
+
+    def out3(c):
+        def out(p, m, v):
+            fin[me.core, c, pl.ds(48 * p, 48)] = v
+        return out
+
+    stages, base = [], 0
+    for c in range(3):
+        row = []
+        for n, (load, out, bufs, count) in enumerate(
+            ((load1, out1, (s1, d1), 8), (load2, out2, (s2, d2), 2), (load3, out3, (s3, d3), 1))
+        ):
+            row.append(ReduceStage(me, ORDERS[c][n], load(c), count, out(c), (bufs[0].at[c], bufs[1].at[c]), (send, recv), base))
+            base += 6
+        stages.append(row)
+    return stages
+
+
+def core_hop(me, scratch, c):
+    r0, csend, crecv, g = scratch[0], scratch[14], scratch[15], scratch[18]
+    return pltpu.make_async_remote_copy(
+        src_ref=g.at[c], dst_ref=r0.at[c], send_sem=csend.at[c], recv_sem=crecv.at[c],
+        device_id=me.device(), device_id_type=MESH)
+
+
+def weight_terms(refs, scratch, h, c, put):
+    nt, ct, gq, gk, gv, masked = refs
+    prod, prod_o = scratch[20:22]
+    columns = pl.ds(pl.multiple_of(h * 384 + c * 128, 128), 128)
+    rhs = jnp.concatenate([gq[:, columns], gk[:, columns], gv[:, columns]], 1)
+    prod[...] = jnp.dot(nt[...], rhs, preferred_element_type=F32)
+    columns = pl.ds(pl.multiple_of(h * 768 + c * 256, 128), 256)
+    prod_o[...] = jnp.dot(ct[...], masked[:, columns], preferred_element_type=F32)
+
+    @pl.loop(0, 32)
+    def _(pair):
+        upper = lax.broadcasted_iota(jnp.int32, (8, 128), 0) < 4
+        at = pl.multiple_of(pair * 24, 8)
+        tiles = [[prod_o[pl.ds(at + 8 * n, 8), pl.ds(128 * b, 128)] for b in range(2)] for n in range(3)]
+        mixed = (
+            jnp.where(upper, tiles[1][0], pltpu.roll(tiles[1][1], 4, 0)),
+            jnp.where(upper, pltpu.roll(tiles[1][0], 4, 0), tiles[1][1]),
+        )
+        yh, z, yl, xh = pair // 16, lax.rem(pair // 4, 4), lax.rem(pair // 2, 2), lax.rem(pair, 2)
+        for odd in range(2):
+            rows = pl.ds(pl.multiple_of(pair * 48 + 24 * odd, 8), 24)
+            parts = [prod[rows, pl.ds(128 * n, 128)] for n in range(3)]
+            parts += [tiles[2 * odd][0], tiles[2 * odd][1], mixed[odd]]
+            put((yh * 2 + yl, z, xh * 2 + odd), jnp.concatenate(parts, 0))
+
+
+def grad_normed(w, gq, gk, gv, out):
+    for s in range(4):
+        total = None
+        for n, g in enumerate((gq, gk, gv)):
+            term = dot(g[...], pair_rows(w, s, n), ROWS)
+            total = term if total is None else total + term
+        for b in range(3 * s, 3 * s + 3):
+            out[b // 2, b % 2] = total[:, 128 * (b - 3 * s):128 * (b - 3 * s) + 128]
+
+
+def norm_backward(frames, cotangent, gain, gn, grad_frames, gain_total):
+    gain_total[0] = jnp.zeros((16, 128), F32)
+
+    @pl.loop(0, 8)
+    def _(n):
+        rows = pl.ds(pl.multiple_of(n * 32, 32), 32)
+        xhat, inverse = norm(frames[rows])
+        grad = jnp.concatenate([gn[b // 2, b % 2, rows] for b in range(12)], 1)
+        gx = grad * xhat
+        for b in range(12):
+            gain_total[0, b:b + 1] += jnp.sum(gx[:, 128 * b: 128 * b + 128], 0, keepdims=True)
+        g = grad * gain[...]
+        first = jnp.mean(g, -1, keepdims=True)
+        second = jnp.mean(gx * gain[...], -1, keepdims=True)
+        back = inverse * (g - first - xhat * second)
+        grad_frames[rows] = (cotangent[rows].astype(F32) + back).astype(BF)
+
+
+def project_out(w, ctx, frames, length, out):
+    base = lax.axis_index("tm") * 256
+    for b in range(2):
+        attn = dot(ctx[:, :384], out_rows(w, 0, b)) + dot(ctx[:, 384:], out_rows(w, 1, b))
+        lanes = pl.ds(768 * b, 768)
+        frame = base + lax.broadcasted_iota(jnp.int32, (256, 768), 0)
+        out[:, lanes] = (frames[:, lanes].astype(F32) + jnp.where(frame < length, attn, 0.0)).astype(BF)
+
+
+def block_kernel(
+    wq, wk, wv, wo, frames_hbm, cotangent_hbm, gain_hbm, lengths, lo_hbm, hi_hbm,
+    total, gain_out, grad_frames_hbm, frames_out_hbm,
+    nt, ct, ctx, gq, gk, gv, masked, frames, cotangent, gain, lo, hi, grad_frames, frames_out,
+    held, w, nm, q6, gc6, kv, center, bias, rim_s, rim_r, send, recv, local, ring_send, ring_recv, *scratch
 ):
     me = Place()
     length = lengths[0]
     base = lax.axis_index("tm") * 256
+    loads = ((frames_hbm, frames), (gain_hbm, gain), (cotangent_hbm, cotangent), (lo_hbm, lo), (hi_hbm, hi))
+    loads = [pltpu.make_async_copy(src, dst, local.at[6 + n]) for n, (src, dst) in enumerate(loads)]
+    for copy in loads:
+        copy.start()
     rows = start_gather(me, (wq, wk, wv, wo), held, w, send, recv, local)
+    for copy in loads:
+        copy.wait()
 
     @pl.loop(0, 8)
     def _(n):
@@ -276,8 +523,6 @@
             bias[b] = jnp.where(seen | (kp == qp), 0.0, -1e30)
 
     finish_gather(rows, under)
-    spread = pltpu.make_async_copy(w, w_out, local.at[6])
-    spread.start()
 
     def project(n):
         total = None
@@ -360,297 +605,10 @@
             lanes = pl.ds(128 * p, 128)
             out[:128, lanes] = (center[p, m, :128] + rim_r[p, 1, m].astype(F32)).astype(BF)
             out[128:, lanes] = (center[p, m, 128:] + rim_r[p, 0, m].astype(F32)).astype(BF)
-    for p in range(6):
-        for right in range(2):
-            halo(p, right).wait_send()
-            rim(p, right).wait_send()
-    for row in rows:
-        for stage in row:
-            stage.drain()
-    spread.wait()
-
-
-def forward(wq, wk, wv, wo, frames, cotangent, gain, lengths, lo, hi):
-    vm, hbm = pl.BlockSpec(memory_space=pltpu.VMEM), pl.BlockSpec(memory_space=pltpu.HBM)
-    sds, sem = jax.ShapeDtypeStruct, pltpu.SemaphoreType.DMA
-    return pl.pallas_call(
-        forward_kernel,
-        out_shape=(
-            sds((2, 4, 2, 3, 2, 4, 16, 768), BF), sds((1536, 256), BF), sds((768, 256), BF),
-            sds((256, 768), BF), sds((256, 768), BF), sds((256, 768), BF), sds((256, 768), BF), sds((256, 1536), BF),
-        ),
-        in_specs=[hbm] * 4 + [vm] * 3 + [pl.BlockSpec(memory_space=pltpu.SMEM)] + [vm] * 2,
-        out_specs=(hbm,) + (vm,) * 7,
-        scratch_shapes=[
-            pltpu.VMEM((48, 16, 768), BF),
-            pltpu.VMEM((2, 4, 2, 3, 2, 4, 16, 768), BF),
-            pltpu.VMEM((256, 1536), BF),
-            pltpu.VMEM((6, 256, 128), BF), pltpu.VMEM((6, 256, 128), BF),
-            pltpu.VMEM((6, 2, 512, 128), BF),
-            pltpu.VMEM((6, 2, 256, 128), F32),
-            pltpu.VMEM((2, 384, 128), F32),
-            pltpu.VMEM((6, 2, 2, 128, 128), BF), pltpu.VMEM((6, 2, 2, 128, 128), BF),
-            sem((GATHER_SEMS,)), sem((GATHER_SEMS,)), sem((7,)), sem((24,)), sem((24,)),
-        ],
-        compiler_params=pltpu.CompilerParams(collective_id=0, has_side_effects=True, vmem_limit_bytes=48 << 20),
-        name="forward",
-    )(wq.reshape(12, 16, 768), wk.reshape(12, 16, 768), wv.reshape(12, 16, 768), wo.reshape(6, 16, 1536),
-      frames, cotangent, gain, lengths, lo, hi)
-
-
-ORDERS = (("x", "y", "z"), ("y", "z", "x"), ("z", "x", "y"))
-DIMS = {"y": 0, "z": 1, "x": 2}
-
-
-class ReduceStage:
-    def __init__(self, me, axis, load, count, out, bufs, sems, base):
-        self.me, self.axis, self.load, self.count, self.out = me, axis, load, count, out
-        self.sent, self.got = bufs
-        self.send, self.recv = sems
-        self.base = base
-
-    def hop(self, k):
-        me = self.me
-        to = me.right(self.axis) if k % 2 == 0 else me.left(self.axis)
-        return pltpu.make_async_remote_copy(
-            src_ref=self.sent.at[k], dst_ref=self.got.at[k],
-            send_sem=self.send.at[self.base + k], recv_sem=self.recv.at[self.base + k],
-            device_id=me.device(self.axis, to), device_id_type=MESH)
-
-    def each(self, body):
-        if self.count == 1:
-            body(0)
-        else:
-            @pl.loop(0, self.count)
-            def _(m):
-                body(m)
-
-    def fill(self, k, j, p, extra=None):
-        def body(m):
-            v = self.load(j, p, m)
-            if extra is not None:
-                v = v + self.got[extra, m].astype(F32)
-            self.sent[k, m] = v.astype(self.sent.dtype)
-        self.each(body)
-        self.hop(k).start()
-
-    def start(self):
-        me = self.me
-        l, r, o = me.left(self.axis), me.right(self.axis), me.over(self.axis)
-        self.fill(0, o, 0)
-        self.fill(1, o, 1)
-        self.fill(2, r, 1)
-        self.fill(3, l, 0)
-
-    def relay(self):
-        me = self.me
-        self.hop(0).wait_recv()
-        self.fill(4, me.right(self.axis), 0, 0)
-        self.hop(1).wait_recv()
-        self.fill(5, me.left(self.axis), 1, 1)
-
-    def finish(self):
-        me = self.me
-        i = me.at(self.axis)
-        for k in (2, 3, 4, 5):
-            self.hop(k).wait_recv()
-
-        for p, a, b in ((0, 4, 3), (1, 2, 5)):
-            def body(m, p=p, a=a, b=b):
-                v = self.load(i, p, m) + self.got[a, m].astype(F32) + self.got[b, m].astype(F32)
-                self.out(p, m, v)
-            self.each(body)
-
-    def drain(self):
-        for k in range(6):
-            self.hop(k).wait_send()
-
-
-class GainSum:
-    def __init__(self, me, total, got, send, recv):
-        self.me, self.total, self.got, self.send, self.recv = me, total, got, send, recv
-
-    def hops(self, s):
-        me = self.me
-        if s == 3:
-            devices = (me.device(),)
-        else:
-            axis = "xyz"[s]
-            devices = tuple(me.device(axis, j) for j in (me.right(axis), me.left(axis), me.over(axis)))
-        return [
-            pltpu.make_async_remote_copy(
-                src_ref=self.total.at[s], dst_ref=self.got.at[3 * s + n], send_sem=self.send.at[3 * s + n],
-                recv_sem=self.recv.at[3 * s + n], device_id=device, device_id_type=MESH)
-            for n, device in enumerate(devices)
-        ]
-
-    def start(self, s):
-        for hop in self.hops(s):
-            hop.start()
-
-    def finish(self, s):
-        v = self.total[s]
-        for n, hop in enumerate(self.hops(s)):
-            hop.wait_recv()
-            v = v + self.got[3 * s + n]
-        self.total[s + 1] = v
-
-    def drain(self):
-        for s in range(4):
-            for hop in self.hops(s):
-                hop.wait_send()
-
-
-def reduce_scratch():
-    sem = pltpu.SemaphoreType.DMA
-    return [
-        pltpu.VMEM((3, 4, 4, 4, 96, 128), BF),
-        pltpu.VMEM((3, 6, 8, 96, 128), BF), pltpu.VMEM((3, 6, 8, 96, 128), BF),
-        pltpu.VMEM((3, 6, 2, 96, 128), BF), pltpu.VMEM((3, 6, 2, 96, 128), BF),
-        pltpu.VMEM((3, 6, 1, 48, 128), F32), pltpu.VMEM((3, 6, 1, 48, 128), F32),
-        pltpu.VMEM((3, 4, 4, 96, 128), F32),
-        pltpu.VMEM((3, 4, 96, 128), F32),
-        pltpu.VMEM((2, 3, 96, 128), F32),
-        pltpu.VMEM((5, 16, 128), F32), pltpu.VMEM((10, 16, 128), F32),
-        sem((54,)), sem((54,)), sem((3,)), sem((3,)), sem((11,)), sem((11,)),
-        pltpu.VMEM((3, 4, 4, 4, 96, 128), BF),
-        pltpu.VMEM((3, 4, 4, 4, 96, 128), F32),
-        pltpu.VMEM((1536, 384), F32), pltpu.VMEM((768, 256), F32),
-        pltpu.VMEM((256, 1536), F32),
-        pltpu.VMEM((2, 4, 2, 3, 2, 4, 16, 768), BF), sem,
-    ]
-
-
-def reduce_stages(me, half, scratch):
-    (r0, s1, d1, s2, d2, s3, d3, t1, t2, fin, gt, gg, send, recv, csend, crecv, gsend, grecv) = scratch[:18]
-
-    def load1(c):
-        axis = ORDERS[c][0]
-
-        def load(j, p, m):
-            a, b = 2 * p + m // 4, lax.rem(m, 4)
-            at = {"x": (a, b, j), "y": (j, a, b), "z": (a, j, b)}[axis]
-            return half[(c,) + at]
-        return load
-
-    def out1(c):
-        def out(p, m, v):
-            t1[c, 2 * p + m // 4, lax.rem(m, 4)] = v
-        return out
-
-    def load2(c):
-        def load(j, p, m):
-            return t1[c, 2 * p + m, j] if c == 2 else t1[c, j, 2 * p + m]
-        return load
-
-    def out2(c):
-        def out(p, m, v):
-            t2[c, 2 * p + m] = v
-        return out
-
-    def load3(c):
-        def load(j, p, m):
-            return t2[c, j, pl.ds(48 * p, 48)]
-        return load
-
-    def out3(c):
-        def out(p, m, v):
-            fin[me.core, c, pl.ds(48 * p, 48)] = v
-        return out
-
-    stages, base = [], 0
-    for c in range(3):
-        row = []
-        for n, (load, out, bufs, count) in enumerate(
-            ((load1, out1, (s1, d1), 8), (load2, out2, (s2, d2), 2), (load3, out3, (s3, d3), 1))
-        ):
-            row.append(ReduceStage(me, ORDERS[c][n], load(c), count, out(c), (bufs[0].at[c], bufs[1].at[c]), (send, recv), base))
-            base += 6
-        stages.append(row)
-    return stages
-
-
-def core_hop(me, scratch, c):
-    r0, csend, crecv, g = scratch[0], scratch[14], scratch[15], scratch[18]
-    return pltpu.make_async_remote_copy(
-        src_ref=g.at[c], dst_ref=r0.at[c], send_sem=csend.at[c], recv_sem=crecv.at[c],
-        device_id=me.device(), device_id_type=MESH)
-
-
-def weight_terms(refs, scratch, h, c, put):
-    nt, ct, gq, gk, gv, masked = refs
-    prod, prod_o = scratch[20:22]
-    columns = pl.ds(pl.multiple_of(h * 384 + c * 128, 128), 128)
-    rhs = jnp.concatenate([gq[:, columns], gk[:, columns], gv[:, columns]], 1)
-    prod[...] = jnp.dot(nt[...], rhs, preferred_element_type=F32)
-    columns = pl.ds(pl.multiple_of(h * 768 + c * 256, 128), 256)
-    prod_o[...] = jnp.dot(ct[...], masked[:, columns], preferred_element_type=F32)
-
-    @pl.loop(0, 32)
-    def _(pair):
-        upper = lax.broadcasted_iota(jnp.int32, (8, 128), 0) < 4
-        at = pl.multiple_of(pair * 24, 8)
-        tiles = [[prod_o[pl.ds(at + 8 * n, 8), pl.ds(128 * b, 128)] for b in range(2)] for n in range(3)]
-        mixed = (
-            jnp.where(upper, tiles[1][0], pltpu.roll(tiles[1][1], 4, 0)),
-            jnp.where(upper, pltpu.roll(tiles[1][0], 4, 0), tiles[1][1]),
-        )
-        yh, z, yl, xh = pair // 16, lax.rem(pair // 4, 4), lax.rem(pair // 2, 2), lax.rem(pair, 2)
-        for odd in range(2):
-            rows = pl.ds(pl.multiple_of(pair * 48 + 24 * odd, 8), 24)
-            parts = [prod[rows, pl.ds(128 * n, 128)] for n in range(3)]
-            parts += [tiles[2 * odd][0], tiles[2 * odd][1], mixed[odd]]
-            put((yh * 2 + yl, z, xh * 2 + odd), jnp.concatenate(parts, 0))
-
-
-def grad_normed(w, gq, gk, gv, out):
-    for s in range(4):
-        total = None
-        for n, g in enumerate((gq, gk, gv)):
-            term = dot(g[...], pair_rows(w, s, n), ROWS)
-            total = term if total is None else total + term
-        out[:, 384 * s: 384 * s + 384] = total
-
-
-def norm_backward(frames, cotangent, gain, gn, grad_frames, gain_total):
-    gain_total[0] = jnp.zeros((16, 128), F32)
-
-    @pl.loop(0, 8)
-    def _(n):
-        rows = pl.ds(pl.multiple_of(n * 32, 32), 32)
-        xhat, inverse = norm(frames[rows])
-        grad = gn[rows]
-        gx = grad * xhat
-        for b in range(12):
-            gain_total[0, b:b + 1] += jnp.sum(gx[:, 128 * b: 128 * b + 128], 0, keepdims=True)
-        g = grad * gain[...]
-        first = jnp.mean(g, -1, keepdims=True)
-        second = jnp.mean(gx * gain[...], -1, keepdims=True)
-        back = inverse * (g - first - xhat * second)
-        grad_frames[rows] = (cotangent[rows].astype(F32) + back).astype(BF)
-
-
-def project_out(w, ctx, frames, length, out):
-    base = lax.axis_index("tm") * 256
-    for b in range(2):
-        attn = dot(ctx[:, :384], out_rows(w, 0, b)) + dot(ctx[:, 384:], out_rows(w, 1, b))
-        lanes = pl.ds(768 * b, 768)
-        frame = base + lax.broadcasted_iota(jnp.int32, (256, 768), 0)
-        out[:, lanes] = (frames[:, lanes].astype(F32) + jnp.where(frame < length, attn, 0.0)).astype(BF)
-
-
-def reduce_kernel(
-    nt, gq, gk, gv, ct, ctx, masked, w_hbm, frames, cotangent, gain, lengths,
-    total, gain_out, grad_frames, frames_out, *scratch
-):
-    me = Place()
+
     r0, fin, gt, gg, gsend, grecv = scratch[0], scratch[9], scratch[10], scratch[11], scratch[16], scratch[17]
     for_other, half = scratch[18:20]
-    gn, w = scratch[22:24]
-    load = pltpu.make_async_copy(w_hbm, w, scratch[24])
-    load.start()
     refs = (nt, ct, gq, gk, gv, masked)
-    greet(me, far=True)
     for c in range(3):
         def put(at, v, c=c):
             for_other[(c,) + at] = v.astype(BF)
@@ -665,13 +623,18 @@
             half[(c,) + at] = v + r0[(c,) + at].astype(F32)
         weight_terms(refs, scratch, me.core, c, put)
         stages[c][0].start()
-    load.wait()
-    grad_normed(w, gq, gk, gv, gn)
+    grad_normed(w, gq, gk, gv, center)
     for c in range(3):
         stages[c][0].relay()
-    norm_backward(frames, cotangent, gain, gn, grad_frames, gt)
+    norm_backward(frames, cotangent, gain, center, grad_frames, gt)
+    stores = [
+        pltpu.make_async_copy(grad_frames, grad_frames_hbm, local.at[11]),
+        pltpu.make_async_copy(frames_out, frames_out_hbm, local.at[12]),
+    ]
+    stores[0].start()
     sum_gain.start(0)
-    project_out(w, ctx, frames, lengths[0], frames_out)
+    project_out(w, ctx, frames, length, frames_out)
+    stores[1].start()
     for n in range(3):
         for c in range(3):
             stages[c][n].finish()
@@ -699,20 +662,44 @@
     last(me.core).wait_send()
     last(1 - me.core).wait_recv()
     total[...] = fin[...]
-
-
-def reduce_grads(*args):
+    for p in range(6):
+        for right in range(2):
+            halo(p, right).wait_send()
+            rim(p, right).wait_send()
+    for row in rows:
+        for stage in row:
+            stage.drain()
+    for copy in stores:
+        copy.wait()
+
+
+def block(wq, wk, wv, wo, *args):
     vm, hbm = pl.BlockSpec(memory_space=pltpu.VMEM), pl.BlockSpec(memory_space=pltpu.HBM)
-    sds = jax.ShapeDtypeStruct
+    sds, sem = jax.ShapeDtypeStruct, pltpu.SemaphoreType.DMA
     return pl.pallas_call(
-        reduce_kernel,
+        block_kernel,
         out_shape=(sds((2, 3, 96, 128), F32), sds((16, 128), F32), sds((256, 1536), BF), sds((256, 1536), BF)),
-        in_specs=[vm] * 7 + [hbm] + [vm] * 3 + [pl.BlockSpec(memory_space=pltpu.SMEM)],
-        out_specs=(vm,) * 4,
-        scratch_shapes=reduce_scratch(),
-        compiler_params=pltpu.CompilerParams(collective_id=1, has_side_effects=True, vmem_limit_bytes=62 << 20),
-        name="reduce_grads",
-    )(*args)
+        in_specs=[hbm] * 7 + [pl.BlockSpec(memory_space=pltpu.SMEM)] + [hbm] * 2,
+        out_specs=(vm, vm, hbm, hbm),
+        scratch_shapes=[
+            pltpu.VMEM((1536, 256), BF), pltpu.VMEM((768, 256), BF), pltpu.VMEM((256, 768), BF),
+            pltpu.VMEM((256, 768), BF), pltpu.VMEM((256, 768), BF), pltpu.VMEM((256, 768), BF),
+            pltpu.VMEM((256, 1536), BF), pltpu.VMEM((256, 1536), BF), pltpu.VMEM((256, 1536), BF),
+            pltpu.VMEM((1, 1536), F32), pltpu.VMEM((1, 256), jnp.int32), pltpu.VMEM((1, 256), jnp.int32),
+            pltpu.VMEM((256, 1536), BF), pltpu.VMEM((256, 1536), BF),
+            pltpu.VMEM((48, 16, 768), BF),
+            pltpu.VMEM((2, 4, 2, 3, 2, 4, 16, 768), BF),
+            pltpu.VMEM((256, 1536), BF),
+            pltpu.VMEM((6, 256, 128), BF), pltpu.VMEM((6, 256, 128), BF),
+            pltpu.VMEM((6, 2, 512, 128), BF),
+            pltpu.VMEM((6, 2, 256, 128), F32),
+            pltpu.VMEM((2, 384, 128), F32),
+            pltpu.VMEM((6, 2, 2, 128, 128), BF), pltpu.VMEM((6, 2, 2, 128, 128), BF),
+            sem((GATHER_SEMS,)), sem((GATHER_SEMS,)), sem((13,)), sem((24,)), sem((24,)),
+        ] + reduce_scratch(),
+        compiler_params=pltpu.CompilerParams(collective_id=0, has_side_effects=True, vmem_limit_bytes=67043328),
+        name="block",
+    )(wq.reshape(12, 16, 768), wk.reshape(12, 16, 768), wv.reshape(12, 16, 768), wo.reshape(6, 16, 1536), *args)
 
 
 def outputs_kernel(total, gain, grad_in, frames_in, out_q, out_k, out_v, out_o, out_gain, grad_frames, frames_out):
@@ -758,9 +745,8 @@
     frames, cotangent, layer_norm_gain, w_query, w_key, w_value, w_out, lengths, win_lo, win_hi
 ):
     gain = layer_norm_gain[None]
-    weights, nt, ct, ctx, gq, gk, gv, masked = forward(
+    sums = block(
         w_query, w_key, w_value, w_out, frames[0], cotangent[0], gain, lengths, win_lo, win_hi)
-    sums = reduce_grads(nt, gq, gk, gv, ct, ctx, masked, weights, frames[0], cotangent[0], gain, lengths)
     grad_wq, grad_wk, grad_wv, grad_wo, grad_gain, grad_frames, frames_out = write_outputs(*sums)
     return (frames_out[None], grad_frames[None], grad_wq, grad_wk, grad_wv, grad_wo, grad_gain.reshape(12))
 

time: 130 us -> 111 us (0.85)
  local copies, waits for them, and re-layouts: 12.5 us -> 0.63 us
  Pallas kernels: 115 us -> 108 us
    unnamed x30 -> x2, local copies, waits for them, and re-layouts: 11.8 us -> 0.03 us
    pallas_call x2 -> x1, Pallas kernels: 113 us -> 106 us  [block(): pl.pallas_call(block_kernel, out_shape=(sds((2, 3, 96, 128), F32), sds((1...]
where the time goes in v4:
time: 111 us; the launch traced here: 110 us
  Pallas kernels  108 us (97%)
  between operations  1.31 us (1%)
    pallas_call x1, Pallas kernels, block(): pl.pallas_call(block_kernel, out_shape=(sds((2, 3, 96, 128), F32), sds((1...  106 us
    pallas_call x1, Pallas kernels, write_outputs(): pl.pallas_call(outputs_kernel, out_shape=(sds((12, 768), F32),) * 3 + (sd...  2.74 us

profile of v4, /device:TPU:1, one launch (start us, length us, event | category | flops | bytes accessed | tf_op | source)
XLA Modules:
  0.0 110.3 jit_solution(11793928115286102055)
XLA Ops:
  0.6 0.0 copy-start
  1.3 0.0 copy-done
  1.3 0.6 broadcast_in_dim.9.gain_hbm
  1.9 105.7 %block.1 = (f32[2,3,96,128]{3,2,1,0:T(8,128)}, f32[16,128]{1,0:T(8,128)}, bf16[256,1536]{1,0:T(8,128)(2,1)}, bf16[256,1536]{1,0:T(8,128)(2,1)}) custom-call(bf16[12,16,768]{2,1,0:T(8,128)(2,1)} %bitcast.11, bf16[12,16,768]{2,1,0:T(8,128)(2,1)} %bitcast.12, bf16[12,16,768]{2,1,0:T(8,128)(2,1)} %bitcast.13, bf16[6,16,1536]{2,1,0:T(8,128)(2,1)} %bitcast.14, ...), custom_call_target="tpu_custom_call" | custom-call | tf_op jit(solution)/shard_map/block/pallas_call | solution.py:679
  107.6 2.7 %write_outputs.1 = (f32[12,768]{1,0:T(8,128)}, f32[12,768]{1,0:T(8,128)}, f32[12,768]{1,0:T(8,128)}, f32[6,1536]{1,0:T(8,128)}, f32[1,12]{1,0:T(1,128)}, /*index...) custom-call(f32[2,3,96,128]{3,2,1,0:T(8,128)} %get-tuple-element.18.total, f32[16,128]{1,0:T(8,128)} %get-tuple-element.19.gain, ...), custom_call_target="tpu_custom_call" | custom-call | tf_op jit(solution)/shard_map/write_outputs/pallas_call | solution.py:734
Async XLA Ops:
  0.6 0.7 copy-start

commit v5 on v4

--- a/solution.py
+++ b/solution.py
@@ -162,7 +162,6 @@
         loads.append(pltpu.make_async_copy(wo.at[:, :, pl.ds(768 * n, 768)], held.at[pl.ds(36 + 6 * n, 6)], local.at[3 + n]))
     for copy in loads:
         copy.start()
-    greet(me, far=True, ring=True)
     for copy in loads:
         copy.wait()
     own = []
@@ -173,6 +172,7 @@
     own = [pltpu.make_async_copy(src, dst, local.at[n]) for n, (src, dst) in enumerate(own)]
     for copy in own:
         copy.start()
+    greet(me, ring=True)
     for copy in own:
         copy.wait()
     rows = gather_stages(me, w, send, recv)
@@ -181,23 +181,24 @@
     return rows
 
 
-def finish_gather(rows, under):
+def finish_gather(rows, first, second):
     a, b, c = rows
     c[0].relay()
+    a[0].relay()
+    b[0].relay()
     c[0].finish()
     c[1].start()
-    a[0].relay()
-    b[0].relay()
     a[0].finish()
     a[1].start()
     b[0].finish()
+    c[1].relay()
     b[1].start()
-    c[1].relay()
     c[1].finish()
     c[2].start()
-    under()
+    first()
     a[1].relay()
     b[1].relay()
+    second()
     c[2].relay()
     a[1].finish()
     b[1].finish()
@@ -309,6 +310,41 @@
     def drain(self):
         for k in range(6):
             self.hop(k).wait_send()
+
+
+class LastStage:
+    def __init__(self, me, axis, terms, got, out, sems, base):
+        self.me, self.axis, self.terms, self.got, self.out = me, axis, terms, got, out
+        self.send, self.recv = sems
+        self.base = base
+
+    def hops(self):
+        me = self.me
+        to = (me.over(self.axis), me.right(self.axis), me.left(self.axis))
+        return [
+            pltpu.make_async_remote_copy(
+                src_ref=self.terms.at[j], dst_ref=self.got.at[n], send_sem=self.send.at[self.base + n],
+                recv_sem=self.recv.at[self.base + n], device_id=me.device(self.axis, j), device_id_type=MESH)
+            for n, j in enumerate(to)
+        ]
+
+    def start(self):
+        for hop in self.hops():
+            hop.start()
+
+    def relay(self):
+        pass
+
+    def finish(self):
+        v = self.terms[self.me.at(self.axis)]
+        for n, hop in enumerate(self.hops()):
+            hop.wait_recv()
+            v = v + self.got[n]
+        self.out[...] = v
+
+    def drain(self):
+        for hop in self.hops():
+            hop.wait_send()
 
 
 class GainSum:
@@ -352,7 +388,7 @@
         pltpu.VMEM((3, 4, 4, 4, 96, 128), BF),
         pltpu.VMEM((3, 6, 8, 96, 128), BF), pltpu.VMEM((3, 6, 8, 96, 128), BF),
         pltpu.VMEM((3, 6, 2, 96, 128), BF), pltpu.VMEM((3, 6, 2, 96, 128), BF),
-        pltpu.VMEM((3, 6, 1, 48, 128), F32), pltpu.VMEM((3, 6, 1, 48, 128), F32),
+        pltpu.VMEM((8, 128), F32), pltpu.VMEM((3, 3, 96, 128), F32),
         pltpu.VMEM((3, 4, 4, 96, 128), F32),
         pltpu.VMEM((3, 4, 96, 128), F32),
         pltpu.VMEM((2, 3, 96, 128), F32),
@@ -391,24 +427,16 @@
             t2[c, 2 * p + m] = v
         return out
 
-    def load3(c):
-        def load(j, p, m):
-            return t2[c, j, pl.ds(48 * p, 48)]
-        return load
-
-    def out3(c):
-        def out(p, m, v):
-            fin[me.core, c, pl.ds(48 * p, 48)] = v
-        return out
-
     stages, base = [], 0
     for c in range(3):
         row = []
         for n, (load, out, bufs, count) in enumerate(
-            ((load1, out1, (s1, d1), 8), (load2, out2, (s2, d2), 2), (load3, out3, (s3, d3), 1))
+            ((load1, out1, (s1, d1), 8), (load2, out2, (s2, d2), 2))
         ):
             row.append(ReduceStage(me, ORDERS[c][n], load(c), count, out(c), (bufs[0].at[c], bufs[1].at[c]), (send, recv), base))
             base += 6
+        row.append(LastStage(me, ORDERS[c][2], t2.at[c], d3.at[c], fin.at[me.core, c], (send, recv), base))
+        base += 6
         stages.append(row)
     return stages
 
@@ -497,16 +525,18 @@
     for copy in loads:
         copy.start()
     rows = start_gather(me, (wq, wk, wv, wo), held, w, send, recv, local)
-    for copy in loads:
-        copy.wait()
-
-    @pl.loop(0, 8)
-    def _(n):
-        at = pl.ds(pl.multiple_of(n * 32, 32), 32)
-        xhat, _ = norm(frames[at])
-        nm[at] = (xhat * gain[...]).astype(BF)
-
-    def under():
+
+    def normalize():
+        for copy in loads:
+            copy.wait()
+
+        @pl.loop(0, 8)
+        def _(n):
+            at = pl.ds(pl.multiple_of(n * 32, 32), 32)
+            xhat, _ = norm(frames[at])
+            nm[at] = (xhat * gain[...]).astype(BF)
+
+    def prepare():
         nt[...] = nm[...].T
 
         @pl.loop(0, 8)
@@ -522,7 +552,7 @@
             seen = (kp >= lo[:, cols]) & (kp < hi[:, cols]) & (kp < length)
             bias[b] = jnp.where(seen | (kp == qp), 0.0, -1e30)
 
-    finish_gather(rows, under)
+    finish_gather(rows, normalize, prepare)
 
     def project(n):
         total = None
@@ -609,23 +639,31 @@
     r0, fin, gt, gg, gsend, grecv = scratch[0], scratch[9], scratch[10], scratch[11], scratch[16], scratch[17]
     for_other, half = scratch[18:20]
     refs = (nt, ct, gq, gk, gv, masked)
-    for c in range(3):
-        def put(at, v, c=c):
+    stages = reduce_stages(me, half, scratch)
+    sum_gain = GainSum(me, gt, gg, gsend, grecv)
+
+    def send_other(c):
+        def put(at, v):
             for_other[(c,) + at] = v.astype(BF)
         weight_terms(refs, scratch, 1 - me.core, c, put)
         core_hop(me, scratch, c).start()
-    stages = reduce_stages(me, half, scratch)
-    sum_gain = GainSum(me, gt, gg, gsend, grecv)
-    for c in range(3):
+
+    def start_own(c):
         core_hop(me, scratch, c).wait_recv()
 
-        def put(at, v, c=c):
+        def put(at, v):
             half[(c,) + at] = v + r0[(c,) + at].astype(F32)
         weight_terms(refs, scratch, me.core, c, put)
         stages[c][0].start()
+
+    for c in range(3):
+        send_other(c)
+    for c in range(3):
+        start_own(c)
+    stages[0][0].relay()
     grad_normed(w, gq, gk, gv, center)
-    for c in range(3):
-        stages[c][0].relay()
+    stages[1][0].relay()
+    stages[2][0].relay()
     norm_backward(frames, cotangent, gain, center, grad_frames, gt)
     stores = [
         pltpu.make_async_copy(grad_frames, grad_frames_hbm, local.at[11]),

time: 111 us -> 104 us (0.937)
  Pallas kernels: 108 us -> 101 us
    pallas_call x1, Pallas kernels: 106 us -> 98.7 us  [block(): pl.pallas_call(block_kernel, out_shape=(sds((2, 3, 96, 128), F32), sds((1...]
where the time goes in v5:
time: 104 us; the launch traced here: 103 us
  Pallas kernels  101 us (97%)
  between operations  1.31 us (1%)
    pallas_call x1, Pallas kernels, block(): pl.pallas_call(block_kernel, out_shape=(sds((2, 3, 96, 128), F32), sds((1...  98.7 us
    pallas_call x1, Pallas kernels, write_outputs(): pl.pallas_call(outputs_kernel, out_shape=(sds((12, 768), F32),) * 3 + (sd...  2.74 us

profile of v5, /device:TPU:1, one launch (start us, length us, event | category | flops | bytes accessed | tf_op | source)
XLA Modules:
  0.0 103.4 jit_solution(4152065716164960161)
XLA Ops:
  0.6 0.0 copy-start
  1.3 0.0 copy-done
  1.3 0.6 broadcast_in_dim.9.gain_hbm
  1.9 98.7 %block.1 = (f32[2,3,96,128]{3,2,1,0:T(8,128)}, f32[16,128]{1,0:T(8,128)}, bf16[256,1536]{1,0:T(8,128)(2,1)}, bf16[256,1536]{1,0:T(8,128)(2,1)}) custom-call(bf16[12,16,768]{2,1,0:T(8,128)(2,1)} %bitcast.11, bf16[12,16,768]{2,1,0:T(8,128)(2,1)} %bitcast.12, bf16[12,16,768]{2,1,0:T(8,128)(2,1)} %bitcast.13, bf16[6,16,1536]{2,1,0:T(8,128)(2,1)} %bitcast.14, ...), custom_call_target="tpu_custom_call" | custom-call | tf_op jit(solution)/shard_map/block/pallas_call | solution.py:717
  100.7 2.7 %write_outputs.1 = (f32[12,768]{1,0:T(8,128)}, f32[12,768]{1,0:T(8,128)}, f32[12,768]{1,0:T(8,128)}, f32[6,1536]{1,0:T(8,128)}, f32[1,12]{1,0:T(1,128)}, /*index...) custom-call(f32[2,3,96,128]{3,2,1,0:T(8,128)} %get-tuple-element.18.total, f32[16,128]{1,0:T(8,128)} %get-tuple-element.19.gain, ...), custom_call_target="tpu_custom_call" | custom-call | tf_op jit(solution)/shard_map/write_outputs/pallas_call | solution.py:772
Async XLA Ops:
  0.6 0.7 copy-start

commit v6 on v5

--- a/solution.py
+++ b/solution.py
@@ -385,23 +385,21 @@
 def reduce_scratch():
     sem = pltpu.SemaphoreType.DMA
     return [
-        pltpu.VMEM((3, 4, 4, 4, 96, 128), BF),
         pltpu.VMEM((3, 6, 8, 96, 128), BF), pltpu.VMEM((3, 6, 8, 96, 128), BF),
         pltpu.VMEM((3, 6, 2, 96, 128), BF), pltpu.VMEM((3, 6, 2, 96, 128), BF),
-        pltpu.VMEM((8, 128), F32), pltpu.VMEM((3, 3, 96, 128), F32),
+        pltpu.VMEM((3, 3, 96, 128), F32),
         pltpu.VMEM((3, 4, 4, 96, 128), F32),
         pltpu.VMEM((3, 4, 96, 128), F32),
         pltpu.VMEM((2, 3, 96, 128), F32),
         pltpu.VMEM((5, 16, 128), F32), pltpu.VMEM((10, 16, 128), F32),
-        sem((54,)), sem((54,)), sem((3,)), sem((3,)), sem((11,)), sem((11,)),
-        pltpu.VMEM((3, 4, 4, 4, 96, 128), BF),
+        sem((54,)), sem((54,)), sem((11,)), sem((11,)),
         pltpu.VMEM((3, 4, 4, 4, 96, 128), F32),
-        pltpu.VMEM((1536, 384), F32), pltpu.VMEM((768, 256), F32),
+        pltpu.VMEM((1536, 384), F32), pltpu.VMEM((3, 768, 256), F32),
     ]
 
 
 def reduce_stages(me, half, scratch):
-    (r0, s1, d1, s2, d2, s3, d3, t1, t2, fin, gt, gg, send, recv, csend, crecv, gsend, grecv) = scratch[:18]
+    s1, d1, s2, d2, d3, t1, t2, fin, gt, gg, send, recv = scratch[:12]
 
     def load1(c):
         axis = ORDERS[c][0]
@@ -441,27 +439,24 @@
     return stages
 
 
-def core_hop(me, scratch, c):
-    r0, csend, crecv, g = scratch[0], scratch[14], scratch[15], scratch[18]
-    return pltpu.make_async_remote_copy(
-        src_ref=g.at[c], dst_ref=r0.at[c], send_sem=csend.at[c], recv_sem=crecv.at[c],
-        device_id=me.device(), device_id_type=MESH)
-
-
-def weight_terms(refs, scratch, h, c, put):
-    nt, ct, gq, gk, gv, masked = refs
-    prod, prod_o = scratch[20:22]
-    columns = pl.ds(pl.multiple_of(h * 384 + c * 128, 128), 128)
+def out_terms(refs, scratch, core, c):
+    ct, masked, prod_o = refs[1], refs[5], scratch[16]
+    columns = pl.ds(pl.multiple_of(core * 768 + c * 256, 128), 256)
+    prod_o[c] = dot(ct[...], masked[:, columns])
+
+
+def weight_terms(refs, scratch, core, c):
+    nt, _, gq, gk, gv, _ = refs
+    half, prod, prod_o = scratch[14:17]
+    columns = pl.ds(pl.multiple_of(core * 384 + c * 128, 128), 128)
     rhs = jnp.concatenate([gq[:, columns], gk[:, columns], gv[:, columns]], 1)
-    prod[...] = jnp.dot(nt[...], rhs, preferred_element_type=F32)
-    columns = pl.ds(pl.multiple_of(h * 768 + c * 256, 128), 256)
-    prod_o[...] = jnp.dot(ct[...], masked[:, columns], preferred_element_type=F32)
+    prod[...] = dot(nt[...], rhs)
 
     @pl.loop(0, 32)
     def _(pair):
         upper = lax.broadcasted_iota(jnp.int32, (8, 128), 0) < 4
         at = pl.multiple_of(pair * 24, 8)
-        tiles = [[prod_o[pl.ds(at + 8 * n, 8), pl.ds(128 * b, 128)] for b in range(2)] for n in range(3)]
+        tiles = [[prod_o[c, pl.ds(at + 8 * n, 8), pl.ds(128 * b, 128)] for b in range(2)] for n in range(3)]
         mixed = (
             jnp.where(upper, tiles[1][0], pltpu.roll(tiles[1][1], 4, 0)),
             jnp.where(upper, pltpu.roll(tiles[1][0], 4, 0), tiles[1][1]),
@@ -471,14 +466,14 @@
             rows = pl.ds(pl.multiple_of(pair * 48 + 24 * odd, 8), 24)
             parts = [prod[rows, pl.ds(128 * n, 128)] for n in range(3)]
             parts += [tiles[2 * odd][0], tiles[2 * odd][1], mixed[odd]]
-            put((yh * 2 + yl, z, xh * 2 + odd), jnp.concatenate(parts, 0))
+            half[c, yh * 2 + yl, z, xh * 2 + odd] = jnp.concatenate(parts, 0)
 
 
 def grad_normed(w, gq, gk, gv, out):
     for s in range(4):
         total = None
         for n, g in enumerate((gq, gk, gv)):
-            term = dot(g[...], pair_rows(w, s, n), ROWS)
+            term = dot(g[:256], pair_rows(w, s, n), ROWS)
             total = term if total is None else total + term
         for b in range(3 * s, 3 * s + 3):
             out[b // 2, b % 2] = total[:, 128 * (b - 3 * s):128 * (b - 3 * s) + 128]
@@ -515,7 +510,7 @@
     wq, wk, wv, wo, frames_hbm, cotangent_hbm, gain_hbm, lengths, lo_hbm, hi_hbm,
     total, gain_out, grad_frames_hbm, frames_out_hbm,
     nt, ct, ctx, gq, gk, gv, masked, frames, cotangent, gain, lo, hi, grad_frames, frames_out,
-    held, w, nm, q6, gc6, kv, center, bias, rim_s, rim_r, send, recv, local, ring_send, ring_recv, *scratch
+    held, w, nm, q6, gc6, kv, center, bias, rim_s, rim_r, send, recv, local, ring_send, ring_recv, twin_send, twin_recv, *scratch
 ):
     me = Place()
     length = lengths[0]
@@ -526,6 +521,18 @@
         copy.start()
     rows = start_gather(me, (wq, wk, wv, wo), held, w, send, recv, local)
 
+    def twin(n):
+        across = lambda width: pl.ds(pl.multiple_of((1 - me.core) * width, 128), width)
+        ref = (nt, masked, ct, gq, gk, gv)[n]
+        if n in (0, 2):
+            src, dst = ref.at[:, pl.ds(0, 256)], ref.at[:, pl.ds(256, 256)]
+        else:
+            lanes = across(768 if n == 1 else 384)
+            src, dst = ref.at[pl.ds(0, 256), lanes], ref.at[pl.ds(256, 256), lanes]
+        return pltpu.make_async_remote_copy(
+            src_ref=src, dst_ref=dst, send_sem=twin_send.at[n], recv_sem=twin_recv.at[n],
+            device_id=me.device(), device_id_type=MESH)
+
     def normalize():
         for copy in loads:
             copy.wait()
@@ -537,13 +544,15 @@
             nm[at] = (xhat * gain[...]).astype(BF)
 
     def prepare():
-        nt[...] = nm[...].T
+        nt[:, :256] = nm[...].T
+        twin(0).start()
 
         @pl.loop(0, 8)
         def _(n):
             at = pl.ds(pl.multiple_of(n * 32, 32), 32)
             frame = base + n * 32 + lax.broadcasted_iota(jnp.int32, (32, 1536), 0)
             masked[at] = jnp.where(frame < length, cotangent[at].astype(F32), 0.0).astype(BF)
+        twin(1).start()
 
         for b in range(2):
             kp = base + 128 * (b - 1) + lax.broadcasted_iota(jnp.int32, (384, 128), 0)
@@ -585,7 +594,7 @@
     for p in range(6):
         q6[p] = q[:, 128 * p:128 * p + 128]
     for yh in range(2):
-        g = (dot(masked[:, :768], out_rows(w, yh, 0), ROWS) + dot(masked[:, 768:], out_rows(w, yh, 1), ROWS)).astype(BF)
+        g = (dot(masked[:256, :768], out_rows(w, yh, 0), ROWS) + dot(masked[:256, 768:], out_rows(w, yh, 1), ROWS)).astype(BF)
         for n in range(3):
             gc6[3 * yh + n] = g[:, 128 * n:128 * n + 128]
 
@@ -628,42 +637,36 @@
         for right in range(2):
             rim(p, right).start()
 
+    twin(2).start()
+    twin(3).start()
     for p in range(6):
         for right in range(2):
             rim(p, right).wait_recv()
         for m, out in enumerate((gk, gv)):
             lanes = pl.ds(128 * p, 128)
             out[:128, lanes] = (center[p, m, :128] + rim_r[p, 1, m].astype(F32)).astype(BF)
-            out[128:, lanes] = (center[p, m, 128:] + rim_r[p, 0, m].astype(F32)).astype(BF)
-
-    r0, fin, gt, gg, gsend, grecv = scratch[0], scratch[9], scratch[10], scratch[11], scratch[16], scratch[17]
-    for_other, half = scratch[18:20]
+            out[128:256, lanes] = (center[p, m, 128:] + rim_r[p, 0, m].astype(F32)).astype(BF)
+
+    twin(4).start()
+    twin(5).start()
+    fin, gt, gg = scratch[7:10]
+    gsend, grecv, half = scratch[12:15]
     refs = (nt, ct, gq, gk, gv, masked)
     stages = reduce_stages(me, half, scratch)
     sum_gain = GainSum(me, gt, gg, gsend, grecv)
 
-    def send_other(c):
-        def put(at, v):
-            for_other[(c,) + at] = v.astype(BF)
-        weight_terms(refs, scratch, 1 - me.core, c, put)
-        core_hop(me, scratch, c).start()
-
-    def start_own(c):
-        core_hop(me, scratch, c).wait_recv()
-
-        def put(at, v):
-            half[(c,) + at] = v + r0[(c,) + at].astype(F32)
-        weight_terms(refs, scratch, me.core, c, put)
+    for n in range(3):
+        twin(n).wait_recv()
+    for c in range(3):
+        out_terms(refs, scratch, me.core, c)
+    for n in range(3, 6):
+        twin(n).wait_recv()
+    for c in range(3):
+        weight_terms(refs, scratch, me.core, c)
         stages[c][0].start()
-
+    grad_normed(w, gq, gk, gv, center)
     for c in range(3):
-        send_other(c)
-    for c in range(3):
-        start_own(c)
-    stages[0][0].relay()
-    grad_normed(w, gq, gk, gv, center)
-    stages[1][0].relay()
-    stages[2][0].relay()
+        stages[c][0].relay()
     norm_backward(frames, cotangent, gain, center, grad_frames, gt)
     stores = [
         pltpu.make_async_copy(grad_frames, grad_frames_hbm, local.at[11]),
@@ -693,10 +696,11 @@
     sum_gain.finish(3)
     gain_out[...] = gt[4]
     for c in range(3):
-        core_hop(me, scratch, c).wait_send()
         for n in range(3):
             stages[c][n].drain()
     sum_gain.drain()
+    for n in range(6):
+        twin(n).wait_send()
     last(me.core).wait_send()
     last(1 - me.core).wait_recv()
     total[...] = fin[...]
@@ -720,9 +724,9 @@
         in_specs=[hbm] * 7 + [pl.BlockSpec(memory_space=pltpu.SMEM)] + [hbm] * 2,
         out_specs=(vm, vm, hbm, hbm),
         scratch_shapes=[
-            pltpu.VMEM((1536, 256), BF), pltpu.VMEM((768, 256), BF), pltpu.VMEM((256, 768), BF),
-            pltpu.VMEM((256, 768), BF), pltpu.VMEM((256, 768), BF), pltpu.VMEM((256, 768), BF),
-            pltpu.VMEM((256, 1536), BF), pltpu.VMEM((256, 1536), BF), pltpu.VMEM((256, 1536), BF),
+            pltpu.VMEM((1536, 512), BF), pltpu.VMEM((768, 512), BF), pltpu.VMEM((256, 768), BF),
+            pltpu.VMEM((512, 768), BF), pltpu.VMEM((512, 768), BF), pltpu.VMEM((512, 768), BF),
+            pltpu.VMEM((512, 1536), BF), pltpu.VMEM((256, 1536), BF), pltpu.VMEM((256, 1536), BF),
             pltpu.VMEM((1, 1536), F32), pltpu.VMEM((1, 256), jnp.int32), pltpu.VMEM((1, 256), jnp.int32),
             pltpu.VMEM((256, 1536), BF), pltpu.VMEM((256, 1536), BF),
             pltpu.VMEM((48, 16, 768), BF),
@@ -733,7 +737,7 @@
             pltpu.VMEM((6, 2, 256, 128), F32),
             pltpu.VMEM((2, 384, 128), F32),
             pltpu.VMEM((6, 2, 2, 128, 128), BF), pltpu.VMEM((6, 2, 2, 128, 128), BF),
-            sem((GATHER_SEMS,)), sem((GATHER_SEMS,)), sem((13,)), sem((24,)), sem((24,)),
+            sem((GATHER_SEMS,)), sem((GATHER_SEMS,)), sem((13,)), sem((24,)), sem((24,)), sem((6,)), sem((6,)),
         ] + reduce_scratch(),
         compiler_params=pltpu.CompilerParams(collective_id=0, has_side_effects=True, vmem_limit_bytes=67043328),
         name="block",

time: 104 us -> 99.9 us (0.961)
  Pallas kernels: 101 us -> 97.7 us
    pallas_call x1, Pallas kernels: 98.7 us -> 95 us  [block(): pl.pallas_call(block_kernel, out_shape=(sds((2, 3, 96, 128), F32), sds((1...]
where the time goes in v6:
time: 99.9 us; the launch traced here: 99.7 us
  Pallas kernels  97.7 us (98%)
  between operations  1.31 us (1%)
    pallas_call x1, Pallas kernels, block(): pl.pallas_call(block_kernel, out_shape=(sds((2, 3, 96, 128), F32), sds((1...  95 us
    pallas_call x1, Pallas kernels, write_outputs(): pl.pallas_call(outputs_kernel, out_shape=(sds((12, 768), F32),) * 3 + (sd...  2.74 us

profile of v6, /device:TPU:1, one launch (start us, length us, event | category | flops | bytes accessed | tf_op | source)
XLA Modules:
  0.0 99.7 jit_solution(8831117798964756707)
XLA Ops:
  0.6 0.0 copy-start
  1.3 0.0 copy-done
  1.3 0.6 broadcast_in_dim.9.gain_hbm
  1.9 95.0 %block.1 = (f32[2,3,96,128]{3,2,1,0:T(8,128)}, f32[16,128]{1,0:T(8,128)}, bf16[256,1536]{1,0:T(8,128)(2,1)}, bf16[256,1536]{1,0:T(8,128)(2,1)}) custom-call(bf16[12,16,768]{2,1,0:T(8,128)(2,1)} %bitcast.11, bf16[12,16,768]{2,1,0:T(8,128)(2,1)} %bitcast.12, bf16[12,16,768]{2,1,0:T(8,128)(2,1)} %bitcast.13, bf16[6,16,1536]{2,1,0:T(8,128)(2,1)} %bitcast.14, ...), custom_call_target="tpu_custom_call" | custom-call | tf_op jit(solution)/shard_map/block/pallas_call | solution.py:721
  96.9 2.7 %write_outputs.1 = (f32[12,768]{1,0:T(8,128)}, f32[12,768]{1,0:T(8,128)}, f32[12,768]{1,0:T(8,128)}, f32[6,1536]{1,0:T(8,128)}, f32[1,12]{1,0:T(1,128)}, /*index...) custom-call(f32[2,3,96,128]{3,2,1,0:T(8,128)} %get-tuple-element.18.total, f32[16,128]{1,0:T(8,128)} %get-tuple-element.19.gain, ...), custom_call_target="tpu_custom_call" | custom-call | tf_op jit(solution)/shard_map/write_outputs/pallas_call | solution.py:776
Async XLA Ops:
  0.6 0.7 copy-start

commit v7 on v6

--- a/solution.py
+++ b/solution.py
@@ -69,9 +69,9 @@
             ("y", lambda j, p: w.at[j // 2, pl.ds(2 * p, 2), h, 1, lax.rem(j, 2)]),
         ),
         (
-            ("z", lambda j, p: w.at[me.yh, j, h, 2, me.yl, me.x, :, pl.ds(384 * p, 384)]),
-            ("y", lambda j, p: w.at[j // 2, pl.ds(2 * p, 2), h, 2, lax.rem(j, 2), me.x]),
-            ("x", lambda j, p: w.at[p, :, h, 2, :, j]),
+            ("z", lambda j, p: w.at[me.yh, j, h, 2, p, me.x]),
+            ("cross", lambda j, p: w.at[j, pl.ds(2 * p, 2), h, 2, :, me.x]),
+            ("x", lambda j, p: w.at[1 - me.yh if p else me.yh, :, h, 2, :, j]),
         ),
     )
 
@@ -102,6 +102,11 @@
         self.hop(1, i, 1, False).start()
         self.hop(2, i, 1, True).start()
         self.hop(3, i, 0, False).start()
+
+    def start_half(self, p):
+        i = self.me.at(self.axis)
+        for k, right in ((1, False), (2, True)) if p else ((0, True), (3, False)):
+            self.hop(k, i, p, right).start()
 
     def relay(self):
         me = self.me
@@ -140,13 +145,41 @@
             self.share(k, j, p).wait_send()
 
 
+class CrossStage(GatherStage):
+    def hop(self, k):
+        me, n = self.me, self.base + k
+        part = self.region(me.yh, k)
+        return pltpu.make_async_remote_copy(
+            src_ref=part, dst_ref=part, send_sem=self.send.at[n], recv_sem=self.recv.at[n],
+            device_id=me.device("y", 3 - me.y), device_id_type=MESH)
+
+    def start(self):
+        for k in range(2):
+            self.hop(k).start()
+
+    def finish(self):
+        for k in range(2):
+            self.hop(k).wait_recv()
+            self.share(k, 1 - self.me.yh, k).start()
+
+    def arrive(self):
+        for k in range(2):
+            self.share(k, 1 - self.me.yh, k, self.other).wait_recv()
+
+    def drain(self):
+        for k in range(2):
+            self.hop(k).wait_send()
+            self.share(k, 1 - self.me.yh, k).wait_send()
+
+
 def gather_stages(me, w, send, recv):
     mine, theirs = gather_regions(me, w, me.core), gather_regions(me, w, 1 - me.core)
     stages, base = [], 0
     for colour, other in zip(mine, theirs):
         row = []
         for (axis, region), (_, other_region) in zip(colour, other):
-            row.append(GatherStage(me, axis, region, other_region, send, recv, base))
+            kind = CrossStage if axis == "cross" else GatherStage
+            row.append(kind(me, axis, region, other_region, send, recv, base))
             base += 12
         stages.append(row)
     return stages
@@ -168,8 +201,9 @@
     for h in range(2):
         for c in range(2):
             own.append((held.at[pl.ds(24 * h + 8 * c + 4 * me.yl, 4)], w.at[me.yh, me.z, h, c, me.yl]))
-        own.append((held.at[24 * h + 16 + 4 * me.yl + me.x], w.at[me.yh, me.z, h, 2, me.yl, me.x]))
-    own = [pltpu.make_async_copy(src, dst, local.at[n]) for n, (src, dst) in enumerate(own)]
+        for yl in range(2):
+            own.append((held.at[24 * h + 16 + 4 * yl + me.x], w.at[me.yh, me.z, h, 2, yl, me.x]))
+    own = [pltpu.make_async_copy(src, dst, local.at[n if n < 6 else 7 + n]) for n, (src, dst) in enumerate(own)]
     for copy in own:
         copy.start()
     greet(me, ring=True)
@@ -188,17 +222,17 @@
     b[0].relay()
     c[0].finish()
     c[1].start()
+    c[2].start_half(0)
     a[0].finish()
     a[1].start()
     b[0].finish()
-    c[1].relay()
     b[1].start()
+    first()
     c[1].finish()
-    c[2].start()
-    first()
+    c[2].start_half(1)
     a[1].relay()
+    second()
     b[1].relay()
-    second()
     c[2].relay()
     a[1].finish()
     b[1].finish()
@@ -737,7 +771,7 @@
             pltpu.VMEM((6, 2, 256, 128), F32),
             pltpu.VMEM((2, 384, 128), F32),
             pltpu.VMEM((6, 2, 2, 128, 128), BF), pltpu.VMEM((6, 2, 2, 128, 128), BF),
-            sem((GATHER_SEMS,)), sem((GATHER_SEMS,)), sem((13,)), sem((24,)), sem((24,)), sem((6,)), sem((6,)),
+            sem((GATHER_SEMS,)), sem((GATHER_SEMS,)), sem((15,)), sem((24,)), sem((24,)), sem((6,)), sem((6,)),
         ] + reduce_scratch(),
         compiler_params=pltpu.CompilerParams(collective_id=0, has_side_effects=True, vmem_limit_bytes=67043328),
         name="block",

time: 99.9 us -> 98.9 us (0.990)
  Pallas kernels: 97.7 us -> 96.5 us
    pallas_call x1, Pallas kernels: 95 us -> 93.8 us  [block(): pl.pallas_call(block_kernel, out_shape=(sds((2, 3, 96, 128), F32), sds((1...]
where the time goes in v7:
time: 98.9 us; the launch traced here: 98.5 us
  Pallas kernels  96.5 us (98%)
  between operations  1.31 us (1%)
    pallas_call x1, Pallas kernels, block(): pl.pallas_call(block_kernel, out_shape=(sds((2, 3, 96, 128), F32), sds((1...  93.8 us
    pallas_call x1, Pallas kernels, write_outputs(): pl.pallas_call(outputs_kernel, out_shape=(sds((12, 768), F32),) * 3 + (sd...  2.74 us

profile of v7, /device:TPU:1, one launch (start us, length us, event | category | flops | bytes accessed | tf_op | source)
XLA Modules:
  0.0 98.5 jit_solution(611901726129233729)
XLA Ops:
  0.6 0.0 copy-start
  1.3 0.0 copy-done
  1.3 0.6 broadcast_in_dim.9.gain_hbm
  1.9 93.8 %block.1 = (f32[2,3,96,128]{3,2,1,0:T(8,128)}, f32[16,128]{1,0:T(8,128)}, bf16[256,1536]{1,0:T(8,128)(2,1)}, bf16[256,1536]{1,0:T(8,128)(2,1)}) custom-call(bf16[12,16,768]{2,1,0:T(8,128)(2,1)} %bitcast.11, bf16[12,16,768]{2,1,0:T(8,128)(2,1)} %bitcast.12, bf16[12,16,768]{2,1,0:T(8,128)(2,1)} %bitcast.13, bf16[6,16,1536]{2,1,0:T(8,128)(2,1)} %bitcast.14, ...), custom_call_target="tpu_custom_call" | custom-call | tf_op jit(solution)/shard_map/block/pallas_call | solution.py:755
  95.7 2.7 %write_outputs.1 = (f32[12,768]{1,0:T(8,128)}, f32[12,768]{1,0:T(8,128)}, f32[12,768]{1,0:T(8,128)}, f32[6,1536]{1,0:T(8,128)}, f32[1,12]{1,0:T(1,128)}, /*index...) custom-call(f32[2,3,96,128]{3,2,1,0:T(8,128)} %get-tuple-element.18.total, f32[16,128]{1,0:T(8,128)} %get-tuple-element.19.gain, ...), custom_call_target="tpu_custom_call" | custom-call | tf_op jit(solution)/shard_map/write_outputs/pallas_call | solution.py:810
Async XLA Ops:
  0.6 0.7 copy-start
